TPU v7x, 32 devices: a whole 2x2x4 slice. The times are simulated.
32 devices in a mesh: region: 8 (over z, y), depth: 4 (over x, core).
Axes of the slice: x: 2, y: 2, z: 4, core: 2. Of those that a mesh axis runs over, the one named last changes fastest.
Arguments:
- displacement: float32 [16, 16, 3, 1024], P('depth', None, None, 'region'), may hold values from -1.5 to 1.5
- velocity: float32 [16, 16, 3, 1024], P('depth', None, None, 'region'), may hold values from -4 to 4
- growth: float32 [16, 16, 1024], P('depth', None, 'region'), may hold values from 1 to 1.6
- shear_modulus: float32 [16, 16, 1024], P('depth', None, 'region'), may hold values from 0.3 to 3
- pair_slots: int32 [4, 8, 3, 16], P('depth', 'region'), may hold values from 0 to 63, as said below
- pair_count: int32 [4, 8], P('depth', 'region'), may hold values from 12 to 16, as said below
- separation: float32 [4, 8, 3, 16], P('depth', 'region'), may hold values from -1 to 1, as said below
Outputs:
- new_velocity: float32 [16, 16, 3, 1024], P('depth', None, None, 'region')
- new_displacement: float32 [16, 16, 3, 1024], P('depth', None, None, 'region')
Inputs may be any that keep to these rules, and one draw needn't show every extreme that they name: `pair_slots`: row 0 of a slot is a patch of the own region below 64, row 1 a region, row 2 a patch of that region below 64. Slots k < pair_count[s, r] are live and name another region; the rest hold arbitrary values in the same ranges. Contact is symmetric: a live slot (l, m, q) with separation o on (s, r) comes with a live slot (q, r, l) with separation -o on (s, m). At most 4 live slots of one region and slab name the same region; in every slab some region has exactly 4 live slots for every region it names. `pair_count`: in every slab some region has 16 live slots. `separation`: opposite on the two sides of a contact, as stated for pair_slots.
All inputs are finite; a program needn't handle non-finite values.
Results may differ from a plain program's by a relative error of at most 0.0003.
Values sent between devices are 32-bit elements; how exact they have to be, the bound alone decides.
No kernel may reach another device: no remote copies, remote signals or barrier semaphores. Data moves between devices by JAX's collectives and lax.ppermute only.
A program may use at most 64 MiB of HBM per device.

v0:
```python
import math

import jax
import jax.numpy as jnp
from jax import lax
from jax.sharding import PartitionSpec as P

CAP = 4


PERMUTATIONS = ((0, 1, 2), (0, 2, 1), (1, 0, 2), (1, 2, 0), (2, 0, 1), (2, 1, 0))
CORNER_SET = (
    (0, 0, 0),
    (0, 0, 1),
    (0, 1, 0),
    (0, 1, 1),
    (1, 0, 0),
    (1, 0, 1),
    (1, 1, 0),
    (1, 1, 1),
)
REST_VOLUME = 1.0 / 6.0
STEP_TIME = 0.2


def with_halo(cells, sides, width):
    for axis, dim in sides:
        count = lax.axis_size(axis)
        head = lax.slice_in_dim(cells, 0, width, axis=dim)
        tail = lax.slice_in_dim(cells, cells.shape[dim] - width, cells.shape[dim], axis=dim)
        cells = jnp.concatenate(
            [
                lax.ppermute(tail, axis, [(i, (i + 1) % count) for i in range(count)]),
                cells,
                lax.ppermute(head, axis, [((i + 1) % count, i) for i in range(count)]),
            ],
            axis=dim,
        )
    return cells


def unit_step(component):
    return tuple((1 if position == 2 - component else 0 for position in range(3)))


def joined(first_offset, second_offset):
    return tuple((first_offset[index] + second_offset[index] for index in range(3)))


def shifted(field, offset):
    return jnp.roll(field, (-offset[0], -offset[1], -offset[2]), axis=(0, 1, 2))


def cell_forces(displacement, growth, shear, valid):
    fields = [displacement[:, :, index, :] for index in range(3)]
    corners = {offset: [shifted(field, offset) for field in fields] for offset in CORNER_SET}
    inverse = 1.0 / growth
    squared = growth * growth
    weight = valid * REST_VOLUME
    totals = {offset: [jnp.zeros_like(growth) for index in range(3)] for offset in CORNER_SET}
    for ordering in PERMUTATIONS:
        first_axis, second_axis, third_axis = ordering
        start = (0, 0, 0)
        middle = unit_step(first_axis)
        upper = joined(middle, unit_step(second_axis))
        summit = (1, 1, 1)
        columns = [None, None, None]
        columns[first_axis] = [corners[middle][row] - corners[start][row] for row in range(3)]
        columns[second_axis] = [corners[upper][row] - corners[middle][row] for row in range(3)]
        columns[third_axis] = [corners[summit][row] - corners[upper][row] for row in range(3)]
        elastic_f = [
            [
                (columns[col][row] + (1.0 if row == col else 0.0)) * (inverse if col < 2 else 1.0)
                for col in range(3)
            ]
            for row in range(3)
        ]
        cofactor = [
            [
                elastic_f[(row + 1) % 3][(col + 1) % 3] * elastic_f[(row + 2) % 3][(col + 2) % 3]
                - elastic_f[(row + 1) % 3][(col + 2) % 3] * elastic_f[(row + 2) % 3][(col + 1) % 3]
                for col in range(3)
            ]
            for row in range(3)
        ]
        jacobian = (
            elastic_f[0][0] * cofactor[0][0]
            + elastic_f[0][1] * cofactor[0][1]
            + elastic_f[0][2] * cofactor[0][2]
        )
        pressure = 4.0 * (jacobian - 1.25)
        stress = [
            [
                shear
                * (elastic_f[row][col] + pressure * cofactor[row][col])
                * (growth if col < 2 else squared)
                * weight
                for col in range(3)
            ]
            for row in range(3)
        ]
        for row in range(3):
            col_first = stress[row][first_axis]
            col_second = stress[row][second_axis]
            col_third = stress[row][third_axis]
            totals[start][row] = totals[start][row] + col_first
            totals[middle][row] = totals[middle][row] + (col_second - col_first)
            totals[upper][row] = totals[upper][row] + (col_third - col_second)
            totals[summit][row] = totals[summit][row] - col_third
    result = []
    for row in range(3):
        summed = jnp.zeros_like(growth)
        for offset in CORNER_SET:
            summed = summed + jnp.roll(totals[offset][row], offset, axis=(0, 1, 2))
        result.append(summed)
    return jnp.stack(result, axis=2)


def pair_forces(near, far):
    deltas = [near[:, index, :, None] - far[:, index, None, :] for index in range(3)]
    distance = deltas[0] * deltas[0] + deltas[1] * deltas[1] + deltas[2] * deltas[2]
    kernel = jnp.exp(-distance)
    return jnp.stack([jnp.sum(delta * kernel, axis=2) for delta in deltas], axis=1)


def blocked_forces(near, far):
    total_rows = near.shape[0]
    block = math.gcd(total_rows, 32)
    shaped = (total_rows // block, block) + near.shape[1:]
    result = lax.map(
        lambda couple: pair_forces(couple[0], couple[1]),
        (near.reshape(shaped), far.reshape(shaped)),
    )
    return result.reshape(near.shape)


def local(displacement, velocity, growth, shear_modulus, pair_slots, pair_count, separation):
    slab_len, width_y, _, patch_len = displacement.shape
    regions = lax.axis_size("region")
    slabs = lax.axis_size("depth")
    depth_index = lax.axis_index("depth")
    stacked = jnp.concatenate(
        [displacement, growth[:, :, None, :], shear_modulus[:, :, None, :]], axis=2
    )
    extended = with_halo(stacked, (("region", 3), ("depth", 0)), 1)
    z_local = jnp.arange(slab_len + 2, dtype=jnp.int32)
    z_global = depth_index * slab_len + z_local - 1
    z_valid = (z_local <= slab_len) & (z_global >= 0) & (z_global <= slab_len * slabs - 2)
    y_valid = jnp.arange(width_y, dtype=jnp.int32) <= width_y - 2
    x_valid = jnp.arange(patch_len + 2, dtype=jnp.int32) <= patch_len
    valid = (z_valid[:, None, None] & y_valid[None, :, None] & x_valid[None, None, :]).astype(
        jnp.float32
    )
    elastic_ext = cell_forces(
        extended[:, :, 0:3, :], extended[:, :, 3, :], extended[:, :, 4, :], valid
    )
    elastic = elastic_ext[1 : slab_len + 1, :, :, 1 : patch_len + 1]
    patches_dev = slab_len * width_y
    component_row = lax.broadcasted_iota(jnp.int32, (3, patch_len), 0)
    along_row = lax.broadcasted_iota(jnp.int32, (3, patch_len), 1).astype(jnp.float32)
    rest_line = jnp.where(component_row == 0, along_row, jnp.zeros_like(along_row))
    own_points = displacement.reshape(patches_dev, 3, patch_len) + rest_line
    slots = pair_slots[0, 0]
    own_patch = slots[0]
    peer_region = slots[1]
    peer_patch = slots[2]
    slot_total = slots.shape[1]
    offsets = jnp.transpose(separation[0, 0])
    live = jnp.arange(slot_total, dtype=jnp.int32) < pair_count[0, 0]
    onehot_peer = (
        (peer_region[:, None] == jnp.arange(regions, dtype=jnp.int32)[None, :]) & live[:, None]
    ).astype(jnp.int32)
    before = jnp.cumsum(onehot_peer, axis=0) - onehot_peer
    rank = jnp.sum(before * onehot_peer, axis=1)
    buckets = regions * CAP
    bucket = jnp.where(live, peer_region * CAP + rank, buckets)
    outgoing = (
        jnp.zeros((buckets, 3, patch_len), jnp.float32)
        .at[bucket]
        .set(own_points[own_patch] - offsets[:, :, None], mode="drop")
    )
    labels = (
        jnp.full((buckets,), -1.0, jnp.float32)
        .at[bucket]
        .set(peer_patch.astype(jnp.float32), mode="drop")
    )
    arrived, arrived_labels = (
        lax.all_to_all(
            outgoing.reshape(regions, CAP, 3, patch_len),
            "region",
            split_axis=0,
            concat_axis=0,
            tiled=True,
        ),
        lax.all_to_all(
            labels.reshape(regions, CAP), "region", split_axis=0, concat_axis=0, tiled=True
        ),
    )
    arrived = arrived.reshape(buckets, 3, patch_len)
    arrived_labels = arrived_labels.reshape(buckets)
    chosen = arrived_labels >= 0.0
    targets = jnp.where(chosen, arrived_labels, 0.0).astype(jnp.int32)
    forces = blocked_forces(own_points[targets], arrived) * chosen[:, None, None].astype(
        jnp.float32
    )
    selector = (
        (targets[:, None] == jnp.arange(patches_dev, dtype=jnp.int32)[None, :]) & chosen[:, None]
    ).astype(jnp.float32)
    contact = jnp.einsum("kp,kcx->pcx", selector, forces, precision=lax.Precision.HIGHEST)
    contact = contact.reshape(slab_len, width_y, 3, patch_len)
    new_velocity = velocity + STEP_TIME * (elastic + contact)
    new_displacement = displacement + STEP_TIME * new_velocity
    return (new_velocity, new_displacement)


def solution(mesh):
    in_specs = (
        P("depth", None, None, "region"),
        P("depth", None, None, "region"),
        P("depth", None, "region"),
        P("depth", None, "region"),
        P("depth", "region", None, None),
        P("depth", "region"),
        P("depth", "region", None, None),
    )
    out_specs = (P("depth", None, None, "region"), P("depth", None, None, "region"))
    return jax.shard_map(local, mesh=mesh, in_specs=in_specs, out_specs=out_specs, check_vma=False)
```

profile of v0, /device:TPU:1, one launch (start us, length us, event | category | flops | bytes accessed | tf_op | source)
XLA Modules:
  0.0 50.1 jit_solution(1736963173095069045)
XLA Ops:
  1.3 0.7 %convert_bitcast_fusion = (f32[16]{0:T(128)S(1)}, s32[16]{0:T(128)S(1)}) fusion(s32[1,1,3,16]{3,1,2,0:T(1,128)} %param.11), kind=kLoop, calls=%fused_computation.623 | loop fusion | flops 16 | bytes 256 | tf_op jit(solution)/shard_map/convert_element_type | solution.py:185
  2.1 0.2 select_reduce_fusion
  2.3 0.7 %fusion.163 = (s32[16]{0:T(128)S(1)}, s32[16]{0:T(128)S(1)}) fusion(s32[1,1,3,16]{3,1,2,0:T(1,128)} %param.11, s32[16]{0:T(128)S(1)} %select_reduce_fusion, s32[]{:T(128)} %bitcast.952), kind=kLoop, calls=%fused_computation.618 | loop fusion | flops 160 | bytes 324 | tf_op jit(solution)/shard_map/select_n | solution.py:180
  2.9 0.6 %scatter_custom_fusion = f32[32]{0:T(128)S(1)} fusion(s32[16]{0:T(128)S(1)} %get-tuple-element.149, f32[16]{0:T(128)S(1)} %get-tuple-element.146, f32[]{:T(128)} %constant.30.clone.1), kind=kCustom, calls=%fused_computation.629 | custom fusion | bytes 132 | tf_op jit(solution)/shard_map/scatter | solution.py:185
  3.6 0.7 %all_to_all.9 = f32[8,1,4]{2,0,1:T(8,128)} reshape(f32[32]{0:T(128)S(1)} %scatter_custom_fusion) | data formatting | bytes 256 | tf_op jit(solution)/shard_map/all_to_all | solution.py:195
  4.3 6.4 %all-to-all-start = ((f32[8,1,4]{2,1,0:T(1,128)}), f32[8,1,4]{2,1,0:T(1,128)S(1)}, u32[]{:S(2)}, u32[]{:S(2)}) async-start(f32[8,1,4]{2,1,0:T(1,128)} %bitcast.104), calls=%async_computation | async-start | bytes 8192 | tf_op jit(solution)/shard_map/all_to_all | solution.py:195
  10.6 1.0 %pad_maximum_fusion.10 = f32[4,16,5,128]{3,1,0,2:T(8,128)S(1)} fusion(f32[4,16,1,128]{3,1,0,2:T(8,128)} %bitcast.1004, f32[4,16,1,128]{3,1,0,2:T(8,128)} %bitcast.1008, f32[4,16,3,128]{3,1,2,0:T(8,128)} %param.7), kind=kLoop, calls=%fused_computation.108 | loop fusion | flops 81920 | bytes 327680 | tf_op jit(solution)/shard_map/concatenate | solution.py:142
  11.7 1.5 %collective-permute-start = (f32[4,16,5,1]{3,1,0,2:T(8,128)S(1)}, f32[4,16,5,1]{3,1,0,2:T(8,128)S(1)}, u32[]{:S(2)}, u32[]{:S(2)}) collective-permute-start(f32[4,16,5,1]{3,1,0,2:T(8,128)S(1)} %get-tuple-element.108), channel_id=1, source_target_pairs={{0,4},{4,8},{8,12},{12,16},{16,20},{20,24},{24,28},{28,0},{1,5},{5... | collective-permute-start | bytes 3848 | tf_op jit(solution)/shard_map/ppermute | solution.py:33
  13.2 2.8 %collective-permute-start.1 = (f32[4,16,5,1]{3,1,0,2:T(8,128)S(1)}, f32[4,16,5,1]{3,1,0,2:T(8,128)S(1)}, u32[]{:S(2)}, u32[]{:S(2)}) collective-permute-start(f32[4,16,5,1]{3,1,0,2:T(8,128)S(1)} %get-tuple-element.109), channel_id=1, source_target_pairs={{4,0},{8,4},{12,8},{16,12},{20,16},{24,20},{28,24},{0,28},{5,1},{9... | collective-permute-start | bytes 3848 | tf_op jit(solution)/shard_map/ppermute | solution.py:35
  16.4 0.6 %gather_fusion.1 = f32[16,3,128]{2,1,0:T(4,128)S(1)} fusion(f32[64,3,128]{2,1,0:T(4,128)S(1)} %copy_add_fusion, s32[1024]{0:T(1024)S(1)} %pad_clamp_fusion), kind=kCustom, calls=%fused_computation.1 | custom fusion | bytes 49216 | tf_op jit(solution)/shard_map/gather | solution.py:180
  17.1 1.0 %scatter_fusion = f32[32,3,128]{2,1,0:T(4,128)S(1)} fusion(f32[32,3,128]{2,1,0:T(4,128)S(1)} %broadcast_in_dim.24, s32[16]{0:T(128)S(1)} %get-tuple-element.149, f32[16,3,128]{2,1,0:T(4,128)S(1)} %broadcast_subtract_fusion), kind=kCustom, calls=%fused_computation.3 | custom fusion | bytes 73792 | tf_op jit(solution)/shard_map/scatter | solution.py:180
  18.2 0.6 %copy.222 = f32[8,4,3,128]{3,1,2,0:T(4,128)} copy(f32[8,4,3,128]{3,2,1,0:T(4,128)S(1)} %bitcast.1018) | data formatting | bytes 98304 | tf_op jit(solution)/shard_map/reshape | solution.py:189
  18.8 3.3 %all-to-all-start.1 = ((f32[8,4,3,128]{3,1,2,0:T(4,128)}), f32[8,4,3,128]{3,1,2,0:T(4,128)S(1)}, u32[]{:S(2)}, u32[]{:S(2)}) async-start(f32[8,4,3,128]{3,1,2,0:T(4,128)} %copy.222), calls=%async_computation.1 | async-start | bytes 98304 | tf_op jit(solution)/shard_map/all_to_all | solution.py:188
  22.3 0.5 %broadcast.1172 = f32[]{:T(128)} broadcast(f32[]{:T(128)} %constant.1063), dimensions={} | broadcast | bytes 8 | tf_op jit(solution)/shard_map/all_to_all | solution.py:195
  22.8 0.7 %reduce.5 = f32[8,4]{1,0:T(8,128)S(1)} reduce(f32[8,1,4]{2,1,0:T(1,128)S(1)} %all-to-all-done, f32[]{:T(128)} %broadcast.1172), dimensions={1}, to_apply=%all_to_all.10.reduce_sub_computation.5 | reduce | bytes 260 | tf_op jit(solution)/shard_map/all_to_all | solution.py:195
  23.5 0.6 %gather_fusion = f32[32,3,128]{2,1,0:T(4,128)S(1)} fusion(f32[64,3,128]{2,1,0:T(4,128)S(1)} %copy_add_fusion, s32[1024]{0:T(1024)S(1)} %pad_clamp_fusion.1), kind=kCustom, calls=%fused_computation | custom fusion | bytes 98432 | tf_op jit(solution)/shard_map/gather | solution.py:203
  24.2 0.1 pad_maximum_fusion.72
  24.4 2.7 %collective-permute-start.2 = (f32[1,16,5,130]{3,1,0,2:T(8,128)S(1)}, f32[1,16,5,130]{3,1,0,2:T(8,128)S(1)}, u32[]{:S(2)}, u32[]{:S(2)}) collective-permute-start(f32[1,16,5,130]{3,1,0,2:T(8,128)S(1)} %get-tuple-element.106), channel_id=1, source_target_pairs={{0,1},{1,2},{2,3},{3,0},{4,5},{5,6},{6,7},{7,4},{8,9},{9,10},{10,1... | collective-permute-start | bytes 124808 | tf_op jit(solution)/shard_map/ppermute | solution.py:33
  27.0 1.5 %collective-permute-done.2 = f32[1,16,5,130]{3,1,0,2:T(8,128)S(1)} collective-permute-done((f32[1,16,5,130]{3,1,0,2:T(8,128)S(1)}, f32[1,16,5,130]{3,1,0,2:T(8,128)S(1)}, u32[]{:S(2)}, u32[]{:S(2)}) %collective-permute-start.2) | collective-permute-done | bytes 41632 | tf_op jit(solution)/shard_map/ppermute | solution.py:33
  28.5 2.4 %collective-permute-done.3 = f32[1,16,5,130]{3,1,0,2:T(8,128)S(1)} collective-permute-done((f32[1,16,5,130]{3,1,0,2:T(8,128)S(1)}, f32[1,16,5,130]{3,1,0,2:T(8,128)S(1)}, u32[]{:S(2)}, u32[]{:S(2)}) %collective-permute-start.3) | collective-permute-done | bytes 41632 | tf_op jit(solution)/shard_map/ppermute | solution.py:35
  30.9 0.1 pad_maximum_fusion.61
  31.2 0.1 fusion.39
  31.4 0.1 fusion.186
  31.5 0.1 fusion.41
  31.6 0.1 fusion.10
  31.7 0.2 pad_maximum_fusion
  32.1 0.1 fusion.188
  32.2 0.1 fusion.44
  32.3 0.1 fusion.190
  32.4 0.1 fusion.43
  32.5 0.1 slice_bitcast_fusion.41
  32.7 0.1 fusion.189
  32.8 0.1 fusion.40
  33.0 0.1 fusion.191
  33.1 0.1 fusion.42
  33.2 0.1 slice_bitcast_fusion.45
  33.3 1.2 %subtract_subtract_fusion.2 = (f32[6,16,130]{2,1,0:T(8,128)S(1)}, f32[6,16,130]{2,1,0:T(8,128)S(1)}, f32[6,16,130]{2,1,0:T(8,128)S(1)}, f32[6,16,130]{2,1,0:T(8,...) fusion(pred[130]{0:T(512)(128)(4,1)S(1)} %iota_compare_fusion.1, ...), kind=kLoop, calls=%fused_computation.403 | loop fusion | flops 2857920 | bytes 4043746 | tf_op jit(solution)/shard_map/sub | solution.py:109
  34.7 0.3 fusion.70
  35.0 0.3 subtract_add_fusion.3
  35.3 0.3 fusion.61
  35.6 0.3 subtract_add_fusion
  35.9 0.3 fusion.67
  36.2 0.3 fusion.58
  36.5 0.3 subtract_add_fusion.2
  36.7 0.3 subtract_add_fusion.5
  37.0 0.6 %subtract_subtract_fusion.1 = f32[6,16,130]{2,1,0:T(8,128)S(1)} fusion(f32[6,16,130]{2,1,0:T(8,128)S(1)} %get-tuple-element.97, f32[6,16,130]{2,1,0:T(8,128)S(1)} %get-tuple-element.99, f32[6,16,130]{2,1,0:T(8,128)S(1)} %get-tuple-element.98, f32[6,16,130]{2,1,0:T(8,128)S(1)} %get-tuple-element.87, f32[6,16,130]{2,1,0:T(8,128)S(1)} %get-tuple-element.85, ...), kind=kLoop, calls=%fused_computation.399 | loop fusion | flops 1235520 | bytes 2246626 | tf_op jit(solution)/shard_map/sub | solution.py:109
  37.6 0.6 %subtract_subtract_fusion = f32[6,16,130]{2,1,0:T(8,128)S(1)} fusion(f32[6,16,130]{2,1,0:T(8,128)S(1)} %get-tuple-element.89, f32[6,16,130]{2,1,0:T(8,128)S(1)} %get-tuple-element.85, f32[6,16,130]{2,1,0:T(8,128)S(1)} %get-tuple-element.95, f32[6,16,130]{2,1,0:T(8,128)S(1)} %get-tuple-element.98, f32[6,16,130]{2,1,0:T(8,128)S(1)} %get-tuple-element.90, ...), kind=kLoop, calls=%fused_computation.391 | loop fusion | flops 1235520 | bytes 2246626 | tf_op jit(solution)/shard_map/sub | solution.py:109
  38.2 0.3 fusion.64
  38.5 0.3 fusion.55
  38.8 0.3 subtract_add_fusion.4
  39.0 0.3 subtract_add_fusion.1
  39.7 0.6 %slice-done = f32[1,16,130]{2,1,0:T(8,128)S(1)} async-done(((f32[6,16,130]{2,1,0:T(8,128)}), f32[1,16,130]{2,1,0:T(8,128)S(1)}, s32[]{:S(2)}) %slice-start) | async-done | bytes 8344 | tf_op jit(solution)/shard_map/jit(_roll_static)/slice | solution.py:114
  40.2 0.2 slice-done.1
  41.2 0.2 fusion.52
  41.3 0.1 subtract_add_fusion.6
  41.5 0.1 fusion.49
  41.6 0.2 subtract_add_fusion.9
  41.8 0.1 fusion.46
  42.0 0.1 subtract_add_fusion.7
  42.6 1.0 %fusion.22 = (f32[6,16,1,130]{3,1,2,0:T(8,128)S(1)}, f32[6,16,1,130]{3,1,0,2:T(8,128)S(1)}, f32[6,16,1,130]{3,1,0,2:T(8,128)S(1)}, f32[6,16,1,130]{3,1,0,2:T(8,1...) fusion(f32[6,16,1,129]{3,1,0,2:T(8,128)S(1)} %slice_bitcast_fus, ...), kind=kLoop, calls=%fused_computation.138 | loop fusion | flops 2882880 | bytes 3045346 | tf_op jit(solution)/shard_map/add | solution.py:114
  43.6 0.8 %fusion.30 = f32[6,16,1,130]{3,1,2,0:T(8,128)S(1)} fusion(f32[6,16,1,129]{3,1,0,2:T(8,128)S(1)} %slice_bitcast_fusion.2, f32[6,16,1,1]{3,1,0,2:T(8,128)S(1)} %slice_bitcast_fusion.16, f32[6,15,1,130]{3,1,0,2:T(8,128)S(1)} %slice_bitcast_fusion.1, f32[6,1,1,130]{3,1,0,2:T(1,128)S(1)} %slice_bitcast_fusion.27, f32[6,16,1,129]{3,1,0,2:T(8,128)S(1)} %fusion.75, ...), kind=kLoop, calls=%fused_computation.146 | loop fusion | flops 2283840 | bytes 2446306 | tf_op jit(solution)/shard_map/add | solution.py:114
  44.5 0.8 %fusion.38 = f32[6,16,1,130]{3,1,2,0:T(8,128)S(1)} fusion(f32[6,16,1,129]{3,1,0,2:T(8,128)S(1)} %slice_bitcast_fusion.5, f32[6,16,1,1]{3,1,0,2:T(8,128)S(1)} %slice_bitcast_fusion.18, f32[6,15,1,130]{3,1,0,2:T(8,128)S(1)} %slice_bitcast_fusion.4, f32[6,1,1,130]{3,1,0,2:T(1,128)S(1)} %slice_bitcast_fusion.28, f32[6,16,1,129]{3,1,0,2:T(8,128)S(1)} %fusion.79, ...), kind=kLoop, calls=%fused_computation.154 | loop fusion | flops 2283840 | bytes 2446306 | tf_op jit(solution)/shard_map/add | solution.py:114
  45.4 3.8 %fusion.4 = (f32[32,128]{1,0:T(8,128)S(1)}, f32[32,128]{1,0:T(8,128)S(1)}, f32[32,128]{1,0:T(8,128)S(1)}) fusion(f32[32,128]{1,0:T(8,128)S(1)} %get-tuple-element.144, f32[32,128]{1,0:T(8,128)S(1)} %bitcast.1036, f32[32,128]{1,0:T(8,128)S(1)} %get-tuple-element.145, f32[32,128]{1,0:T(8,128)S(1)} %bitcast.1035, f32[32,128]{1,0:T(8,128)S(1)} %get-tuple-element.143, ...), kind=kLoop, calls=%fused_computation.14 | loop fusion | flops 7852032 | bytes 147456 | tf_op jit(solution)/shard_map/while/body/eval_jaxpr/reduce_sum | solution.py:123
  49.2 0.9 %multiply_add_fusion = (f32[4,16,3,128]{3,1,2,0:T(8,128)}, f32[4,16,3,128]{3,1,2,0:T(8,128)}) fusion(f32[4,16,3,128]{3,1,2,0:T(8,128)S(1)} %copy-done, f32[4,16,3,128]{3,1,2,0:T(8,128)S(1)} %copy-done.4, f32[32,1,128]{2,0,1:T(8,128)S(1)} %bitcast.1032, f32[32,1,128]{2,0,1:T(8,128)S(1)} %bitcast.1033, f32[32,1,128]{2,0,1:T(8,128)S(1)} %bitcast.1031, ...), kind=kOutput, calls=%fused_computation.390 | convolution fusion | flops 9650176 | bytes 592672 | tf_op jit(solution)/shard_map/kp,kcx->pcx/dot_general | solution.py:209
  (129 shorter events, 2.7 us)
Async XLA Ops:
  4.3 14.6 %all-to-all-start = ((f32[8,1,4]{2,1,0:T(1,128)}), f32[8,1,4]{2,1,0:T(1,128)S(1)}, u32[]{:S(2)}, u32[]{:S(2)}) async-start(f32[8,1,4]{2,1,0:T(1,128)} %bitcast.104), calls=%async_computation | async-start | bytes 8192 | tf_op jit(solution)/shard_map/all_to_all | solution.py:195
  10.6 5.4 %copy-start = (f32[4,16,3,128]{3,1,2,0:T(8,128)S(1)}, f32[4,16,3,128]{3,1,2,0:T(8,128)}, u32[]{:S(2)}) copy-start(f32[4,16,3,128]{3,1,2,0:T(8,128)} %param.7) | copy-start | bytes 294916
  11.6 4.5 %copy-start.5 = (f32[1,1,3,16]{3,1,2,0:T(1,128)S(1)}, f32[1,1,3,16]{3,1,2,0:T(1,128)}, u32[]{:S(2)}) copy-start(f32[1,1,3,16]{3,1,2,0:T(1,128)} %param.13) | copy-start | bytes 580
  11.7 12.5 %collective-permute-start = (f32[4,16,5,1]{3,1,0,2:T(8,128)S(1)}, f32[4,16,5,1]{3,1,0,2:T(8,128)S(1)}, u32[]{:S(2)}, u32[]{:S(2)}) collective-permute-start(f32[4,16,5,1]{3,1,0,2:T(8,128)S(1)} %get-tuple-element.108), channel_id=1, source_target_pairs={{0,4},{4,8},{8,12},{12,16},{16,20},{20,24},{24,28},{28,0},{1,5},{5... | collective-permute-start | bytes 3848 | tf_op jit(solution)/shard_map/ppermute | solution.py:33
  13.2 11.0 %collective-permute-start.1 = (f32[4,16,5,1]{3,1,0,2:T(8,128)S(1)}, f32[4,16,5,1]{3,1,0,2:T(8,128)S(1)}, u32[]{:S(2)}, u32[]{:S(2)}) collective-permute-start(f32[4,16,5,1]{3,1,0,2:T(8,128)S(1)} %get-tuple-element.109), channel_id=1, source_target_pairs={{4,0},{8,4},{12,8},{16,12},{20,16},{24,20},{28,24},{0,28},{5,1},{9... | collective-permute-start | bytes 3848 | tf_op jit(solution)/shard_map/ppermute | solution.py:35
  16.4 7.9 %copy-start.1 = (f32[4,16,128]{2,1,0:T(8,128)S(1)}, f32[4,16,128]{2,1,0:T(8,128)}, u32[]{:S(2)}) copy-start(f32[4,16,128]{2,1,0:T(8,128)} %param.10) | copy-start | bytes 98308
  16.4 7.9 %copy-start.2 = (f32[4,16,128]{2,1,0:T(8,128)S(1)}, f32[4,16,128]{2,1,0:T(8,128)}, u32[]{:S(2)}) copy-start(f32[4,16,128]{2,1,0:T(8,128)} %param.9) | copy-start | bytes 98308
  18.8 26.5 %all-to-all-start.1 = ((f32[8,4,3,128]{3,1,2,0:T(4,128)}), f32[8,4,3,128]{3,1,2,0:T(4,128)S(1)}, u32[]{:S(2)}, u32[]{:S(2)}) async-start(f32[8,4,3,128]{3,1,2,0:T(4,128)} %copy.222), calls=%async_computation.1 | async-start | bytes 98304 | tf_op jit(solution)/shard_map/all_to_all | solution.py:188
  24.4 4.1 %collective-permute-start.2 = (f32[1,16,5,130]{3,1,0,2:T(8,128)S(1)}, f32[1,16,5,130]{3,1,0,2:T(8,128)S(1)}, u32[]{:S(2)}, u32[]{:S(2)}) collective-permute-start(f32[1,16,5,130]{3,1,0,2:T(8,128)S(1)} %get-tuple-element.106), channel_id=1, source_target_pairs={{0,1},{1,2},{2,3},{3,0},{4,5},{5,6},{6,7},{7,4},{8,9},{9,10},{10,1... | collective-permute-start | bytes 124808 | tf_op jit(solution)/shard_map/ppermute | solution.py:33
  27.0 3.9 %collective-permute-start.3 = (f32[1,16,5,130]{3,1,0,2:T(8,128)S(1)}, f32[1,16,5,130]{3,1,0,2:T(8,128)S(1)}, u32[]{:S(2)}, u32[]{:S(2)}) collective-permute-start(f32[1,16,5,130]{3,1,0,2:T(8,128)S(1)} %get-tuple-element.107), channel_id=1, source_target_pairs={{1,0},{2,1},{3,2},{0,3},{5,4},{6,5},{7,6},{4,7},{9,8},{10,9},{11,1... | collective-permute-start | bytes 124808 | tf_op jit(solution)/shard_map/ppermute | solution.py:35
  38.2 1.3 %copy-start.3 = (f32[6,16,130]{2,1,0:T(8,128)}, f32[6,16,130]{2,1,0:T(8,128)S(1)}, u32[]{:S(2)}) copy-start(f32[6,16,130]{2,1,0:T(8,128)S(1)} %subtract_subtract_fusion) | copy-start | bytes 149764
  39.5 0.7 %slice-start = ((f32[6,16,130]{2,1,0:T(8,128)}), f32[1,16,130]{2,1,0:T(8,128)S(1)}, s32[]{:S(2)}) async-start(f32[6,16,130]{2,1,0:T(8,128)} %copy-done.3), calls=%async_computation.2 | async-start | bytes 32768 | tf_op jit(solution)/shard_map/jit(_roll_static)/slice | solution.py:114
  39.5 0.9 %slice-start.1 = ((f32[6,16,130]{2,1,0:T(8,128)}), f32[5,16,130]{2,1,0:T(8,128)S(1)}, s32[]{:S(2)}) async-start(f32[6,16,130]{2,1,0:T(8,128)} %copy-done.3), calls=%async_computation.3 | async-start | bytes 163840 | tf_op jit(solution)/shard_map/jit(_roll_static)/slice | solution.py:114
  45.4 3.8 %copy-start.4 = (f32[4,16,3,128]{3,1,2,0:T(8,128)S(1)}, f32[4,16,3,128]{3,1,2,0:T(8,128)}, u32[]{:S(2)}) copy-start(f32[4,16,3,128]{3,1,2,0:T(8,128)} %param.8) | copy-start | bytes 294916
where the time goes:
time: 50.5 us; the launch traced here: 50.1 us
  other arithmetic  19.6 us (39%)
  starting transfers between devices  16.7 us (33%)
  local copies, waits for them, and re-layouts  6.76 us (13%)
  waiting for transfers between devices  3.87 us (8%)
  between operations  2.34 us (5%)
  matrix products  0.93 us (2%)
    all_to_all x1, starting transfers between devices, local(): lax.all_to_all(labels.reshape(regions, CAP), 'region', split_axis=0, conc...  6.37 us
    ppermute x2, starting transfers between devices, with_halo(): lax.ppermute(tail, axis, [(i, (i + 1) % count) for i in range(count)])  4.18 us
    reduce_sum x1, other arithmetic, pair_forces(): jnp.sum(delta * kernel, axis=2)  3.82 us
    all_to_all x1, starting transfers between devices, local(): lax.all_to_all(outgoing.reshape(regions, CAP, 3, patch_len), 'region', sp...  3.35 us
    ppermute x2, starting transfers between devices, with_halo(): lax.ppermute(head, axis, [((i + 1) % count, i) for i in range(count)])  2.77 us
    add x3, other arithmetic, cell_forces(): summed = summed + jnp.roll(totals[offset][row], offset, axis=(0, 1, 2))  2.72 us
    sub x3, other arithmetic, cell_forces(): totals[summit][row] = totals[summit][row] - col_third  2.38 us
    ppermute x2, waiting for transfers between devices, with_halo(): lax.ppermute(head, axis, [((i + 1) % count, i) for i in range(count)])  2.38 us
  transfers between devices with their start and end apart: 6, of which 2 were waited for; matrix products, arithmetic and copies ran while one was open for 37% of the time, Pallas kernels for 0%

commit v1 on v0

v1 whole, which is shorter than its diff:
```python
import functools

import jax
import jax.numpy as jnp
from jax import lax
from jax.experimental import pallas as pl
from jax.experimental.pallas import tpu as pltpu
from jax.sharding import PartitionSpec as P

CAP = 4
STEP_TIME = 0.2
REST_VOLUME = 1.0 / 6.0
PERMUTATIONS = ((0, 1, 2), (0, 2, 1), (1, 0, 2), (1, 2, 0), (2, 0, 1), (2, 1, 0))
ROWS = 4

VMEM = pl.BlockSpec(memory_space=pltpu.VMEM)
SMEM = pl.BlockSpec(memory_space=pltpu.SMEM)


def add(total, term):
    return term if total is None else total + term


def unit(axis):
    return tuple(1 if position == 2 - axis else 0 for position in range(3))


def tensions(edges, growth, scale_side, scale_up):
    inverse = 1.0 / growth
    columns = {}
    for (axis, start), rows in edges.items():
        made = []
        for row in range(3):
            value = rows[row] + 1.0 if row == axis else rows[row]
            made.append(value * inverse if axis < 2 else value)
        columns[(axis, start)] = made
    pulls = {}
    for first, second, third in PERMUTATIONS:
        middle = unit(first)
        upper = tuple(a + b for a, b in zip(middle, unit(second)))
        keys = {first: (first, (0, 0, 0)), second: (second, middle), third: (third, upper)}
        fe = [[columns[keys[col]][row] for col in range(3)] for row in range(3)]
        cof = [
            [
                fe[(row + 1) % 3][(col + 1) % 3] * fe[(row + 2) % 3][(col + 2) % 3]
                - fe[(row + 1) % 3][(col + 2) % 3] * fe[(row + 2) % 3][(col + 1) % 3]
                for col in range(3)
            ]
            for row in range(3)
        ]
        jacobian = fe[0][0] * cof[0][0] + fe[0][1] * cof[0][1] + fe[0][2] * cof[0][2]
        pressure = 4.0 * jacobian - 5.0
        for col in range(3):
            key = keys[col]
            for row in range(3):
                pulls.setdefault(key, [None] * 3)
                pulls[key][row] = add(pulls[key][row], fe[row][col] + pressure * cof[row][col])
    return {
        key: [value * (scale_side if key[0] < 2 else scale_up) for value in rows]
        for key, rows in pulls.items()
    }


def roll(value, shift, axis):
    size = value.shape[axis]
    shift = shift % size
    return value if shift == 0 else pltpu.roll(value, shift, axis)


def lane_of(shape):
    return lax.broadcasted_iota(jnp.int32, shape, len(shape) - 1)


def column_pack(fields, lane_from, stride, offset):
    shape = fields[0][0].shape
    lane = lane_of(shape)
    packed = jnp.zeros(shape, jnp.float32)
    for c, layers in enumerate(fields):
        for z, field in enumerate(layers):
            to = c * stride + z + offset
            packed = jnp.where(lane == to, roll(field, to - lane_from, 1), packed)
    return packed


def pack_kernel(dims, disp, growth, shear, slots, count, packet, z_up, z_down, table, face):
    slab_len, width_y, patch_len, regions, slabs, pairs = dims
    region = lax.axis_index("region")
    depth = lax.axis_index("depth")
    patches = slab_len * width_y
    stride = slab_len + 2
    live_slots = count[0, 0]

    z_up[0:3] = disp[slab_len - 1]
    z_up[3] = growth[slab_len - 1]
    z_up[4] = shear[slab_len - 1]
    z_down[...] = disp[0]

    def order_key(k):
        own, other, far = slots[0, 0, 0, k], slots[0, 1, 0, k], slots[0, 2, 0, k]
        code = jnp.where(other > region, own * patches + far, far * patches + own)
        code = (other * (patches * patches) + code) * pairs + k
        return jnp.where(k < live_slots, code, -1)

    def place(k, keys):
        own, other = slots[0, 0, 0, k], slots[0, 1, 0, k]
        mine = keys[k] if isinstance(k, int) else order_key(k)
        floor = other * (patches * patches * pairs)
        if isinstance(k, int):
            rank = jnp.int32(0)
            for t in range(pairs):
                if t != k:
                    rank = rank + jnp.where((keys[t] >= floor) & (keys[t] < mine), 1, 0)
        else:

            def count_one(t, rank):
                key = order_key(t)
                return rank + jnp.where((key >= floor) & (key < mine), 1, 0)

            rank = lax.fori_loop(0, pairs, count_one, jnp.int32(0))
        rank = jnp.minimum(rank, CAP - 1)
        live = k < live_slots
        target = (jnp.where(live, other, region) * slabs + depth) * CAP + jnp.where(live, rank, 0)
        table[0, k] = target
        z, y = own // width_y, own % width_y
        for c in range(3):
            packet[target, c : c + 1, :] = disp[z, c, pl.ds(y, 1), :]

    if pairs <= 16:
        keys = [order_key(k) for k in range(pairs)]
        for k in range(pairs):
            place(k, keys)
    else:

        def place_one(k, carry):
            place(k, None)
            return carry

        lax.fori_loop(0, pairs, place_one, 0)

    groups = width_y // CAP
    width = patch_len // groups
    fields = [[disp[z, c] for z in range(slab_len)] for c in range(3)]
    fields = fields + [[growth[z] for z in range(slab_len)], [shear[z] for z in range(slab_len)]]
    sides = ((patch_len - 1, fields, 1), (0, fields[:3], regions - 1))
    lane = lane_of((CAP, patch_len))
    for side, (lane_from, chosen, step) in enumerate(sides):
        face[side] = column_pack(chosen, lane_from, stride, 1)
        folded = jnp.zeros((CAP, patch_len), jnp.float32)
        for g in range(groups):
            part = roll(face[side, g * CAP : (g + 1) * CAP, :], g * width, 1)
            folded = jnp.where((lane >= g * width) & (lane < (g + 1) * width), part, folded)
        other = lax.rem(region + step, regions)
        for s in range(slabs):
            base = (other * slabs + s) * CAP
            for j in range(CAP):
                packet[base + j, 3:4, :] = folded[j : j + 1, :]


def inner_kernel(
    dims, disp, growth, shear, velocity, below, above, slots, before, near, own_columns
):
    slab_len, width_y, patch_len, regions, slabs, pairs = dims
    depth = lax.axis_index("depth")
    shape = (width_y, patch_len)
    lane = lane_of(shape)
    row_y = lax.broadcasted_iota(jnp.int32, shape, 0)
    inside = (lane < patch_len - 1) & (row_y < width_y - 1)
    nodes = [[below[c] for c in range(3)]]
    nodes += [[disp[z, c] for c in range(3)] for z in range(slab_len)]
    nodes += [[above[c] for c in range(3)]]
    has_below = depth > 0
    has_above = depth < slabs - 1
    cell_growth = [jnp.where(has_below, below[3], 1.0)] + [growth[z] for z in range(slab_len)]
    cell_shear = [below[4]] + [shear[z] for z in range(slab_len)]

    own_columns[0] = column_pack(
        [[nodes[z][c] for z in range(slab_len + 2)] for c in range(3)]
        + [cell_growth, cell_shear],
        patch_len - 1,
        slab_len + 2,
        0,
    )
    own_columns[1] = column_pack(
        [[nodes[z][c] for z in range(slab_len + 2)] for c in range(3)], 0, slab_len + 2, 0
    )

    axis_x, axis_y, axis_z = 0, 1, 2
    pull_x = [[None] * 3 for _ in range(slab_len + 2)]
    pull_y = [[None] * 3 for _ in range(slab_len + 2)]
    pull_z = [[None] * 3 for _ in range(slab_len + 2)]

    def layer_edges(layer):
        along_x, along_y, moved = {}, {}, {}
        for c in range(3):
            base = layer[c]
            next_x = roll(base, -1, 1)
            next_y = roll(base, -1, 0)
            next_xy = roll(next_y, -1, 1)
            moved[c] = {(0, 0): base, (0, 1): next_x, (1, 0): next_y, (1, 1): next_xy}
            along_x[c] = {0: next_x - base, 1: next_xy - next_y}
            along_y[c] = {0: next_y - base, 1: next_xy - next_x}
        return along_x, along_y, moved

    low = layer_edges(nodes[0])
    for zc in range(slab_len + 1):
        high = layer_edges(nodes[zc + 1])
        edges = {}
        for dz, (along_x, along_y, _) in enumerate((low, high)):
            for other in range(2):
                edges[(axis_x, (dz, other, 0))] = [along_x[c][other] for c in range(3)]
                edges[(axis_y, (dz, 0, other))] = [along_y[c][other] for c in range(3)]
        for dy in range(2):
            for dx in range(2):
                edges[(axis_z, (0, dy, dx))] = [
                    high[2][c][(dy, dx)] - low[2][c][(dy, dx)] for c in range(3)
                ]
        growth_here = cell_growth[zc]
        valid = inside
        if zc == 0:
            valid = valid & has_below
        if zc == slab_len:
            valid = valid & has_above
        scale = jnp.where(valid, cell_shear[zc] * REST_VOLUME, 0.0) * growth_here
        pulls = tensions(edges, growth_here, scale, scale * growth_here)
        for c in range(3):
            for dz in range(2):
                near_row = pulls[(axis_x, (dz, 0, 0))][c]
                far_row = pulls[(axis_x, (dz, 1, 0))][c]
                pull_x[zc + dz][c] = add(pull_x[zc + dz][c], near_row + roll(far_row, 1, 0))
                near_row = pulls[(axis_y, (dz, 0, 0))][c]
                far_row = pulls[(axis_y, (dz, 0, 1))][c]
                pull_y[zc + dz][c] = add(pull_y[zc + dz][c], near_row + roll(far_row, 1, 1))
            at_zero = pulls[(axis_z, (0, 0, 0))][c] + roll(pulls[(axis_z, (0, 1, 0))][c], 1, 0)
            at_one = pulls[(axis_z, (0, 0, 1))][c] + roll(pulls[(axis_z, (0, 1, 1))][c], 1, 0)
            pull_z[zc][c] = at_zero + roll(at_one, 1, 1)
        low = high
        if zc > 0:
            for c in range(3):
                force = pull_x[zc][c] - roll(pull_x[zc][c], 1, 1)
                force = force + (pull_y[zc][c] - roll(pull_y[zc][c], 1, 0))
                force = force + (pull_z[zc][c] - pull_z[zc - 1][c])
                before[zc - 1, c] = velocity[zc - 1, c] + STEP_TIME * force

    def fetch(k):
        own = slots[0, 0, 0, k]
        z, y = own // width_y, own % width_y
        for c in range(3):
            near[c, pl.ds(k, 1), :] = disp[z, c, pl.ds(y, 1), :]

    if pairs <= 16:
        for k in range(pairs):
            fetch(k)
    else:

        def fetch_one(k, carry):
            fetch(k)
            return carry

        lax.fori_loop(0, pairs, fetch_one, 0)


def border_forces(dims, arrived, own_columns, unfold):
    slab_len, width_y, patch_len, regions, slabs, pairs = dims
    region = lax.axis_index("region")
    depth = lax.axis_index("depth")
    stride = slab_len + 2
    groups = width_y // CAP
    width = patch_len // groups
    half = patch_len // 2
    fold_lane = lane_of((CAP, patch_len))
    fold_z = lax.rem(lax.rem(fold_lane, width), stride)
    for side, step in enumerate((regions - 1, 1)):
        other = lax.rem(region + step, regions)

        def block(slab):
            base = (other * slabs + slab) * CAP
            return jnp.concatenate([arrived[base + j, 3:4, :] for j in range(CAP)], axis=0)

        merged = block(depth)
        lower = block(lax.rem(depth + slabs - 1, slabs))
        upper = block(lax.rem(depth + 1, slabs))
        merged = jnp.where(fold_z == 0, roll(lower, -slab_len, 1), merged)
        merged = jnp.where(fold_z == slab_len + 1, roll(upper, slab_len, 1), merged)
        for g in range(groups):
            unfold[side, g * CAP : (g + 1) * CAP, :] = roll(merged, -g * width, 1)
    from_left = unfold[0]
    from_right = unfold[1]
    own_last = own_columns[0]
    own_first = own_columns[1]
    shape = (width_y, patch_len)
    lane = lane_of(shape)
    row_y = lax.broadcasted_iota(jnp.int32, shape, 0)
    first_side = lane < half
    z_cell = jnp.where(first_side, lane, lane - half)
    z_global = depth * slab_len + z_cell - 1
    valid = (z_cell <= slab_len) & (z_global >= 0) & (z_global <= slab_len * slabs - 2)
    valid = valid & (row_y < width_y - 1)

    def joined(at_first, at_last, c):
        return jnp.where(
            first_side, roll(at_first, -c * stride, 1), roll(at_last, half - c * stride, 1)
        )

    low_x = [joined(from_left, own_last, c) for c in range(5)]
    high_x = [joined(own_first, from_right, c) for c in range(3)]
    growth = jnp.where(valid, low_x[3], 1.0)
    scale = jnp.where(valid, low_x[4] * REST_VOLUME, 0.0) * growth
    corner = {}
    for c in range(3):
        for dx, base in ((0, low_x[c]), (1, high_x[c])):
            up = roll(base, -1, 1)
            corner[(c, 0, 0, dx)] = base
            corner[(c, 0, 1, dx)] = roll(base, -1, 0)
            corner[(c, 1, 0, dx)] = up
            corner[(c, 1, 1, dx)] = roll(up, -1, 0)
    edges = {}
    for one in range(2):
        for two in range(2):
            for axis, start in ((0, (one, two, 0)), (1, (one, 0, two)), (2, (0, one, two))):
                end = tuple(a + b for a, b in zip(start, unit(axis)))
                edges[(axis, start)] = [corner[(c, *end)] - corner[(c, *start)] for c in range(3)]
    pulls = tensions(edges, growth, scale, scale * growth)
    forces = []
    for c in range(3):

        def chosen(axis, one):
            at = ((one, 0, 0), (one, 0, 1)) if axis == 1 else ((0, one, 0), (0, one, 1))
            return jnp.where(first_side, pulls[(axis, at[1])][c], pulls[(axis, at[0])][c])

        level = []
        for dz in range(2):
            both = pulls[(0, (dz, 0, 0))][c] + roll(pulls[(0, (dz, 1, 0))][c], 1, 0)
            both = jnp.where(first_side, -both, both)
            along_y = chosen(1, dz)
            level.append(both + (along_y - roll(along_y, 1, 0)))
        along_z = chosen(2, 0) + roll(chosen(2, 1), 1, 0)
        forces.append((level[0] + along_z) + roll(level[1] - along_z, 1, 1))
    return forces


def finish_kernel(
    dims,
    arrived,
    before,
    near,
    own_columns,
    disp,
    table,
    separation,
    slots,
    count,
    new_velocity,
    new_disp,
    far,
    unfold,
    pushes,
):
    slab_len, width_y, patch_len, regions, slabs, pairs = dims
    half = patch_len // 2
    patches = slab_len * width_y
    block = min(pairs, 16)

    def fetch(k):
        place = table[0, k]
        for c in range(3):
            far[c, pl.ds(k, 1), :] = arrived[place, c : c + 1, :] + separation[0, c, 0, k]

    if pairs <= 16:
        for k in range(pairs):
            fetch(k)
    else:

        def fetch_one(k, carry):
            fetch(k)
            return carry

        lax.fori_loop(0, pairs, fetch_one, 0)

    live_slots = count[0, 0]
    along = lane_of((block, patch_len)).astype(jnp.float32)
    slot_row = lax.broadcasted_iota(jnp.int32, (block, patch_len), 0)

    def contact(start):
        rows = pl.ds(start, block)
        mine = [near[c, rows, :] for c in range(3)]
        mine[0] = mine[0] + along
        theirs = [far[c, rows, :] for c in range(3)]
        theirs[0] = theirs[0] + along
        inner = 8

        def some(step, carry):
            other, total = carry
            total = list(total)
            for t in range(inner):
                delta = [mine[c] - roll(other[c], t, 1) for c in range(3)]
                square = delta[0] * delta[0] + delta[1] * delta[1] + delta[2] * delta[2]
                weight = jnp.exp(-square)
                for c in range(3):
                    total[c] = total[c] + delta[c] * weight
            return tuple(roll(value, inner, 1) for value in other), tuple(total)

        zero = jnp.zeros((block, patch_len), jnp.float32)
        _, total = lax.fori_loop(
            0, patch_len // inner, some, (tuple(theirs), (zero, zero, zero))
        )
        live = (slot_row + start) < live_slots
        for c in range(3):
            pushes[c, rows, :] = jnp.where(live, total[c], 0.0)

    if pairs <= 16:
        contact(0)
    else:

        def contact_one(step, carry):
            contact(pl.multiple_of(step * block, block))
            return carry

        lax.fori_loop(0, pairs // block, contact_one, 0)

    borders = border_forces(dims, arrived, own_columns, unfold)

    patch_row = lax.broadcasted_iota(jnp.int32, (patches, pairs), 0)
    selector = (patch_row == slots[0, 0]).astype(jnp.float32)
    lane = lane_of((width_y, patch_len))
    for c in range(3):
        push = lax.dot(
            selector,
            pushes[c],
            precision=lax.Precision.HIGHEST,
            preferred_element_type=jnp.float32,
        )
        for z in range(slab_len):
            force = push[z * width_y : (z + 1) * width_y, :]
            edge = borders[c]
            force = force + jnp.where(lane == 0, roll(edge, -(z + 1), 1), 0.0)
            last = patch_len - 1
            force = force + jnp.where(lane == last, roll(edge, last - (half + z + 1), 1), 0.0)
            speed = before[z, c] + STEP_TIME * force
            new_velocity[z, c] = speed
            new_disp[z, c] = disp[z, c] + STEP_TIME * speed


def local(displacement, velocity, growth, shear_modulus, pair_slots, pair_count, separation):
    slab_len, width_y, _, patch_len = displacement.shape
    regions = lax.axis_size("region")
    slabs = lax.axis_size("depth")
    pairs = pair_slots.shape[3]
    dims = (slab_len, width_y, patch_len, regions, slabs, pairs)
    f32 = jnp.float32
    disp = jnp.transpose(displacement, (0, 2, 1, 3))
    speed = jnp.transpose(velocity, (0, 2, 1, 3))
    slots = jnp.transpose(pair_slots, (0, 2, 1, 3))
    apart = jnp.transpose(separation, (0, 2, 1, 3))

    packet, z_up, z_down, table = pl.pallas_call(
        functools.partial(pack_kernel, dims),
        out_shape=(
            jax.ShapeDtypeStruct((regions * slabs * CAP, ROWS, patch_len), f32),
            jax.ShapeDtypeStruct((5, width_y, patch_len), f32),
            jax.ShapeDtypeStruct((3, width_y, patch_len), f32),
            jax.ShapeDtypeStruct((1, pairs), jnp.int32),
        ),
        in_specs=[VMEM, VMEM, VMEM, SMEM, SMEM],
        out_specs=(VMEM, VMEM, VMEM, SMEM),
        scratch_shapes=[pltpu.VMEM((2, width_y, patch_len), f32)],
        name="pack",
    )(disp, growth, shear_modulus, slots, pair_count)

    arrived = lax.all_to_all(packet, ("region", "depth"), 0, 0, tiled=True)
    below = lax.ppermute(z_up, "depth", [(i, i + 1) for i in range(slabs - 1)])
    above = lax.ppermute(z_down, "depth", [(i + 1, i) for i in range(slabs - 1)])

    plane = (width_y, patch_len)
    before, near, own_columns = pl.pallas_call(
        functools.partial(inner_kernel, dims),
        out_shape=(
            jax.ShapeDtypeStruct((slab_len, 3, *plane), f32),
            jax.ShapeDtypeStruct((3, pairs, patch_len), f32),
            jax.ShapeDtypeStruct((2, *plane), f32),
        ),
        in_specs=[VMEM] * 6 + [SMEM],
        out_specs=(VMEM, VMEM, VMEM),
        name="inner",
        cost_estimate=pl.CostEstimate(flops=6000 * 1024, bytes_accessed=1 << 20, transcendentals=0),
    )(disp, growth, shear_modulus, speed, below, above, slots)

    new_velocity, new_disp = pl.pallas_call(
        functools.partial(finish_kernel, dims),
        out_shape=(
            jax.ShapeDtypeStruct((slab_len, 3, *plane), f32),
            jax.ShapeDtypeStruct((slab_len, 3, *plane), f32),
        ),
        in_specs=[VMEM] * 5 + [SMEM, SMEM, VMEM, SMEM],
        out_specs=(VMEM, VMEM),
        scratch_shapes=[
            pltpu.VMEM((3, pairs, patch_len), f32),
            pltpu.VMEM((2, *plane), f32),
            pltpu.VMEM((3, pairs, patch_len), f32),
        ],
        name="finish",
    )(arrived, before, near, own_columns, disp, table, apart, slots, pair_count)
    order = (0, 2, 1, 3)
    return jnp.transpose(new_velocity, order), jnp.transpose(new_disp, order)


def solution(mesh):
    in_specs = (
        P("depth", None, None, "region"),
        P("depth", None, None, "region"),
        P("depth", None, "region"),
        P("depth", None, "region"),
        P("depth", "region", None, None),
        P("depth", "region"),
        P("depth", "region", None, None),
    )
    out_specs = (P("depth", None, None, "region"), P("depth", None, None, "region"))
    return jax.shard_map(local, mesh=mesh, in_specs=in_specs, out_specs=out_specs, check_vma=False)
```

time: 50.5 us -> 28.5 us (0.56)
  other arithmetic: 19.6 us -> 0 us
  Pallas kernels: 0 us -> 9.26 us
  local copies, waits for them, and re-layouts: 6.76 us -> 1.34 us
  starting transfers between devices: 16.7 us -> 12.6 us
  between operations: 2.34 us -> 1.35 us
  matrix products: 0.93 us -> 0 us
    pallas_call x0 -> x3, Pallas kernels: none -> 9.26 us  [the longest x1 4.38 us: local(): pl.pallas_call(functools.partial(finish_kernel, dims), out_shape=(jax.Sha...]
    add x22 -> x0, other arithmetic: 6.97 us -> none  [the longest x3 2.72 us: cell_forces(): summed = summed + jnp.roll(totals[offset][row], offset, axis=(0, 1, 2))]
    reduce_sum x2 -> x0, other arithmetic: 4.01 us -> none  [the longest x1 3.82 us: pair_forces(): jnp.sum(delta * kernel, axis=2)]
    concatenate x50 -> x0, other arithmetic: 3.66 us -> none  [the longest x26 1.64 us: shifted(): return jnp.roll(field, (-offset[0], -offset[1], -offset[2]), axis=(0, 1, 2))]
    all_to_all x2 -> x1, starting transfers between devices: 9.72 us -> 7.09 us  [local(): arrived = lax.all_to_all(packet, ('region', 'depth'), 0, 0, tiled=True)]
    sub x4 -> x0, other arithmetic: 2.46 us -> none  [the longest x3 2.38 us: cell_forces(): totals[summit][row] = totals[summit][row] - col_third]
    scatter x2 -> x0, local copies, waits for them, and re-layouts: 1.65 us -> none  [the longest x1 1.03 us: local(): outgoing = jnp.zeros((buckets, 3, patch_len), jnp.float32).at[bucket].set...]
    ppermute x4 -> x2, starting transfers between devices: 6.95 us -> 5.46 us  [the longest x1 3.54 us: local(): below = lax.ppermute(z_up, 'depth', [(i, i + 1) for i in range(slabs - 1)])]
  transfers between devices with their start and end apart: 6 -> 3, of which waited for: 2 -> 1; matrix products, arithmetic and copies ran while one was open for 37% -> 0% of each run, Pallas kernels for 0% -> 9%
where the time goes in v1:
time: 28.5 us; the launch traced here: 28.2 us
  starting transfers between devices  12.6 us (44%)
  Pallas kernels  9.26 us (32%)
  waiting for transfers between devices  3.69 us (13%)
  between operations  1.35 us (5%)
  local copies, waits for them, and re-layouts  1.34 us (5%)
    all_to_all x1, starting transfers between devices, local(): arrived = lax.all_to_all(packet, ('region', 'depth'), 0, 0, tiled=True)  7.09 us
    pallas_call x1, Pallas kernels, local(): pl.pallas_call(functools.partial(finish_kernel, dims), out_shape=(jax.Sha...  4.38 us
    ppermute x1, waiting for transfers between devices, local(): lax.ppermute(z_down, 'depth', [(i + 1, i) for i in range(slabs - 1)])  3.69 us
    ppermute x1, starting transfers between devices, local(): below = lax.ppermute(z_up, 'depth', [(i, i + 1) for i in range(slabs - 1)])  3.54 us
    pallas_call x1, Pallas kernels, local(): pl.pallas_call(functools.partial(inner_kernel, dims), out_shape=(jax.Shap...  2.49 us
    pallas_call x1, Pallas kernels, local(): pl.pallas_call(functools.partial(pack_kernel, dims), out_shape=(jax.Shape...  2.39 us
    ppermute x1, starting transfers between devices, local(): lax.ppermute(z_down, 'depth', [(i + 1, i) for i in range(slabs - 1)])  1.92 us
    unnamed x10, local copies, waits for them, and re-layouts  1.34 us
  transfers between devices with their start and end apart: 3, of which 1 were waited for; matrix products, arithmetic and copies ran while one was open for 0% of the time, Pallas kernels for 9%

profile of v1, /device:TPU:1, one launch (start us, length us, event | category | flops | bytes accessed | tf_op | source)
XLA Modules:
  0.0 28.2 jit_solution(8488858270011344906)
XLA Ops:
  1.3 2.4 %pack.1 = (f32[128,4,128]{2,1,0:T(4,128)}, f32[5,16,128]{2,1,0:T(8,128)}, f32[3,16,128]{2,1,0:T(8,128)}, s32[1,16]{1,0:T(1,128)}) custom-call(f32[4,3,16,128]{3,2,1,0:T(8,128)} %bitcast.6, f32[4,16,128]{2,1,0:T(8,128)} %growth.3, f32[4,16,128]{2,1,0:T(8,128)} %shear.3, s32[1,3,1,16]{3,2,1,0:T(1,128)} %bitcast.10, s32[1,1]{1,0:T(1,128)S(6)} %copy.9.count), custom_call_target="tpu_custom_call" | custom-call | tf_op jit(solution)/shard_map/pack/pallas_call | solution.py:455
  3.7 0.0 copy-start.3
  3.7 0.0 copy-start.4
  3.7 7.1 %all-to-all-start = ((f32[128,4,128]{2,1,0:T(4,128)}), f32[128,4,128]{2,1,0:T(4,128)S(1)}, u32[]{:S(2)}, u32[]{:S(2)}) async-start(f32[128,4,128]{2,1,0:T(4,128)} %get-tuple-element.11), calls=%async_computation | async-start | bytes 524288 | tf_op jit(solution)/shard_map/all_to_all | solution.py:469
  10.8 0.0 copy-done.3
  10.8 3.5 %collective-permute-start = (f32[5,16,128]{2,1,0:T(8,128)S(1)}, f32[5,16,128]{2,1,0:T(8,128)S(1)}, u32[]{:S(2)}, u32[]{:S(2)}) collective-permute-start(f32[5,16,128]{2,1,0:T(8,128)S(1)} %copy-done.3), channel_id=1, source_target_pairs={{0,1},{1,2},{2,3},{4,5},{5,6},{6,7},{8,9},{9,10},{10,11},{12,13},{... | collective-permute-start | bytes 122888 | tf_op jit(solution)/shard_map/ppermute | solution.py:470
  14.4 0.0 copy-done.4
  14.4 1.9 %collective-permute-start.1 = (f32[3,16,128]{2,1,0:T(8,128)S(1)}, f32[3,16,128]{2,1,0:T(8,128)S(1)}, u32[]{:S(2)}, u32[]{:S(2)}) collective-permute-start(f32[3,16,128]{2,1,0:T(8,128)S(1)} %copy-done.4), channel_id=1, source_target_pairs={{1,0},{2,1},{3,2},{5,4},{6,5},{7,6},{9,8},{10,9},{11,10},{13,12},{... | collective-permute-start | bytes 73736 | tf_op jit(solution)/shard_map/ppermute | solution.py:471
  16.3 3.7 %collective-permute-done.1.above = f32[3,16,128]{2,1,0:T(8,128)S(1)} collective-permute-done((f32[3,16,128]{2,1,0:T(8,128)S(1)}, f32[3,16,128]{2,1,0:T(8,128)S(1)}, u32[]{:S(2)}, u32[]{:S(2)}) %collective-permute-start.1) | collective-permute-done | bytes 24608 | tf_op jit(solution)/shard_map/ppermute | solution.py:471
  20.0 0.0 copy-start.2
  20.0 0.0 collective-permute-done.below
  20.0 0.0 copy-start.1
  20.0 0.6 %copy-done.2 = f32[3,16,128]{2,1,0:T(8,128)} copy-done((f32[3,16,128]{2,1,0:T(8,128)}, f32[3,16,128]{2,1,0:T(8,128)S(1)}, u32[]{:S(2)}) %copy-start.2) | copy-done | bytes 24600
  20.6 0.0 copy-done.1
  20.6 2.5 %inner.1 = (f32[4,3,16,128]{3,2,1,0:T(8,128)}, f32[3,16,128]{2,1,0:T(8,128)}, f32[2,16,128]{2,1,0:T(8,128)}) custom-call(f32[4,3,16,128]{3,2,1,0:T(8,128)} %bitcast.7, f32[4,16,128]{2,1,0:T(8,128)} %growth.3, f32[4,16,128]{2,1,0:T(8,128)} %shear.3, f32[4,3,16,128]{3,2,1,0:T(8,128)} %bitcast.9, f32[5,16,128]{2,1,0:T(8,128)} %copy-done.1, ...), custom_call_target="tpu_custom_call" | custom-call | flops 6144000 | bytes 1048576 | tf_op jit(solution)/shard_map/inner/pallas_call | solution.py:474
  23.1 0.0 all-to-all-done.arrived
  23.1 0.0 copy-start
  23.1 0.7 %copy-done = f32[128,4,128]{2,1,0:T(4,128)} copy-done((f32[128,4,128]{2,1,0:T(4,128)}, f32[128,4,128]{2,1,0:T(4,128)S(1)}, u32[]{:S(2)}) %copy-start) | copy-done | bytes 262168
  23.8 4.4 %finish.1 = (f32[4,3,16,128]{3,2,1,0:T(8,128)}, f32[4,3,16,128]{3,2,1,0:T(8,128)}) custom-call(f32[128,4,128]{2,1,0:T(4,128)} %copy-done, f32[4,3,16,128]{3,2,1,0:T(8,128)} %get-tuple-element.14.before, f32[3,16,128]{2,1,0:T(8,128)} %get-tuple-element.15.near, f32[2,16,128]{2,1,0:T(8,128)} %get-tuple-element.16.own_columns, f32[4,3,16,128]{3,2,1,0:T(8,128)} %bitcast.8, ...), custom_call_target="tpu_custom_call" | custom-call | tf_op jit(solution)/shard_map/finish/pallas_call | solution.py:487
Async XLA Ops:
  3.7 7.1 %copy-start.3 = (f32[5,16,128]{2,1,0:T(8,128)S(1)}, f32[5,16,128]{2,1,0:T(8,128)}, u32[]{:S(2)}) copy-start(f32[5,16,128]{2,1,0:T(8,128)} %get-tuple-element.12) | copy-start | bytes 122884
  3.7 10.7 %copy-start.4 = (f32[3,16,128]{2,1,0:T(8,128)S(1)}, f32[3,16,128]{2,1,0:T(8,128)}, u32[]{:S(2)}) copy-start(f32[3,16,128]{2,1,0:T(8,128)} %get-tuple-element.13) | copy-start | bytes 73732
  3.7 19.4 %all-to-all-start = ((f32[128,4,128]{2,1,0:T(4,128)}), f32[128,4,128]{2,1,0:T(4,128)S(1)}, u32[]{:S(2)}, u32[]{:S(2)}) async-start(f32[128,4,128]{2,1,0:T(4,128)} %get-tuple-element.11), calls=%async_computation | async-start | bytes 524288 | tf_op jit(solution)/shard_map/all_to_all | solution.py:469
  10.8 9.2 %collective-permute-start = (f32[5,16,128]{2,1,0:T(8,128)S(1)}, f32[5,16,128]{2,1,0:T(8,128)S(1)}, u32[]{:S(2)}, u32[]{:S(2)}) collective-permute-start(f32[5,16,128]{2,1,0:T(8,128)S(1)} %copy-done.3), channel_id=1, source_target_pairs={{0,1},{1,2},{2,3},{4,5},{5,6},{6,7},{8,9},{9,10},{10,11},{12,13},{... | collective-permute-start | bytes 122888 | tf_op jit(solution)/shard_map/ppermute | solution.py:470
  14.4 5.6 %collective-permute-start.1 = (f32[3,16,128]{2,1,0:T(8,128)S(1)}, f32[3,16,128]{2,1,0:T(8,128)S(1)}, u32[]{:S(2)}, u32[]{:S(2)}) collective-permute-start(f32[3,16,128]{2,1,0:T(8,128)S(1)} %copy-done.4), channel_id=1, source_target_pairs={{1,0},{2,1},{3,2},{5,4},{6,5},{7,6},{9,8},{10,9},{11,10},{13,12},{... | collective-permute-start | bytes 73736 | tf_op jit(solution)/shard_map/ppermute | solution.py:471
  20.0 0.6 %copy-start.2 = (f32[3,16,128]{2,1,0:T(8,128)}, f32[3,16,128]{2,1,0:T(8,128)S(1)}, u32[]{:S(2)}) copy-start(f32[3,16,128]{2,1,0:T(8,128)S(1)} %collective-permute-done.1.above) | copy-start | bytes 73732
  20.0 0.6 %copy-start.1 = (f32[5,16,128]{2,1,0:T(8,128)}, f32[5,16,128]{2,1,0:T(8,128)S(1)}, u32[]{:S(2)}) copy-start(f32[5,16,128]{2,1,0:T(8,128)S(1)} %collective-permute-done.below) | copy-start | bytes 122884
  23.1 0.7 %copy-start = (f32[128,4,128]{2,1,0:T(4,128)}, f32[128,4,128]{2,1,0:T(4,128)S(1)}, u32[]{:S(2)}) copy-start(f32[128,4,128]{2,1,0:T(4,128)S(1)} %all-to-all-done.arrived) | copy-start | bytes 786436

commit v2 on v1

--- a/solution.py
+++ b/solution.py
@@ -1,4 +1,5 @@
 import functools
+import math
 
 import jax
 import jax.numpy as jnp
@@ -15,6 +16,10 @@
 
 VMEM = pl.BlockSpec(memory_space=pltpu.VMEM)
 SMEM = pl.BlockSpec(memory_space=pltpu.SMEM)
+HBM = pl.BlockSpec(memory_space=pltpu.HBM)
+PARAMS = pltpu.CompilerParams(vmem_limit_bytes=16 << 20)
+UNROLL = 32
+ROOT = math.sqrt(math.log2(math.e))
 
 
 def add(total, term):
@@ -82,60 +87,85 @@
     return packed
 
 
-def pack_kernel(dims, disp, growth, shear, slots, count, packet, z_up, z_down, table, face):
+def each(count, body, unrolled):
+    if count <= unrolled:
+        for index in range(count):
+            body(index)
+    else:
+
+        def one(index, carry):
+            body(index)
+            return carry
+
+        lax.fori_loop(0, count, one, 0)
+
+
+def pack_kernel(
+    dims,
+    disp_in,
+    growth_in,
+    shear_in,
+    slots_in,
+    packet,
+    face_a,
+    face_b,
+    disp,
+    growth,
+    shear,
+    slots,
+    counted,
+    face,
+    sems,
+):
     slab_len, width_y, patch_len, regions, slabs, pairs = dims
     region = lax.axis_index("region")
     depth = lax.axis_index("depth")
-    patches = slab_len * width_y
     stride = slab_len + 2
-    live_slots = count[0, 0]
-
-    z_up[0:3] = disp[slab_len - 1]
-    z_up[3] = growth[slab_len - 1]
-    z_up[4] = shear[slab_len - 1]
-    z_down[...] = disp[0]
-
-    def order_key(k):
-        own, other, far = slots[0, 0, 0, k], slots[0, 1, 0, k], slots[0, 2, 0, k]
-        code = jnp.where(other > region, own * patches + far, far * patches + own)
-        code = (other * (patches * patches) + code) * pairs + k
-        return jnp.where(k < live_slots, code, -1)
-
-    def place(k, keys):
+    moves = [
+        pltpu.make_async_copy(source, target, sems.at[index])
+        for index, (source, target) in enumerate(
+            ((slots_in, slots), (disp_in, disp), (growth_in, growth), (shear_in, shear))
+        )
+    ]
+    for move in moves:
+        move.start()
+    tall = CAP * ROWS
+    blank = jnp.zeros((tall, patch_len), jnp.float32)
+
+    def base_of(m, slab):
+        return pl.multiple_of((m * slabs + slab) * tall, tall)
+
+    def clear(m):
+        counted[m] = 0
+        packet[pl.ds(base_of(m, depth), tall), :] = blank
+
+    each(regions, clear, 16)
+    moves[0].wait()
+    moves[1].wait()
+
+    def place(k):
         own, other = slots[0, 0, 0, k], slots[0, 1, 0, k]
-        mine = keys[k] if isinstance(k, int) else order_key(k)
-        floor = other * (patches * patches * pairs)
-        if isinstance(k, int):
-            rank = jnp.int32(0)
-            for t in range(pairs):
-                if t != k:
-                    rank = rank + jnp.where((keys[t] >= floor) & (keys[t] < mine), 1, 0)
-        else:
-
-            def count_one(t, rank):
-                key = order_key(t)
-                return rank + jnp.where((key >= floor) & (key < mine), 1, 0)
-
-            rank = lax.fori_loop(0, pairs, count_one, jnp.int32(0))
-        rank = jnp.minimum(rank, CAP - 1)
-        live = k < live_slots
-        target = (jnp.where(live, other, region) * slabs + depth) * CAP + jnp.where(live, rank, 0)
-        table[0, k] = target
+        position = counted[other]
+        counted[other] = position + 1
+        fits = position < CAP
+        base = (jnp.where(fits, other, region) * slabs + depth) * tall
+        base = base + jnp.where(fits, position, 0) * ROWS
         z, y = own // width_y, own % width_y
         for c in range(3):
-            packet[target, c : c + 1, :] = disp[z, c, pl.ds(y, 1), :]
-
-    if pairs <= 16:
-        keys = [order_key(k) for k in range(pairs)]
-        for k in range(pairs):
-            place(k, keys)
-    else:
-
-        def place_one(k, carry):
-            place(k, None)
-            return carry
-
-        lax.fori_loop(0, pairs, place_one, 0)
+            packet[pl.ds(base + c, 1), :] = disp[z, c, pl.ds(y, 1), :]
+        label = jnp.full((1, patch_len), own, jnp.int32).astype(jnp.float32)
+        packet[pl.ds(base + 3, 1), :] = label
+
+    each(pairs, place, 16)
+    moves[2].wait()
+    moves[3].wait()
+
+    even = lax.rem(depth, 2) == 0
+    last = slab_len - 1
+    for out, from_z in ((face_a, jnp.where(even, last, 0)), (face_b, jnp.where(even, 0, last))):
+        out[0:3] = disp[from_z]
+        out[3] = growth[last]
+        out[4] = shear[last]
 
     groups = width_y // CAP
     width = patch_len // groups
@@ -151,13 +181,26 @@
             folded = jnp.where((lane >= g * width) & (lane < (g + 1) * width), part, folded)
         other = lax.rem(region + step, regions)
         for s in range(slabs):
-            base = (other * slabs + s) * CAP
-            for j in range(CAP):
-                packet[base + j, 3:4, :] = folded[j : j + 1, :]
+            rows = pl.ds(base_of(other, s) + 3, CAP, stride=ROWS)
+            packet[rows, :] = jnp.where(lane < patch_len - 1, folded, packet[rows, :])
 
 
 def inner_kernel(
-    dims, disp, growth, shear, velocity, below, above, slots, before, near, own_columns
+    dims,
+    disp,
+    growth,
+    shear,
+    velocity,
+    face_a,
+    face_b,
+    slots,
+    slot_row,
+    count,
+    separation,
+    before,
+    near,
+    own_columns,
+    selector,
 ):
     slab_len, width_y, patch_len, regions, slabs, pairs = dims
     depth = lax.axis_index("depth")
@@ -165,9 +208,12 @@
     lane = lane_of(shape)
     row_y = lax.broadcasted_iota(jnp.int32, shape, 0)
     inside = (lane < patch_len - 1) & (row_y < width_y - 1)
-    nodes = [[below[c] for c in range(3)]]
+    even = lax.rem(depth, 2) == 0
+    below = [jnp.where(even, face_b[c], face_a[c]) for c in range(5)]
+    above = [jnp.where(even, face_a[c], face_b[c]) for c in range(3)]
+    nodes = [below[0:3]]
     nodes += [[disp[z, c] for c in range(3)] for z in range(slab_len)]
-    nodes += [[above[c] for c in range(3)]]
+    nodes += [above]
     has_below = depth > 0
     has_above = depth < slabs - 1
     cell_growth = [jnp.where(has_below, below[3], 1.0)] + [growth[z] for z in range(slab_len)]
@@ -241,22 +287,21 @@
                 force = force + (pull_z[zc][c] - pull_z[zc - 1][c])
                 before[zc - 1, c] = velocity[zc - 1, c] + STEP_TIME * force
 
+    along = lane_of((1, patch_len)).astype(jnp.float32)
+
     def fetch(k):
         own = slots[0, 0, 0, k]
         z, y = own // width_y, own % width_y
         for c in range(3):
-            near[c, pl.ds(k, 1), :] = disp[z, c, pl.ds(y, 1), :]
-
-    if pairs <= 16:
-        for k in range(pairs):
-            fetch(k)
-    else:
-
-        def fetch_one(k, carry):
-            fetch(k)
-            return carry
-
-        lax.fori_loop(0, pairs, fetch_one, 0)
+            point = disp[z, c, pl.ds(y, 1), :]
+            if c == 0:
+                point = point + along
+            near[c, pl.ds(k, 1), :] = (point - separation[0, c, 0, k]) * ROOT
+
+    each(pairs, fetch, 16)
+    patch_row = lax.broadcasted_iota(jnp.int32, selector.shape, 0)
+    live = lax.broadcasted_iota(jnp.int32, selector.shape, 1) < count[0, 0]
+    selector[...] = jnp.where((patch_row == slot_row[0, 0]) & live, 1.0, 0.0)
 
 
 def border_forces(dims, arrived, own_columns, unfold):
@@ -273,8 +318,8 @@
         other = lax.rem(region + step, regions)
 
         def block(slab):
-            base = (other * slabs + slab) * CAP
-            return jnp.concatenate([arrived[base + j, 3:4, :] for j in range(CAP)], axis=0)
+            base = (other * slabs + slab) * (CAP * ROWS)
+            return arrived[pl.ds(base + 3, CAP, stride=ROWS), :]
 
         merged = block(depth)
         lower = block(lax.rem(depth + slabs - 1, slabs))
@@ -340,53 +385,62 @@
 
 def finish_kernel(
     dims,
+    inner,
     arrived,
     before,
     near,
     own_columns,
     disp,
-    table,
-    separation,
+    selector,
     slots,
-    count,
     new_velocity,
     new_disp,
     far,
     unfold,
     pushes,
+    tiles,
 ):
     slab_len, width_y, patch_len, regions, slabs, pairs = dims
     half = patch_len // 2
-    patches = slab_len * width_y
     block = min(pairs, 16)
-
-    def fetch(k):
-        place = table[0, k]
-        for c in range(3):
-            far[c, pl.ds(k, 1), :] = arrived[place, c : c + 1, :] + separation[0, c, 0, k]
-
-    if pairs <= 16:
-        for k in range(pairs):
-            fetch(k)
-    else:
-
-        def fetch_one(k, carry):
-            fetch(k)
-            return carry
-
-        lax.fori_loop(0, pairs, fetch_one, 0)
-
-    live_slots = count[0, 0]
+    depth = lax.axis_index("depth")
+    tall = CAP * ROWS
+
+    def take(m):
+        rows = pl.ds(pl.multiple_of((m * slabs + depth) * tall, tall), tall)
+        tiles[pl.ds(pl.multiple_of(m * tall, tall), tall), :] = arrived[rows, :]
+
+    each(regions, take, 16)
+
+    total_tiles = regions * CAP
+    wide = (total_tiles, pairs)
+    label = tiles[pl.ds(3, total_tiles, stride=ROWS), :][:, patch_len - 1 :]
+    label = jnp.broadcast_to(label, (total_tiles, max(pairs, patch_len)))
+    tile_row = lax.broadcasted_iota(jnp.int32, label.shape, 0)
+    again = tile_row < 0
+    for back in range(1, CAP):
+        same = (roll(label, back, 0) == label) & (lax.rem(tile_row, CAP) >= back)
+        again = again | same
+    label = jnp.where(again, -1.0, label)[:, 0:pairs]
+    tile_row = lax.broadcasted_iota(jnp.int32, wide, 0) // CAP
+    wanted = (tile_row == slots[0, 1]) & (label == slots[0, 2].astype(jnp.float32))
+    chosen = jnp.where(wanted, 1.0, 0.0)
+    for c in range(3):
+        far[c] = lax.dot_general(
+            chosen,
+            tiles[pl.ds(c, total_tiles, stride=ROWS), :],
+            (((0,), (0,)), ((), ())),
+            precision=lax.Precision.HIGHEST,
+            preferred_element_type=jnp.float32,
+        )
+    borders = border_forces(dims, arrived, own_columns, unfold)
     along = lane_of((block, patch_len)).astype(jnp.float32)
-    slot_row = lax.broadcasted_iota(jnp.int32, (block, patch_len), 0)
 
     def contact(start):
         rows = pl.ds(start, block)
         mine = [near[c, rows, :] for c in range(3)]
-        mine[0] = mine[0] + along
         theirs = [far[c, rows, :] for c in range(3)]
-        theirs[0] = theirs[0] + along
-        inner = 8
+        theirs = [(theirs[0] + along) * ROOT, theirs[1] * ROOT, theirs[2] * ROOT]
 
         def some(step, carry):
             other, total = carry
@@ -394,43 +448,34 @@
             for t in range(inner):
                 delta = [mine[c] - roll(other[c], t, 1) for c in range(3)]
                 square = delta[0] * delta[0] + delta[1] * delta[1] + delta[2] * delta[2]
-                weight = jnp.exp(-square)
+                weight = jnp.exp2(-square)
                 for c in range(3):
                     total[c] = total[c] + delta[c] * weight
-            return tuple(roll(value, inner, 1) for value in other), tuple(total)
+            if inner < patch_len:
+                other = tuple(roll(value, inner, 1) for value in other)
+            return other, tuple(total)
 
         zero = jnp.zeros((block, patch_len), jnp.float32)
-        _, total = lax.fori_loop(
-            0, patch_len // inner, some, (tuple(theirs), (zero, zero, zero))
-        )
-        live = (slot_row + start) < live_slots
+        carry = (tuple(theirs), (zero, zero, zero))
+        if inner == patch_len:
+            _, total = some(0, carry)
+        else:
+            _, total = lax.fori_loop(0, patch_len // inner, some, carry)
         for c in range(3):
-            pushes[c, rows, :] = jnp.where(live, total[c], 0.0)
-
-    if pairs <= 16:
-        contact(0)
-    else:
-
-        def contact_one(step, carry):
-            contact(pl.multiple_of(step * block, block))
-            return carry
-
-        lax.fori_loop(0, pairs // block, contact_one, 0)
-
-    borders = border_forces(dims, arrived, own_columns, unfold)
-
-    patch_row = lax.broadcasted_iota(jnp.int32, (patches, pairs), 0)
-    selector = (patch_row == slots[0, 0]).astype(jnp.float32)
+            pushes[c, rows, :] = total[c]
+
+    each(pairs // block, lambda step: contact(step * block), 1)
+
     lane = lane_of((width_y, patch_len))
     for c in range(3):
         push = lax.dot(
-            selector,
+            selector[...],
             pushes[c],
             precision=lax.Precision.HIGHEST,
             preferred_element_type=jnp.float32,
         )
         for z in range(slab_len):
-            force = push[z * width_y : (z + 1) * width_y, :]
+            force = push[z * width_y : (z + 1) * width_y, :] * (1.0 / ROOT)
             edge = borders[c]
             force = force + jnp.where(lane == 0, roll(edge, -(z + 1), 1), 0.0)
             last = patch_len - 1
@@ -447,58 +492,74 @@
     pairs = pair_slots.shape[3]
     dims = (slab_len, width_y, patch_len, regions, slabs, pairs)
     f32 = jnp.float32
+    i32 = jnp.int32
     disp = jnp.transpose(displacement, (0, 2, 1, 3))
     speed = jnp.transpose(velocity, (0, 2, 1, 3))
     slots = jnp.transpose(pair_slots, (0, 2, 1, 3))
     apart = jnp.transpose(separation, (0, 2, 1, 3))
-
-    packet, z_up, z_down, table = pl.pallas_call(
+    plane = (width_y, patch_len)
+
+    packet, face_a, face_b = pl.pallas_call(
         functools.partial(pack_kernel, dims),
         out_shape=(
-            jax.ShapeDtypeStruct((regions * slabs * CAP, ROWS, patch_len), f32),
-            jax.ShapeDtypeStruct((5, width_y, patch_len), f32),
-            jax.ShapeDtypeStruct((3, width_y, patch_len), f32),
-            jax.ShapeDtypeStruct((1, pairs), jnp.int32),
+            jax.ShapeDtypeStruct((regions * slabs * CAP * ROWS, patch_len), f32),
+            jax.ShapeDtypeStruct((5, *plane), f32),
+            jax.ShapeDtypeStruct((5, *plane), f32),
         ),
-        in_specs=[VMEM, VMEM, VMEM, SMEM, SMEM],
-        out_specs=(VMEM, VMEM, VMEM, SMEM),
-        scratch_shapes=[pltpu.VMEM((2, width_y, patch_len), f32)],
+        in_specs=[HBM] * 4,
+        out_specs=(VMEM, VMEM, VMEM),
+        scratch_shapes=[
+            pltpu.VMEM((slab_len, 3, *plane), f32),
+            pltpu.VMEM((slab_len, *plane), f32),
+            pltpu.VMEM((slab_len, *plane), f32),
+            pltpu.SMEM(slots.shape, i32),
+            pltpu.SMEM((regions,), i32),
+            pltpu.VMEM((2, *plane), f32),
+            pltpu.SemaphoreType.DMA((4,)),
+        ],
         name="pack",
-    )(disp, growth, shear_modulus, slots, pair_count)
+    )(disp, growth, shear_modulus, slots)
 
     arrived = lax.all_to_all(packet, ("region", "depth"), 0, 0, tiled=True)
-    below = lax.ppermute(z_up, "depth", [(i, i + 1) for i in range(slabs - 1)])
-    above = lax.ppermute(z_down, "depth", [(i + 1, i) for i in range(slabs - 1)])
-
-    plane = (width_y, patch_len)
-    before, near, own_columns = pl.pallas_call(
+    links = [[(i, i + 1) for i in range(first, slabs - 1, 2)] for first in (0, 1)]
+    links = [link + [(b, a) for a, b in link] for link in links]
+    face_a = lax.ppermute(face_a, "depth", links[0])
+    face_b = lax.ppermute(face_b, "depth", links[1])
+
+    face_a, pair_count = lax.optimization_barrier((face_a, pair_count))
+
+    before, near, own_columns, selector = pl.pallas_call(
         functools.partial(inner_kernel, dims),
         out_shape=(
             jax.ShapeDtypeStruct((slab_len, 3, *plane), f32),
             jax.ShapeDtypeStruct((3, pairs, patch_len), f32),
             jax.ShapeDtypeStruct((2, *plane), f32),
+            jax.ShapeDtypeStruct((slab_len * width_y, pairs), f32),
         ),
-        in_specs=[VMEM] * 6 + [SMEM],
-        out_specs=(VMEM, VMEM, VMEM),
+        in_specs=[VMEM] * 6 + [SMEM, VMEM, SMEM, SMEM],
+        out_specs=(VMEM,) * 4,
+        compiler_params=PARAMS,
         name="inner",
         cost_estimate=pl.CostEstimate(flops=6000 * 1024, bytes_accessed=1 << 20, transcendentals=0),
-    )(disp, growth, shear_modulus, speed, below, above, slots)
+    )(disp, growth, shear_modulus, speed, face_a, face_b, slots, slots, pair_count, apart)
 
     new_velocity, new_disp = pl.pallas_call(
-        functools.partial(finish_kernel, dims),
+        functools.partial(finish_kernel, dims, UNROLL if pairs <= 16 else 8),
         out_shape=(
             jax.ShapeDtypeStruct((slab_len, 3, *plane), f32),
             jax.ShapeDtypeStruct((slab_len, 3, *plane), f32),
         ),
-        in_specs=[VMEM] * 5 + [SMEM, SMEM, VMEM, SMEM],
+        in_specs=[VMEM] * 7,
         out_specs=(VMEM, VMEM),
         scratch_shapes=[
             pltpu.VMEM((3, pairs, patch_len), f32),
             pltpu.VMEM((2, *plane), f32),
             pltpu.VMEM((3, pairs, patch_len), f32),
+            pltpu.VMEM((regions * CAP * ROWS, patch_len), f32),
         ],
+        compiler_params=PARAMS,
         name="finish",
-    )(arrived, before, near, own_columns, disp, table, apart, slots, pair_count)
+    )(arrived, before, near, own_columns, disp, selector, slots)
     order = (0, 2, 1, 3)
     return jnp.transpose(new_velocity, order), jnp.transpose(new_disp, order)
 

time: 28.5 us -> 23.4 us (0.82)
  the two profiles are of different devices: /device:TPU:1 before, /device:TPU:0 now
where the time goes in v2:
time: 23.4 us; the launch traced here: 23.1 us
  starting transfers between devices  8.3 us (35%)
  waiting for transfers between devices  6.76 us (29%)
  Pallas kernels  5.97 us (26%)
  between operations  1.43 us (6%)
  local copies, waits for them, and re-layouts  0.66 us (3%)
    all_to_all x1, starting transfers between devices, local(): arrived = lax.all_to_all(packet, ('region', 'depth'), 0, 0, tiled=True)  7.33 us
    all_to_all x1, waiting for transfers between devices, local(): arrived = lax.all_to_all(packet, ('region', 'depth'), 0, 0, tiled=True)  6.76 us
    pallas_call x1, Pallas kernels, local(): pl.pallas_call(functools.partial(finish_kernel, dims, UNROLL if pairs <=...  2.5 us
    pallas_call x1, Pallas kernels, local(): pl.pallas_call(functools.partial(pack_kernel, dims), out_shape=(jax.Shape...  2 us
    pallas_call x1, Pallas kernels, local(): pl.pallas_call(functools.partial(inner_kernel, dims), out_shape=(jax.Shap...  1.47 us
    unnamed x16, local copies, waits for them, and re-layouts  0.66 us
    ppermute x1, starting transfers between devices, local(): face_b = lax.ppermute(face_b, 'depth', links[1])  0.65 us
  transfers between devices with their start and end apart: 3, of which 1 were waited for; matrix products, arithmetic and copies ran while one was open for 0% of the time, Pallas kernels for 6%

profile of v2, /device:TPU:0, one launch (start us, length us, event | category | flops | bytes accessed | tf_op | source)
XLA Modules:
  0.0 23.1 jit_solution(16485132812834919720)
XLA Ops:
  0.6 2.0 %pack.1 = (f32[512,128]{1,0:T(8,128)}, f32[5,16,128]{2,1,0:T(8,128)}, f32[5,16,128]{2,1,0:T(8,128)}) custom-call(f32[4,3,16,128]{3,2,1,0:T(8,128)} %bitcast.9, f32[4,16,128]{2,1,0:T(8,128)} %growth.1, f32[4,16,128]{2,1,0:T(8,128)} %shear.1, s32[1,3,1,16]{3,2,1,0:T(1,128)} %bitcast.13), custom_call_target="tpu_custom_call" | custom-call | tf_op jit(solution)/shard_map/pack/pallas_call | solution.py:502
  2.6 0.0 copy-start.7
  2.6 0.0 copy-start.6
  2.7 0.0 copy-start
  2.7 0.0 copy-start.1
  2.7 0.0 copy-start.2
  2.7 0.0 copy-start.3
  2.7 7.3 %all-to-all-start = ((f32[32,16,128]{2,1,0:T(8,128)}), f32[32,16,128]{2,1,0:T(8,128)S(1)}, u32[]{:S(2)}, u32[]{:S(2)}) async-start(f32[32,16,128]{2,1,0:T(8,128)} %bitcast.18), calls=%async_computation | async-start | bytes 524288 | tf_op jit(solution)/shard_map/all_to_all | solution.py:523
  10.0 0.0 copy-done.7
  10.1 0.3 %collective-permute-start = (f32[5,16,128]{2,1,0:T(8,128)S(1)}, f32[5,16,128]{2,1,0:T(8,128)S(1)}, u32[]{:S(2)}, u32[]{:S(2)}) collective-permute-start(f32[5,16,128]{2,1,0:T(8,128)S(1)} %copy-done.7), channel_id=1, source_target_pairs={{0,1},{2,3},{1,0},{3,2},{4,5},{6,7},{5,4},{7,6},{8,9},{10,11},{9,8... | collective-permute-start | bytes 122888 | tf_op jit(solution)/shard_map/ppermute | solution.py:526
  10.4 0.0 copy-done.6
  10.4 0.7 %collective-permute-start.1 = (f32[5,16,128]{2,1,0:T(8,128)S(1)}, f32[5,16,128]{2,1,0:T(8,128)S(1)}, u32[]{:S(2)}, u32[]{:S(2)}) collective-permute-start(f32[5,16,128]{2,1,0:T(8,128)S(1)} %copy-done.6), channel_id=1, source_target_pairs={{1,2},{2,1},{5,6},{6,5},{9,10},{10,9},{13,14},{14,13},{17,18},{18,... | collective-permute-start | bytes 122888 | tf_op jit(solution)/shard_map/ppermute | solution.py:527
  11.7 0.0 copy-start.4
  11.7 0.0 copy-start.5
  11.7 0.0 collective-permute-done.face_a
  11.7 0.0 collective-permute-done.1.face_b
  11.7 0.0 copy-done
  11.7 0.0 copy-done.1
  11.7 0.0 copy-done.2
  11.8 0.0 copy-done.3
  11.8 0.6 %copy-done.4 = s32[1,1,3,16]{3,1,2,0:T(1,128)S(1)} copy-done((s32[1,1,3,16]{3,1,2,0:T(1,128)S(1)}, s32[1,1,3,16]{3,1,2,0:T(1,128)}, u32[]{:S(2)}) %copy-start.4) | copy-done | bytes 216
  12.4 0.0 copy-done.5
  12.4 1.5 %inner.1 = (f32[4,3,16,128]{3,2,1,0:T(8,128)S(1)}, f32[3,16,128]{2,1,0:T(8,128)S(1)}, f32[2,16,128]{2,1,0:T(8,128)S(1)}, f32[64,16]{1,0:T(8,128)S(1)}) custom-call(f32[4,3,16,128]{3,2,1,0:T(8,128)S(1)} %bitcast.10, f32[4,16,128]{2,1,0:T(8,128)S(1)} %copy-done.1, f32[4,16,128]{2,1,0:T(8,128)S(1)} %copy-done.2, f32[4,3,16,128]{3,2,1,0:T(8,128)S(1)} %bitcast.12, ...), custom_call_target="tpu_custom_call" | custom-call | flops 6144000 | bytes 1048576 | tf_op jit(solution)/shard_map/inner/pallas_call | solution.py:531
  13.9 6.8 %all-to-all-done = f32[32,16,128]{2,1,0:T(8,128)S(1)} async-done(((f32[32,16,128]{2,1,0:T(8,128)}), f32[32,16,128]{2,1,0:T(8,128)S(1)}, u32[]{:S(2)}, u32[]{:S(2)}) %all-to-all-start) | async-done | bytes 262176 | tf_op jit(solution)/shard_map/all_to_all | solution.py:523
  20.6 2.5 %finish.1 = (f32[4,3,16,128]{3,2,1,0:T(8,128)}, f32[4,3,16,128]{3,2,1,0:T(8,128)}) custom-call(f32[512,128]{1,0:T(8,128)S(1)} %bitcast.8, f32[4,3,16,128]{3,2,1,0:T(8,128)S(1)} %get-tuple-element.18.before, f32[3,16,128]{2,1,0:T(8,128)S(1)} %get-tuple-element.19.near, f32[2,16,128]{2,1,0:T(8,128)S(1)} %get-tuple-element.20.own_columns, ...), custom_call_target="tpu_custom_call" | custom-call | tf_op jit(solution)/shard_map/finish/pallas_call | solution.py:546
Async XLA Ops:
  2.6 7.4 %copy-start.7 = (f32[5,16,128]{2,1,0:T(8,128)S(1)}, f32[5,16,128]{2,1,0:T(8,128)}, u32[]{:S(2)}) copy-start(f32[5,16,128]{2,1,0:T(8,128)} %get-tuple-element.14) | copy-start | bytes 122884
  2.6 7.7 %copy-start.6 = (f32[5,16,128]{2,1,0:T(8,128)S(1)}, f32[5,16,128]{2,1,0:T(8,128)}, u32[]{:S(2)}) copy-start(f32[5,16,128]{2,1,0:T(8,128)} %get-tuple-element.16) | copy-start | bytes 122884
  2.7 9.1 %copy-start = (f32[4,16,3,128]{3,1,2,0:T(8,128)S(1)}, f32[4,16,3,128]{3,1,2,0:T(8,128)}, u32[]{:S(2)}) copy-start(f32[4,16,3,128]{3,1,2,0:T(8,128)} %param.7) | copy-start | bytes 294916
  2.7 9.1 %copy-start.1 = (f32[4,16,128]{2,1,0:T(8,128)S(1)}, f32[4,16,128]{2,1,0:T(8,128)}, u32[]{:S(2)}) copy-start(f32[4,16,128]{2,1,0:T(8,128)} %growth.1) | copy-start | bytes 98308
  2.7 9.1 %copy-start.2 = (f32[4,16,128]{2,1,0:T(8,128)S(1)}, f32[4,16,128]{2,1,0:T(8,128)}, u32[]{:S(2)}) copy-start(f32[4,16,128]{2,1,0:T(8,128)} %shear.1) | copy-start | bytes 98308
  2.7 9.1 %copy-start.3 = (f32[4,16,3,128]{3,1,2,0:T(8,128)S(1)}, f32[4,16,3,128]{3,1,2,0:T(8,128)}, u32[]{:S(2)}) copy-start(f32[4,16,3,128]{3,1,2,0:T(8,128)} %param.8) | copy-start | bytes 294916
  2.7 17.9 %all-to-all-start = ((f32[32,16,128]{2,1,0:T(8,128)}), f32[32,16,128]{2,1,0:T(8,128)S(1)}, u32[]{:S(2)}, u32[]{:S(2)}) async-start(f32[32,16,128]{2,1,0:T(8,128)} %bitcast.18), calls=%async_computation | async-start | bytes 524288 | tf_op jit(solution)/shard_map/all_to_all | solution.py:523
  10.1 1.7 %collective-permute-start = (f32[5,16,128]{2,1,0:T(8,128)S(1)}, f32[5,16,128]{2,1,0:T(8,128)S(1)}, u32[]{:S(2)}, u32[]{:S(2)}) collective-permute-start(f32[5,16,128]{2,1,0:T(8,128)S(1)} %copy-done.7), channel_id=1, source_target_pairs={{0,1},{2,3},{1,0},{3,2},{4,5},{6,7},{5,4},{7,6},{8,9},{10,11},{9,8... | collective-permute-start | bytes 122888 | tf_op jit(solution)/shard_map/ppermute | solution.py:526
  10.4 1.3 %collective-permute-start.1 = (f32[5,16,128]{2,1,0:T(8,128)S(1)}, f32[5,16,128]{2,1,0:T(8,128)S(1)}, u32[]{:S(2)}, u32[]{:S(2)}) collective-permute-start(f32[5,16,128]{2,1,0:T(8,128)S(1)} %copy-done.6), channel_id=1, source_target_pairs={{1,2},{2,1},{5,6},{6,5},{9,10},{10,9},{13,14},{14,13},{17,18},{18,... | collective-permute-start | bytes 122888 | tf_op jit(solution)/shard_map/ppermute | solution.py:527
  11.7 0.7 %copy-start.4 = (s32[1,1,3,16]{3,1,2,0:T(1,128)S(1)}, s32[1,1,3,16]{3,1,2,0:T(1,128)}, u32[]{:S(2)}) copy-start(s32[1,1,3,16]{3,1,2,0:T(1,128)} %param.11) | copy-start | bytes 580
  11.7 0.7 %copy-start.5 = (f32[1,1,3,16]{3,1,2,0:T(1,128)S(1)}, f32[1,1,3,16]{3,1,2,0:T(1,128)}, u32[]{:S(2)}) copy-start(f32[1,1,3,16]{3,1,2,0:T(1,128)} %param.13) | copy-start | bytes 580

commit v3 on v2

--- a/solution.py
+++ b/solution.py
@@ -6,6 +6,7 @@
 from jax import lax
 from jax.experimental import pallas as pl
 from jax.experimental.pallas import tpu as pltpu
+from jax.sharding import Mesh
 from jax.sharding import PartitionSpec as P
 
 CAP = 4
@@ -18,7 +19,7 @@
 SMEM = pl.BlockSpec(memory_space=pltpu.SMEM)
 HBM = pl.BlockSpec(memory_space=pltpu.HBM)
 PARAMS = pltpu.CompilerParams(vmem_limit_bytes=16 << 20)
-UNROLL = 32
+UNROLL = 128
 ROOT = math.sqrt(math.log2(math.e))
 
 
@@ -100,6 +101,10 @@
         lax.fori_loop(0, count, one, 0)
 
 
+def slab_index():
+    return lax.axis_index("pair") * lax.axis_size("core") + lax.axis_index("core")
+
+
 def pack_kernel(
     dims,
     disp_in,
@@ -119,7 +124,9 @@
 ):
     slab_len, width_y, patch_len, regions, slabs, pairs = dims
     region = lax.axis_index("region")
-    depth = lax.axis_index("depth")
+    depth = slab_index()
+    pair = lax.axis_index("pair")
+    blocks = slabs // 2
     stride = slab_len + 2
     moves = [
         pltpu.make_async_copy(source, target, sems.at[index])
@@ -132,23 +139,23 @@
     tall = CAP * ROWS
     blank = jnp.zeros((tall, patch_len), jnp.float32)
 
-    def base_of(m, slab):
-        return pl.multiple_of((m * slabs + slab) * tall, tall)
+    def base_of(m, block):
+        return pl.multiple_of((m * blocks + block) * tall, tall)
 
     def clear(m):
         counted[m] = 0
-        packet[pl.ds(base_of(m, depth), tall), :] = blank
+        packet[pl.ds(base_of(m, pair), tall), :] = blank
 
     each(regions, clear, 16)
-    moves[0].wait()
-    moves[1].wait()
+    for move in moves:
+        move.wait()
 
     def place(k):
         own, other = slots[0, 0, 0, k], slots[0, 1, 0, k]
         position = counted[other]
         counted[other] = position + 1
         fits = position < CAP
-        base = (jnp.where(fits, other, region) * slabs + depth) * tall
+        base = (jnp.where(fits, other, region) * blocks + pair) * tall
         base = base + jnp.where(fits, position, 0) * ROWS
         z, y = own // width_y, own % width_y
         for c in range(3):
@@ -157,8 +164,6 @@
         packet[pl.ds(base + 3, 1), :] = label
 
     each(pairs, place, 16)
-    moves[2].wait()
-    moves[3].wait()
 
     even = lax.rem(depth, 2) == 0
     last = slab_len - 1
@@ -180,8 +185,8 @@
             part = roll(face[side, g * CAP : (g + 1) * CAP, :], g * width, 1)
             folded = jnp.where((lane >= g * width) & (lane < (g + 1) * width), part, folded)
         other = lax.rem(region + step, regions)
-        for s in range(slabs):
-            rows = pl.ds(base_of(other, s) + 3, CAP, stride=ROWS)
+        for block in range(blocks):
+            rows = pl.ds(base_of(other, block) + 3, CAP, stride=ROWS)
             packet[rows, :] = jnp.where(lane < patch_len - 1, folded, packet[rows, :])
 
 
@@ -203,7 +208,7 @@
     selector,
 ):
     slab_len, width_y, patch_len, regions, slabs, pairs = dims
-    depth = lax.axis_index("depth")
+    depth = slab_index()
     shape = (width_y, patch_len)
     lane = lane_of(shape)
     row_y = lax.broadcasted_iota(jnp.int32, shape, 0)
@@ -304,10 +309,13 @@
     selector[...] = jnp.where((patch_row == slot_row[0, 0]) & live, 1.0, 0.0)
 
 
-def border_forces(dims, arrived, own_columns, unfold):
+def border_forces(dims, arrived, relayed, own_columns, unfold):
     slab_len, width_y, patch_len, regions, slabs, pairs = dims
     region = lax.axis_index("region")
-    depth = lax.axis_index("depth")
+    depth = slab_index()
+    pair = lax.axis_index("pair")
+    core = lax.axis_index("core")
+    blocks = slabs // 2
     stride = slab_len + 2
     groups = width_y // CAP
     width = patch_len // groups
@@ -317,13 +325,13 @@
     for side, step in enumerate((regions - 1, 1)):
         other = lax.rem(region + step, regions)
 
-        def block(slab):
-            base = (other * slabs + slab) * (CAP * ROWS)
-            return arrived[pl.ds(base + 3, CAP, stride=ROWS), :]
-
-        merged = block(depth)
-        lower = block(lax.rem(depth + slabs - 1, slabs))
-        upper = block(lax.rem(depth + 1, slabs))
+        def columns(source, block):
+            base = (other * blocks + lax.rem(block + blocks, blocks)) * (CAP * ROWS)
+            return source[pl.ds(base + 3, CAP, stride=ROWS), :]
+
+        merged = columns(arrived, pair)
+        lower = columns(relayed, pair - 1 + core)
+        upper = columns(relayed, pair + core)
         merged = jnp.where(fold_z == 0, roll(lower, -slab_len, 1), merged)
         merged = jnp.where(fold_z == slab_len + 1, roll(upper, slab_len, 1), merged)
         for g in range(groups):
@@ -383,31 +391,15 @@
     return forces
 
 
-def finish_kernel(
-    dims,
-    inner,
-    arrived,
-    before,
-    near,
-    own_columns,
-    disp,
-    selector,
-    slots,
-    new_velocity,
-    new_disp,
-    far,
-    unfold,
-    pushes,
-    tiles,
-):
+def contact_kernel(dims, inner, arrived, near, slots, pushes, far, tiles):
     slab_len, width_y, patch_len, regions, slabs, pairs = dims
-    half = patch_len // 2
     block = min(pairs, 16)
-    depth = lax.axis_index("depth")
+    pair = lax.axis_index("pair")
+    blocks = slabs // 2
     tall = CAP * ROWS
 
     def take(m):
-        rows = pl.ds(pl.multiple_of((m * slabs + depth) * tall, tall), tall)
+        rows = pl.ds(pl.multiple_of((m * blocks + pair) * tall, tall), tall)
         tiles[pl.ds(pl.multiple_of(m * tall, tall), tall), :] = arrived[rows, :]
 
     each(regions, take, 16)
@@ -433,7 +425,6 @@
             precision=lax.Precision.HIGHEST,
             preferred_element_type=jnp.float32,
         )
-    borders = border_forces(dims, arrived, own_columns, unfold)
     along = lane_of((block, patch_len)).astype(jnp.float32)
 
     def contact(start):
@@ -466,6 +457,23 @@
 
     each(pairs // block, lambda step: contact(step * block), 1)
 
+
+def finish_kernel(
+    dims,
+    arrived,
+    relayed,
+    before,
+    pushes,
+    own_columns,
+    disp,
+    selector,
+    new_velocity,
+    new_disp,
+    unfold,
+):
+    slab_len, width_y, patch_len, regions, slabs, pairs = dims
+    half = patch_len // 2
+    borders = border_forces(dims, arrived, relayed, own_columns, unfold)
     lane = lane_of((width_y, patch_len))
     for c in range(3):
         push = lax.dot(
@@ -488,7 +496,7 @@
 def local(displacement, velocity, growth, shear_modulus, pair_slots, pair_count, separation):
     slab_len, width_y, _, patch_len = displacement.shape
     regions = lax.axis_size("region")
-    slabs = lax.axis_size("depth")
+    slabs = lax.axis_size("pair") * lax.axis_size("core")
     pairs = pair_slots.shape[3]
     dims = (slab_len, width_y, patch_len, regions, slabs, pairs)
     f32 = jnp.float32
@@ -502,7 +510,7 @@
     packet, face_a, face_b = pl.pallas_call(
         functools.partial(pack_kernel, dims),
         out_shape=(
-            jax.ShapeDtypeStruct((regions * slabs * CAP * ROWS, patch_len), f32),
+            jax.ShapeDtypeStruct((regions * (slabs // 2) * CAP * ROWS, patch_len), f32),
             jax.ShapeDtypeStruct((5, *plane), f32),
             jax.ShapeDtypeStruct((5, *plane), f32),
         ),
@@ -520,11 +528,11 @@
         name="pack",
     )(disp, growth, shear_modulus, slots)
 
-    arrived = lax.all_to_all(packet, ("region", "depth"), 0, 0, tiled=True)
+    arrived = lax.all_to_all(packet, ("region", "pair"), 0, 0, tiled=True)
     links = [[(i, i + 1) for i in range(first, slabs - 1, 2)] for first in (0, 1)]
     links = [link + [(b, a) for a, b in link] for link in links]
-    face_a = lax.ppermute(face_a, "depth", links[0])
-    face_b = lax.ppermute(face_b, "depth", links[1])
+    face_a = lax.ppermute(face_a, ("pair", "core"), links[0])
+    face_b = lax.ppermute(face_b, ("pair", "core"), links[1])
 
     face_a, pair_count = lax.optimization_barrier((face_a, pair_count))
 
@@ -543,36 +551,52 @@
         cost_estimate=pl.CostEstimate(flops=6000 * 1024, bytes_accessed=1 << 20, transcendentals=0),
     )(disp, growth, shear_modulus, speed, face_a, face_b, slots, slots, pair_count, apart)
 
+    arrived, before = lax.optimization_barrier((arrived, before))
+    relayed = lax.ppermute(arrived, ("pair", "core"), links[0])
+
+    pushes = pl.pallas_call(
+        functools.partial(contact_kernel, dims, UNROLL if pairs <= 16 else 8),
+        out_shape=jax.ShapeDtypeStruct((3, pairs, patch_len), f32),
+        in_specs=[VMEM] * 3,
+        out_specs=VMEM,
+        scratch_shapes=[
+            pltpu.VMEM((3, pairs, patch_len), f32),
+            pltpu.VMEM((regions * CAP * ROWS, patch_len), f32),
+        ],
+        compiler_params=PARAMS,
+        name="contact",
+        cost_estimate=pl.CostEstimate(flops=6000 * 1024, bytes_accessed=1 << 20, transcendentals=0),
+    )(arrived, near, slots)
+
     new_velocity, new_disp = pl.pallas_call(
-        functools.partial(finish_kernel, dims, UNROLL if pairs <= 16 else 8),
+        functools.partial(finish_kernel, dims),
         out_shape=(
             jax.ShapeDtypeStruct((slab_len, 3, *plane), f32),
             jax.ShapeDtypeStruct((slab_len, 3, *plane), f32),
         ),
         in_specs=[VMEM] * 7,
         out_specs=(VMEM, VMEM),
-        scratch_shapes=[
-            pltpu.VMEM((3, pairs, patch_len), f32),
-            pltpu.VMEM((2, *plane), f32),
-            pltpu.VMEM((3, pairs, patch_len), f32),
-            pltpu.VMEM((regions * CAP * ROWS, patch_len), f32),
-        ],
+        scratch_shapes=[pltpu.VMEM((2, *plane), f32)],
         compiler_params=PARAMS,
         name="finish",
-    )(arrived, before, near, own_columns, disp, selector, slots)
+    )(arrived, relayed, before, pushes, own_columns, disp, selector)
     order = (0, 2, 1, 3)
     return jnp.transpose(new_velocity, order), jnp.transpose(new_disp, order)
 
 
 def solution(mesh):
+    shape = dict(mesh.shape)
+    devices = mesh.devices.reshape(shape["region"], shape["depth"] // 2, 2)
+    fine = Mesh(devices, ("region", "pair", "core"))
+    depth = ("pair", "core")
     in_specs = (
-        P("depth", None, None, "region"),
-        P("depth", None, None, "region"),
-        P("depth", None, "region"),
-        P("depth", None, "region"),
-        P("depth", "region", None, None),
-        P("depth", "region"),
-        P("depth", "region", None, None),
+        P(depth, None, None, "region"),
+        P(depth, None, None, "region"),
+        P(depth, None, "region"),
+        P(depth, None, "region"),
+        P(depth, "region", None, None),
+        P(depth, "region"),
+        P(depth, "region", None, None),
     )
-    out_specs = (P("depth", None, None, "region"), P("depth", None, None, "region"))
-    return jax.shard_map(local, mesh=mesh, in_specs=in_specs, out_specs=out_specs, check_vma=False)
+    out_specs = (P(depth, None, None, "region"), P(depth, None, None, "region"))
+    return jax.shard_map(local, mesh=fine, in_specs=in_specs, out_specs=out_specs, check_vma=False)

time: 23.4 us -> 21.9 us (0.936)
  waiting for transfers between devices: 6.76 us -> 4.3 us
  starting transfers between devices: 8.3 us -> 9.43 us
    all_to_all x1, waiting for transfers between devices: 6.76 us -> 4.22 us  [local(): arrived = lax.all_to_all(packet, ('region', 'pair'), 0, 0, tiled=True)]
    all_to_all x1, starting transfers between devices: 7.33 us -> 8.48 us  [local(): arrived = lax.all_to_all(packet, ('region', 'pair'), 0, 0, tiled=True)]
    pallas_call x1 -> x2, Pallas kernels: 2.5 us -> 2.57 us  [the longest x1 1.29 us: local(): pl.pallas_call(functools.partial(contact_kernel, dims, UNROLL if pairs <=...]
    unnamed x16 -> x12, local copies, waits for them, and re-layouts: 0.66 us -> 0.6 us
    ppermute x2 -> x3, starting transfers between devices: 0.97 us -> 0.94 us  [the longest x1 0.66 us: local(): face_b = lax.ppermute(face_b, ('pair', 'core'), links[1])]
  transfers between devices with their start and end apart: 3 -> 4, of which waited for: 1 -> 2; matrix products, arithmetic and copies ran while one was open for 0% -> 0% of each run, Pallas kernels for 6% -> 13%
where the time goes in v3:
time: 21.9 us; the launch traced here: 21.6 us
  starting transfers between devices  9.43 us (43%)
  Pallas kernels  5.92 us (27%)
  waiting for transfers between devices  4.3 us (20%)
  between operations  1.4 us (6%)
  local copies, waits for them, and re-layouts  0.6 us (3%)
    all_to_all x1, starting transfers between devices, local(): arrived = lax.all_to_all(packet, ('region', 'pair'), 0, 0, tiled=True)  8.48 us
    all_to_all x1, waiting for transfers between devices, local(): arrived = lax.all_to_all(packet, ('region', 'pair'), 0, 0, tiled=True)  4.22 us
    pallas_call x1, Pallas kernels, local(): pl.pallas_call(functools.partial(pack_kernel, dims), out_shape=(jax.Shape...  1.88 us
    pallas_call x1, Pallas kernels, local(): pl.pallas_call(functools.partial(inner_kernel, dims), out_shape=(jax.Shap...  1.47 us
    pallas_call x1, Pallas kernels, local(): pl.pallas_call(functools.partial(contact_kernel, dims, UNROLL if pairs <=...  1.29 us
    pallas_call x1, Pallas kernels, local(): pl.pallas_call(functools.partial(finish_kernel, dims), out_shape=(jax.Sha...  1.27 us
    ppermute x1, starting transfers between devices, local(): face_b = lax.ppermute(face_b, ('pair', 'core'), links[1])  0.66 us
    unnamed x12, local copies, waits for them, and re-layouts  0.6 us
  transfers between devices with their start and end apart: 4, of which 2 were waited for; matrix products, arithmetic and copies ran while one was open for 0% of the time, Pallas kernels for 13%

profile of v3, /device:TPU:0, one launch (start us, length us, event | category | flops | bytes accessed | tf_op | source)
XLA Modules:
  0.0 21.6 jit_solution(18169332720998212415)
XLA Ops:
  0.6 1.9 %pack.1 = (f32[256,128]{1,0:T(8,128)}, f32[5,16,128]{2,1,0:T(8,128)}, f32[5,16,128]{2,1,0:T(8,128)}) custom-call(f32[4,3,16,128]{3,2,1,0:T(8,128)} %bitcast.11, f32[4,16,128]{2,1,0:T(8,128)} %growth.1, f32[4,16,128]{2,1,0:T(8,128)} %shear.1, s32[1,3,1,16]{3,2,1,0:T(1,128)} %bitcast.15), custom_call_target="tpu_custom_call" | custom-call | tf_op jit(solution)/shard_map/pack/pallas_call | solution.py:510
  2.5 0.0 copy-start
  2.5 0.0 copy-start.1
  2.5 0.0 copy-start.2
  2.5 0.0 copy-start.3
  2.6 8.5 %all-to-all-start = ((f32[16,16,128]{2,1,0:T(8,128)}), f32[16,16,128]{2,1,0:T(8,128)S(1)}, u32[]{:S(2)}, u32[]{:S(2)}) async-start(f32[16,16,128]{2,1,0:T(8,128)} %bitcast.20), calls=%async_computation | async-start | bytes 262144 | tf_op jit(solution)/shard_map/all_to_all | solution.py:531
  11.1 0.1 collective-permute-start
  11.1 0.7 %collective-permute-start.1 = (f32[5,16,128]{2,1,0:T(8,128)}, f32[5,16,128]{2,1,0:T(8,128)S(1)}, u32[]{:S(2)}, u32[]{:S(2)}) collective-permute-start(f32[5,16,128]{2,1,0:T(8,128)} %get-tuple-element.18), channel_id=1, source_target_pairs={{1,2},{2,1},{5,6},{6,5},{9,10},{10,9},{13,14},{14,13},{17,18},{18,... | collective-permute-start | bytes 122888 | tf_op jit(solution)/shard_map/ppermute | solution.py:535
  12.5 0.0 copy-start.4
  12.5 0.0 copy-start.5
  12.5 0.1 collective-permute-done.face_a
  12.5 0.0 collective-permute-done.1.face_b
  12.6 0.0 copy-done
  12.6 0.0 copy-done.1
  12.6 0.0 copy-done.2
  12.6 0.0 copy-done.3
  12.6 0.6 %copy-done.4 = s32[1,1,3,16]{3,1,2,0:T(1,128)S(1)} copy-done((s32[1,1,3,16]{3,1,2,0:T(1,128)S(1)}, s32[1,1,3,16]{3,1,2,0:T(1,128)}, u32[]{:S(2)}) %copy-start.4) | copy-done | bytes 216
  13.1 0.0 copy-done.5
  13.2 1.5 %inner.1 = (f32[4,3,16,128]{3,2,1,0:T(8,128)S(1)}, f32[3,16,128]{2,1,0:T(8,128)S(1)}, f32[2,16,128]{2,1,0:T(8,128)S(1)}, f32[64,16]{1,0:T(8,128)S(1)}) custom-call(f32[4,3,16,128]{3,2,1,0:T(8,128)S(1)} %bitcast.12, f32[4,16,128]{2,1,0:T(8,128)S(1)} %copy-done.1, f32[4,16,128]{2,1,0:T(8,128)S(1)} %copy-done.2, f32[4,3,16,128]{3,2,1,0:T(8,128)S(1)} %bitcast.14, ...), custom_call_target="tpu_custom_call" | custom-call | flops 6144000 | bytes 1048576 | tf_op jit(solution)/shard_map/inner/pallas_call | solution.py:539
  14.6 4.2 %all-to-all-done = f32[16,16,128]{2,1,0:T(8,128)S(1)} async-done(((f32[16,16,128]{2,1,0:T(8,128)}), f32[16,16,128]{2,1,0:T(8,128)S(1)}, u32[]{:S(2)}, u32[]{:S(2)}) %all-to-all-start) | async-done | bytes 131104 | tf_op jit(solution)/shard_map/all_to_all | solution.py:531
  18.9 0.2 collective-permute-start.2
  19.1 1.3 %contact.1.pushes = f32[3,16,128]{2,1,0:T(8,128)S(1)} custom-call(f32[256,128]{1,0:T(8,128)S(1)} %bitcast.9, f32[3,16,128]{2,1,0:T(8,128)S(1)} %get-tuple-element.23.near, s32[1,3,1,16]{3,2,1,0:T(1,128)S(1)} %bitcast.18), custom_call_target="tpu_custom_call" | custom-call | flops 6144000 | bytes 1048576 | tf_op jit(solution)/shard_map/contact/pallas_call | solution.py:557
  20.4 0.0 collective-permute-done.2.relayed
  20.4 1.3 %finish.1 = (f32[4,3,16,128]{3,2,1,0:T(8,128)}, f32[4,3,16,128]{3,2,1,0:T(8,128)}) custom-call(f32[256,128]{1,0:T(8,128)S(1)} %bitcast.10, f32[256,128]{1,0:T(8,128)S(1)} %collective-permute-done.2.relayed, f32[4,3,16,128]{3,2,1,0:T(8,128)S(1)} %get-tuple-element.22.before, f32[3,16,128]{2,1,0:T(8,128)S(1)} %contact.1.pushes, ...), custom_call_target="tpu_custom_call" | custom-call | tf_op jit(solution)/shard_map/finish/pallas_call | solution.py:571
Async XLA Ops:
  2.5 10.0 %copy-start = (f32[4,16,3,128]{3,1,2,0:T(8,128)S(1)}, f32[4,16,3,128]{3,1,2,0:T(8,128)}, u32[]{:S(2)}) copy-start(f32[4,16,3,128]{3,1,2,0:T(8,128)} %param.7) | copy-start | bytes 294916
  2.5 10.0 %copy-start.1 = (f32[4,16,128]{2,1,0:T(8,128)S(1)}, f32[4,16,128]{2,1,0:T(8,128)}, u32[]{:S(2)}) copy-start(f32[4,16,128]{2,1,0:T(8,128)} %growth.1) | copy-start | bytes 98308
  2.5 10.0 %copy-start.2 = (f32[4,16,128]{2,1,0:T(8,128)S(1)}, f32[4,16,128]{2,1,0:T(8,128)}, u32[]{:S(2)}) copy-start(f32[4,16,128]{2,1,0:T(8,128)} %shear.1) | copy-start | bytes 98308
  2.5 10.0 %copy-start.3 = (f32[4,16,3,128]{3,1,2,0:T(8,128)S(1)}, f32[4,16,3,128]{3,1,2,0:T(8,128)}, u32[]{:S(2)}) copy-start(f32[4,16,3,128]{3,1,2,0:T(8,128)} %param.8) | copy-start | bytes 294916
  2.6 16.3 %all-to-all-start = ((f32[16,16,128]{2,1,0:T(8,128)}), f32[16,16,128]{2,1,0:T(8,128)S(1)}, u32[]{:S(2)}, u32[]{:S(2)}) async-start(f32[16,16,128]{2,1,0:T(8,128)} %bitcast.20), calls=%async_computation | async-start | bytes 262144 | tf_op jit(solution)/shard_map/all_to_all | solution.py:531
  11.1 1.5 %collective-permute-start = (f32[5,16,128]{2,1,0:T(8,128)}, f32[5,16,128]{2,1,0:T(8,128)S(1)}, u32[]{:S(2)}, u32[]{:S(2)}) collective-permute-start(f32[5,16,128]{2,1,0:T(8,128)} %get-tuple-element.16), channel_id=1, source_target_pairs={{0,1},{2,3},{1,0},{3,2},{4,5},{6,7},{5,4},{7,6},{8,9},{10,11},{9,8... | collective-permute-start | bytes 122888 | tf_op jit(solution)/shard_map/ppermute | solution.py:534
  11.1 1.4 %collective-permute-start.1 = (f32[5,16,128]{2,1,0:T(8,128)}, f32[5,16,128]{2,1,0:T(8,128)S(1)}, u32[]{:S(2)}, u32[]{:S(2)}) collective-permute-start(f32[5,16,128]{2,1,0:T(8,128)} %get-tuple-element.18), channel_id=1, source_target_pairs={{1,2},{2,1},{5,6},{6,5},{9,10},{10,9},{13,14},{14,13},{17,18},{18,... | collective-permute-start | bytes 122888 | tf_op jit(solution)/shard_map/ppermute | solution.py:535
  12.5 0.7 %copy-start.4 = (s32[1,1,3,16]{3,1,2,0:T(1,128)S(1)}, s32[1,1,3,16]{3,1,2,0:T(1,128)}, u32[]{:S(2)}) copy-start(s32[1,1,3,16]{3,1,2,0:T(1,128)} %param.11) | copy-start | bytes 580
  12.5 0.7 %copy-start.5 = (f32[1,1,3,16]{3,1,2,0:T(1,128)S(1)}, f32[1,1,3,16]{3,1,2,0:T(1,128)}, u32[]{:S(2)}) copy-start(f32[1,1,3,16]{3,1,2,0:T(1,128)} %param.13) | copy-start | bytes 580
  18.9 1.5 %collective-permute-start.2 = (f32[256,128]{1,0:T(8,128)S(1)}, f32[256,128]{1,0:T(8,128)S(1)}, u32[]{:S(2)}, u32[]{:S(2)}) collective-permute-start(f32[256,128]{1,0:T(8,128)S(1)} %bitcast.8), channel_id=1, source_target_pairs={{0,1},{2,3},{1,0},{3,2},{4,5},{6,7},{5,4},{7,6},{8,9},{10,11},{9,8... | collective-permute-start | bytes 393224 | tf_op jit(solution)/shard_map/ppermute | solution.py:555

commit v4 on v3

v4 whole, which is shorter than its diff:
```python
import functools
import math

import jax
import jax.numpy as jnp
from jax import lax
from jax.experimental import pallas as pl
from jax.experimental.pallas import tpu as pltpu
from jax.sharding import Mesh
from jax.sharding import PartitionSpec as P

CAP = 4
STEP_TIME = 0.2
REST_VOLUME = 1.0 / 6.0
PERMUTATIONS = ((0, 1, 2), (0, 2, 1), (1, 0, 2), (1, 2, 0), (2, 0, 1), (2, 1, 0))
ROWS = 4

VMEM = pl.BlockSpec(memory_space=pltpu.VMEM)
SMEM = pl.BlockSpec(memory_space=pltpu.SMEM)
HBM = pl.BlockSpec(memory_space=pltpu.HBM)
PARAMS = pltpu.CompilerParams(vmem_limit_bytes=16 << 20)
NEAR_TURNS = 4
ROOT = math.sqrt(math.log2(math.e))


def add(total, term):
    return term if total is None else total + term


def unit(axis):
    return tuple(1 if position == 2 - axis else 0 for position in range(3))


def tensions(edges, growth, scale_side, scale_up):
    inverse = 1.0 / growth
    columns = {}
    for (axis, start), rows in edges.items():
        made = []
        for row in range(3):
            value = rows[row] + 1.0 if row == axis else rows[row]
            made.append(value * inverse if axis < 2 else value)
        columns[(axis, start)] = made
    pulls = {}
    for first, second, third in PERMUTATIONS:
        middle = unit(first)
        upper = tuple(a + b for a, b in zip(middle, unit(second)))
        keys = {first: (first, (0, 0, 0)), second: (second, middle), third: (third, upper)}
        fe = [[columns[keys[col]][row] for col in range(3)] for row in range(3)]
        cof = [
            [
                fe[(row + 1) % 3][(col + 1) % 3] * fe[(row + 2) % 3][(col + 2) % 3]
                - fe[(row + 1) % 3][(col + 2) % 3] * fe[(row + 2) % 3][(col + 1) % 3]
                for col in range(3)
            ]
            for row in range(3)
        ]
        jacobian = fe[0][0] * cof[0][0] + fe[0][1] * cof[0][1] + fe[0][2] * cof[0][2]
        pressure = 4.0 * jacobian - 5.0
        for col in range(3):
            key = keys[col]
            for row in range(3):
                pulls.setdefault(key, [None] * 3)
                pulls[key][row] = add(pulls[key][row], fe[row][col] + pressure * cof[row][col])
    return {
        key: [value * (scale_side if key[0] < 2 else scale_up) for value in rows]
        for key, rows in pulls.items()
    }


def roll(value, shift, axis):
    size = value.shape[axis]
    shift = shift % size
    return value if shift == 0 else pltpu.roll(value, shift, axis)


def lane_of(shape):
    return lax.broadcasted_iota(jnp.int32, shape, len(shape) - 1)


def column_pack(fields, lane_from, stride, offset):
    shape = fields[0][0].shape
    lane = lane_of(shape)
    packed = jnp.zeros(shape, jnp.float32)
    for c, layers in enumerate(fields):
        for z, field in enumerate(layers):
            to = c * stride + z + offset
            packed = jnp.where(lane == to, roll(field, to - lane_from, 1), packed)
    return packed


def each(count, body, unrolled):
    if count <= unrolled:
        for index in range(count):
            body(index)
    else:

        def one(index, carry):
            body(index)
            return carry

        lax.fori_loop(0, count, one, 0)


def split(value, size):
    if size & (size - 1):
        return lax.div(value, size), lax.rem(value, size)
    return lax.shift_right_logical(value, size.bit_length() - 1), lax.bitwise_and(value, size - 1)


def slab_index():
    return lax.axis_index("pair") * lax.axis_size("core") + lax.axis_index("core")


def thirds(value):
    high = value.astype(jnp.bfloat16)
    rest = value - high.astype(jnp.float32)
    middle = rest.astype(jnp.bfloat16)
    low = (rest - middle.astype(jnp.float32)).astype(jnp.bfloat16)
    return high, middle, low


def picked(chosen, value, contract):
    chosen = chosen.astype(jnp.bfloat16)
    total = None
    for part in thirds(value):
        term = lax.dot_general(
            chosen,
            part,
            (((contract,), (0,)), ((), ())),
            preferred_element_type=jnp.float32,
        )
        total = add(total, term)
    return total


def shift_y(value, step, half_lanes, first_row, last_row):
    moved = roll(value, step, 0)
    return jnp.where(
        first_row if step > 0 else last_row, roll(moved, step * half_lanes, 1), moved
    )


def pack_kernel(
    dims,
    disp_in,
    growth_in,
    shear_in,
    slots_in,
    packet,
    face_a,
    face_b,
    disp,
    growth,
    shear,
    slots,
    counted,
    face,
    sems,
):
    slab_len, width_y, patch_len, regions, slabs, pairs = dims
    region = lax.axis_index("region")
    depth = slab_index()
    pair = lax.axis_index("pair")
    blocks = slabs // 2
    stride = slab_len + 2
    moves = [
        pltpu.make_async_copy(source, target, sems.at[index])
        for index, (source, target) in enumerate(
            (
                (slots_in, slots),
                (disp_in, disp.at[0 : slab_len * 3 * width_y]),
                (growth_in, growth),
                (shear_in, shear),
            )
        )
    ]
    for move in moves:
        move.start()
    tall = CAP * ROWS
    blank = jnp.zeros((tall, patch_len), jnp.float32)

    def base_of(m, block):
        return pl.multiple_of((m * blocks + block) * tall, tall)

    def clear(m):
        counted[m] = 0
        packet[pl.ds(base_of(m, pair), tall), :] = blank

    disp[slab_len * 3 * width_y :, :] = jnp.zeros((ROWS * width_y, patch_len), jnp.float32)
    each(regions, clear, 16)
    for move in moves:
        move.wait()

    tile_row = lax.broadcasted_iota(jnp.int32, (ROWS, patch_len), 0)

    def place(k):
        own, other = slots[0, 0, 0, k], slots[0, 1, 0, k]
        position = counted[other]
        counted[other] = position + 1
        fits = position < CAP
        base = (jnp.where(fits, other, region) * blocks + pair) * tall
        base = pl.multiple_of(base + jnp.where(fits, position, 0) * ROWS, ROWS)
        z, y = split(own, width_y)
        row = z * (3 * width_y) + y
        tile = disp[pl.ds(row, ROWS, stride=width_y), :]
        label = jnp.full((ROWS, patch_len), own, jnp.int32).astype(jnp.float32)
        packet[pl.ds(base, ROWS), :] = jnp.where(tile_row == 3, label, tile)

    each(pairs, place, 16)

    even = lax.rem(depth, 2) == 0
    last = slab_len - 1
    for out, from_z in ((face_a, jnp.where(even, last, 0)), (face_b, jnp.where(even, 0, last))):
        for c in range(3):
            start = pl.multiple_of((from_z * 3 + c) * width_y, width_y)
            out[c] = disp[pl.ds(start, width_y), :]
        out[3] = growth[last]
        out[4] = shear[last]

    groups = width_y // CAP
    width = patch_len // groups
    def plane(z, c):
        start = (z * 3 + c) * width_y
        return disp[start : start + width_y, :]

    fields = [[plane(z, c) for z in range(slab_len)] for c in range(3)]
    fields = fields + [[growth[z] for z in range(slab_len)], [shear[z] for z in range(slab_len)]]
    sides = ((patch_len - 1, fields, 1), (0, fields[:3], regions - 1))
    lane = lane_of((CAP, patch_len))
    for side, (lane_from, chosen, step) in enumerate(sides):
        ringed = [[layers[-1]] + layers + [layers[0]] for layers in chosen]
        face[side] = column_pack(ringed, lane_from, stride, 0)
        folded = jnp.zeros((CAP, patch_len), jnp.float32)
        for g in range(groups):
            at = (g % 2) * (groups // 2) + g // 2
            part = roll(face[side, at * CAP : (at + 1) * CAP, :], g * width, 1)
            folded = jnp.where((lane >= g * width) & (lane < (g + 1) * width), part, folded)
        other = lax.rem(region + step, regions)
        for block in range(blocks):
            rows = pl.ds(base_of(other, block) + 3, CAP, stride=ROWS)
            packet[rows, :] = jnp.where(lane < patch_len - 1, folded, packet[rows, :])


def layer_edges(layer):
    along_x, along_y, moved = {}, {}, {}
    for c in range(3):
        base = layer[c]
        next_x = roll(base, -1, 1)
        next_y = roll(base, -1, 0)
        next_xy = roll(next_y, -1, 1)
        moved[c] = {(0, 0): base, (0, 1): next_x, (1, 0): next_y, (1, 1): next_xy}
        along_x[c] = {0: next_x - base, 1: next_xy - next_y}
        along_y[c] = {0: next_y - base, 1: next_xy - next_x}
    return along_x, along_y, moved


def cell_layer(low, high, growth, shear, valid):
    edges = {}
    for dz, (along_x, along_y, _) in enumerate((low, high)):
        for other in range(2):
            edges[(0, (dz, other, 0))] = [along_x[c][other] for c in range(3)]
            edges[(1, (dz, 0, other))] = [along_y[c][other] for c in range(3)]
    for dy in range(2):
        for dx in range(2):
            edges[(2, (0, dy, dx))] = [
                high[2][c][(dy, dx)] - low[2][c][(dy, dx)] for c in range(3)
            ]
    scale = jnp.where(valid, shear * REST_VOLUME, 0.0) * growth
    pulls = tensions(edges, growth, scale, scale * growth)
    levels = []
    for dz in range(2):
        level = []
        for c in range(3):
            pull_x = pulls[(0, (dz, 0, 0))][c] + roll(pulls[(0, (dz, 1, 0))][c], 1, 0)
            pull_y = pulls[(1, (dz, 0, 0))][c] + roll(pulls[(1, (dz, 0, 1))][c], 1, 1)
            level.append((pull_x - roll(pull_x, 1, 1)) + (pull_y - roll(pull_y, 1, 0)))
        levels.append(level)
    for c in range(3):
        at_zero = pulls[(2, (0, 0, 0))][c] + roll(pulls[(2, (0, 1, 0))][c], 1, 0)
        at_one = pulls[(2, (0, 0, 1))][c] + roll(pulls[(2, (0, 1, 1))][c], 1, 0)
        pull_z = at_zero + roll(at_one, 1, 1)
        levels[0][c] = levels[0][c] + pull_z
        levels[1][c] = levels[1][c] - pull_z
    return levels


def inner_cells(width_y, patch_len):
    shape = (width_y, patch_len)
    row_y = lax.broadcasted_iota(jnp.int32, shape, 0)
    return (lane_of(shape) < patch_len - 1) & (row_y < width_y - 1)


def inner_kernel(
    dims,
    disp,
    growth,
    shear,
    velocity,
    slots,
    slot_row,
    count,
    separation,
    before,
    near,
    selector,
):
    slab_len, width_y, patch_len, regions, slabs, pairs = dims
    inside = inner_cells(width_y, patch_len)
    forces = [[None] * 3 for _ in range(slab_len)]
    low = layer_edges([disp[0, c] for c in range(3)])
    for z in range(slab_len - 1):
        high = layer_edges([disp[z + 1, c] for c in range(3)])
        levels = cell_layer(low, high, growth[z], shear[z], inside)
        low = high
        for dz in range(2):
            for c in range(3):
                forces[z + dz][c] = add(forces[z + dz][c], levels[dz][c])
        for c in range(3):
            before[z, c] = velocity[z, c] + STEP_TIME * forces[z][c]
    for c in range(3):
        before[slab_len - 1, c] = velocity[slab_len - 1, c] + STEP_TIME * forces[slab_len - 1][c]

    along = lane_of((1, patch_len)).astype(jnp.float32)

    def fetch(k):
        z, y = split(slots[0, 0, 0, k], width_y)
        for c in range(3):
            point = disp[z, c, pl.ds(y, 1), :]
            if c == 0:
                point = point + along
            near[c, pl.ds(k, 1), :] = (point - separation[0, c, 0, k]) * ROOT

    each(pairs, fetch, 16)
    patch_row = lax.broadcasted_iota(jnp.int32, selector.shape, 0)
    live = lax.broadcasted_iota(jnp.int32, selector.shape, 1) < count[0, 0]
    selector[...] = jnp.where((patch_row == slot_row[0, 0]) & live, 1.0, 0.0)


def outer_kernel(dims, disp, growth, shear, face_a, face_b, lowest, highest, own_columns):
    slab_len, width_y, patch_len, regions, slabs, pairs = dims
    depth = slab_index()
    inside = inner_cells(width_y, patch_len)
    even = lax.rem(depth, 2) == 0
    below = [jnp.where(even, face_b[c], face_a[c]) for c in range(5)]
    above = [jnp.where(even, face_a[c], face_b[c]) for c in range(3)]
    has_below = depth > 0
    last = slab_len - 1
    below_growth = jnp.where(has_below, below[3], 1.0)
    first_nodes = [disp[0, c] for c in range(3)]
    last_nodes = [disp[last, c] for c in range(3)]
    low, high = layer_edges(below[0:3]), layer_edges(first_nodes)
    levels = cell_layer(low, high, below_growth, below[4], inside & has_below)
    for c in range(3):
        lowest[c] = levels[1][c]
    low, high = layer_edges(last_nodes), layer_edges(above)
    levels = cell_layer(low, high, growth[last], shear[last], inside & (depth < slabs - 1))
    for c in range(3):
        highest[c] = levels[0][c]

    half_rows = width_y // 2
    stride = slab_len + 2
    lane_half = lane_of((half_rows, patch_len)) < patch_len // 4
    side_fields = [
        [below[c]] + [disp[z, c] for z in range(slab_len)] + [above[c]] for c in range(3)
    ]
    cell_fields = [
        [below_growth] + [growth[z] for z in range(slab_len)],
        [below[4]] + [shear[z] for z in range(slab_len)],
    ]
    for side, (chosen, lane_from) in enumerate(
        ((side_fields + cell_fields, patch_len - 1), (side_fields, 0))
    ):
        column = column_pack(chosen, lane_from, stride, 0)
        upper = roll(column[half_rows:], patch_len // 4, 1)
        own_columns[side] = jnp.where(lane_half, column[:half_rows], upper)


def border_forces(dims, arrived, relayed, own_columns):
    slab_len, width_y, patch_len, regions, slabs, pairs = dims
    region = lax.axis_index("region")
    depth = slab_index()
    pair = lax.axis_index("pair")
    core = lax.axis_index("core")
    blocks = slabs // 2
    stride = slab_len + 2
    groups = width_y // CAP
    width = patch_len // groups
    half = patch_len // 2
    fold_lane = lane_of((CAP, patch_len))
    fold_z = lax.rem(lax.rem(fold_lane, width), stride)
    gathered = []
    for step in (regions - 1, 1):
        other = lax.rem(region + step, regions)

        def columns(block):
            base = (other * blocks + lax.rem(block + blocks, blocks)) * CAP
            return relayed[pl.ds(pl.multiple_of(base, CAP), CAP), :]

        base = (other * blocks + pair) * (CAP * ROWS)
        merged = arrived[pl.ds(base + 3, CAP, stride=ROWS), :]
        merged = jnp.where(fold_z == 0, columns(pair - 1 + core), merged)
        merged = jnp.where(fold_z == slab_len + 1, columns(pair + core), merged)
        gathered.append(jnp.concatenate([merged] * (groups // 2), axis=0))
    from_left, from_right = gathered
    own_last = own_columns[0]
    own_first = own_columns[1]
    half_rows = width_y // 2
    shape = (half_rows, patch_len)
    lane = lane_of(shape)
    row = lax.broadcasted_iota(jnp.int32, shape, 0)
    first_row, last_row = row == 0, row == half_rows - 1
    first_side = lane < half
    quarter = half // 2
    z_cell = lax.rem(lane, quarter)
    row_y = row + jnp.where(lax.rem(lane, half) >= quarter, half_rows, 0)

    def at_y(value, step):
        return shift_y(value, step, quarter, first_row, last_row)

    z_global = depth * slab_len + z_cell - 1
    valid = (z_cell <= slab_len) & (z_global >= 0) & (z_global <= slab_len * slabs - 2)
    valid = valid & (row_y < width_y - 1)

    part = row // CAP

    def unfolded(source, shift):
        value = roll(source, shift, 1)
        for p in range(1, groups // 2):
            value = jnp.where(part == p, roll(source, shift - p * 2 * width, 1), value)
        return value

    low_x = [
        jnp.where(
            first_side, unfolded(from_left, -c * stride), roll(own_last, half - c * stride, 1)
        )
        for c in range(5)
    ]
    high_x = [
        jnp.where(
            first_side, roll(own_first, -c * stride, 1), unfolded(from_right, half - c * stride)
        )
        for c in range(3)
    ]
    growth = jnp.where(valid, low_x[3], 1.0)
    scale = jnp.where(valid, low_x[4] * REST_VOLUME, 0.0) * growth
    corner = {}
    for c in range(3):
        for dx, base in ((0, low_x[c]), (1, high_x[c])):
            up = roll(base, -1, 1)
            corner[(c, 0, 0, dx)] = base
            corner[(c, 0, 1, dx)] = at_y(base, -1)
            corner[(c, 1, 0, dx)] = up
            corner[(c, 1, 1, dx)] = at_y(up, -1)
    edges = {}
    for one in range(2):
        for two in range(2):
            for axis, start in ((0, (one, two, 0)), (1, (one, 0, two)), (2, (0, one, two))):
                end = tuple(a + b for a, b in zip(start, unit(axis)))
                edges[(axis, start)] = [corner[(c, *end)] - corner[(c, *start)] for c in range(3)]
    pulls = tensions(edges, growth, scale, scale * growth)
    forces = []
    for c in range(3):

        def chosen(axis, one):
            at = ((one, 0, 0), (one, 0, 1)) if axis == 1 else ((0, one, 0), (0, one, 1))
            return jnp.where(first_side, pulls[(axis, at[1])][c], pulls[(axis, at[0])][c])

        level = []
        for dz in range(2):
            both = pulls[(0, (dz, 0, 0))][c] + at_y(pulls[(0, (dz, 1, 0))][c], 1)
            both = jnp.where(first_side, -both, both)
            along_y = chosen(1, dz)
            level.append(both + (along_y - at_y(along_y, 1)))
        along_z = chosen(2, 0) + at_y(chosen(2, 1), 1)
        forces.append((level[0] + along_z) + roll(level[1] - along_z, 1, 1))
    return forces


def contact_kernel(
    dims, arrived, near, slots, before, lowest, highest, selector, moved, far, tiles, pushes
):
    slab_len, width_y, patch_len, regions, slabs, pairs = dims
    block = 8
    pair = lax.axis_index("pair")
    blocks = slabs // 2
    tall = CAP * ROWS

    def take(m):
        rows = pl.ds(pl.multiple_of((m * blocks + pair) * tall, tall), tall)
        tiles[pl.ds(pl.multiple_of(m * tall, tall), tall), :] = arrived[rows, :]

    each(regions, take, 16)

    total_tiles = regions * CAP
    wide = (total_tiles, pairs)
    label = tiles[pl.ds(3, total_tiles, stride=ROWS), :][:, patch_len - 1 :]
    label = jnp.broadcast_to(label, (total_tiles, max(pairs, patch_len)))
    tile_row = lax.broadcasted_iota(jnp.int32, label.shape, 0)
    again = tile_row < 0
    for back in range(1, CAP):
        same = (roll(label, back, 0) == label) & (lax.rem(tile_row, CAP) >= back)
        again = again | same
    label = jnp.where(again, -1.0, label)[:, 0:pairs]
    tile_row = lax.broadcasted_iota(jnp.int32, wide, 0) // CAP
    wanted = (tile_row == slots[0, 1]) & (label == slots[0, 2].astype(jnp.float32))
    chosen = jnp.where(wanted, 1.0, 0.0)
    for c in range(3):
        far[c] = picked(chosen, tiles[pl.ds(c, total_tiles, stride=ROWS), :], 0)
    along = lane_of((block, patch_len)).astype(jnp.float32)

    def contact(start):
        rows = pl.ds(start, block)
        mine = [near[c, rows, :] for c in range(3)]
        theirs = [far[c, rows, :] for c in range(3)]
        theirs = [(theirs[0] + along) * ROOT, theirs[1] * ROOT, theirs[2] * ROOT]

        starts = range(0, patch_len, patch_len // NEAR_TURNS)
        turned = [[roll(value, -a, 1) for value in mine] for a in starts]
        sums = [[None] * 3 for _ in starts]
        for b in range(patch_len // NEAR_TURNS):
            other = [roll(value, b, 1) for value in theirs]
            for total, here in zip(sums, turned):
                delta = [here[c] - other[c] for c in range(3)]
                square = delta[0] * delta[0] + delta[1] * delta[1] + delta[2] * delta[2]
                weight = jnp.exp2(-square)
                for c in range(3):
                    total[c] = add(total[c], delta[c] * weight)
        total = [None] * 3
        for a, part in zip(starts, sums):
            for c in range(3):
                total[c] = add(total[c], roll(part[c], a, 1))
        for c in range(3):
            pushes[c, rows, :] = total[c]

    each(pairs // block, lambda step: contact(step * block), 2)

    for c in range(3):
        push = picked(selector[...], pushes[c], 1) * (1.0 / ROOT)
        for z in range(slab_len):
            force = push[z * width_y : (z + 1) * width_y, :]
            if z == 0:
                force = force + lowest[c]
            if z == slab_len - 1:
                force = force + highest[c]
            moved[z, c] = before[z, c] + STEP_TIME * force


def finish_kernel(dims, arrived, relayed, moved, own_columns, disp, new_velocity, new_disp):
    slab_len, width_y, patch_len, regions, slabs, pairs = dims
    half = patch_len // 2
    borders = border_forces(dims, arrived, relayed, own_columns)
    half_rows = width_y // 2
    lane = lane_of((half_rows, patch_len))
    last = patch_len - 1
    for c in range(3):
        edge = borders[c] * STEP_TIME
        for z in range(slab_len):
            for part in range(2):
                at = part * (half // 2) + z + 1
                rows = slice(part * half_rows, (part + 1) * half_rows)
                speed = moved[z, c, rows, :]
                speed = speed + jnp.where(lane == 0, roll(edge, -at, 1), 0.0)
                speed = speed + jnp.where(lane == last, roll(edge, last - half - at, 1), 0.0)
                new_velocity[z, c, rows, :] = speed
                new_disp[z, c, rows, :] = disp[z, c, rows, :] + STEP_TIME * speed


def local(displacement, velocity, growth, shear_modulus, pair_slots, pair_count, separation):
    slab_len, width_y, _, patch_len = displacement.shape
    regions = lax.axis_size("region")
    slabs = lax.axis_size("pair") * lax.axis_size("core")
    pairs = pair_slots.shape[3]
    dims = (slab_len, width_y, patch_len, regions, slabs, pairs)
    f32 = jnp.float32
    i32 = jnp.int32
    disp = jnp.transpose(displacement, (0, 2, 1, 3))
    speed = jnp.transpose(velocity, (0, 2, 1, 3))
    slots = jnp.transpose(pair_slots, (0, 2, 1, 3))
    apart = jnp.transpose(separation, (0, 2, 1, 3))
    plane = (width_y, patch_len)

    packet, face_a, face_b = pl.pallas_call(
        functools.partial(pack_kernel, dims),
        out_shape=(
            jax.ShapeDtypeStruct((regions * (slabs // 2) * CAP * ROWS, patch_len), f32),
            jax.ShapeDtypeStruct((5, *plane), f32),
            jax.ShapeDtypeStruct((5, *plane), f32),
        ),
        in_specs=[HBM] * 4,
        out_specs=(VMEM, VMEM, VMEM),
        scratch_shapes=[
            pltpu.VMEM(((slab_len * 3 + ROWS) * width_y, patch_len), f32),
            pltpu.VMEM((slab_len, *plane), f32),
            pltpu.VMEM((slab_len, *plane), f32),
            pltpu.SMEM(slots.shape, i32),
            pltpu.SMEM((regions,), i32),
            pltpu.VMEM((2, *plane), f32),
            pltpu.SemaphoreType.DMA((4,)),
        ],
        name="pack",
    )(disp.reshape(slab_len * 3 * width_y, patch_len), growth, shear_modulus, slots)

    links = [[(i, i + 1) for i in range(first, slabs - 1, 2)] for first in (0, 1)]
    links = [link + [(b, a) for a, b in link] for link in links]
    face_a = lax.ppermute(face_a, ("pair", "core"), links[0])
    face_b = lax.ppermute(face_b, ("pair", "core"), links[1])

    packet, pair_count = lax.optimization_barrier((packet, pair_count))
    arrived = lax.all_to_all(packet, ("region", "pair"), 0, 0, tiled=True)

    before, near, selector = pl.pallas_call(
        functools.partial(inner_kernel, dims),
        out_shape=(
            jax.ShapeDtypeStruct((slab_len, 3, *plane), f32),
            jax.ShapeDtypeStruct((3, pairs, patch_len), f32),
            jax.ShapeDtypeStruct((slab_len * width_y, pairs), f32),
        ),
        in_specs=[VMEM] * 4 + [SMEM, VMEM, SMEM, SMEM],
        out_specs=(VMEM,) * 3,
        compiler_params=PARAMS,
        name="inner",
        cost_estimate=pl.CostEstimate(flops=4000 * 1024, bytes_accessed=1 << 20, transcendentals=0),
    )(disp, growth, shear_modulus, speed, slots, slots, pair_count, apart)

    lowest, highest, own_columns = pl.pallas_call(
        functools.partial(outer_kernel, dims),
        out_shape=(
            jax.ShapeDtypeStruct((3, *plane), f32),
            jax.ShapeDtypeStruct((3, *plane), f32),
            jax.ShapeDtypeStruct((2, width_y // 2, patch_len), f32),
        ),
        in_specs=[VMEM] * 5,
        out_specs=(VMEM,) * 3,
        compiler_params=PARAMS,
        name="outer",
        cost_estimate=pl.CostEstimate(flops=2000 * 1024, bytes_accessed=1 << 20, transcendentals=0),
    )(disp, growth, shear_modulus, face_a, face_b)

    arrived, before, lowest = lax.optimization_barrier((arrived, before, lowest))
    columns = arrived.reshape(-1, ROWS, patch_len)[:, ROWS - 1, :]
    relayed = lax.ppermute(columns, ("pair", "core"), links[0])

    moved = pl.pallas_call(
        functools.partial(contact_kernel, dims),
        out_shape=jax.ShapeDtypeStruct((slab_len, 3, *plane), f32),
        in_specs=[VMEM] * 7,
        out_specs=VMEM,
        scratch_shapes=[
            pltpu.VMEM((3, pairs, patch_len), f32),
            pltpu.VMEM((regions * CAP * ROWS, patch_len), f32),
            pltpu.VMEM((3, pairs, patch_len), f32),
        ],
        compiler_params=PARAMS,
        name="contact",
        cost_estimate=pl.CostEstimate(flops=6000 * 1024, bytes_accessed=1 << 20, transcendentals=0),
    )(arrived, near, slots, before, lowest, highest, selector)

    new_velocity, new_disp = pl.pallas_call(
        functools.partial(finish_kernel, dims),
        out_shape=(
            jax.ShapeDtypeStruct((slab_len, 3, *plane), f32),
            jax.ShapeDtypeStruct((slab_len, 3, *plane), f32),
        ),
        in_specs=[VMEM] * 5,
        out_specs=(VMEM, VMEM),
        compiler_params=PARAMS,
        name="finish",
    )(arrived, relayed, moved, own_columns, disp)
    order = (0, 2, 1, 3)
    return jnp.transpose(new_velocity, order), jnp.transpose(new_disp, order)


def solution(mesh):
    shape = dict(mesh.shape)
    devices = mesh.devices.reshape(shape["region"], shape["depth"] // 2, 2)
    fine = Mesh(devices, ("region", "pair", "core"))
    depth = ("pair", "core")
    in_specs = (
        P(depth, None, None, "region"),
        P(depth, None, None, "region"),
        P(depth, None, "region"),
        P(depth, None, "region"),
        P(depth, "region", None, None),
        P(depth, "region"),
        P(depth, "region", None, None),
    )
    out_specs = (P(depth, None, None, "region"), P(depth, None, None, "region"))
    return jax.shard_map(local, mesh=fine, in_specs=in_specs, out_specs=out_specs, check_vma=False)
```

time: 21.9 us -> 21.7 us (level)
    pallas_call x1, Pallas kernels: 1.47 us -> 1.09 us  [local(): pl.pallas_call(functools.partial(inner_kernel, dims), out_shape=(jax.Shap...]
    pallas_call x1 -> x2, Pallas kernels: 1.29 us -> 1.62 us  [the longest x1 1.22 us: local(): pl.pallas_call(functools.partial(contact_kernel, dims), out_shape=jax.Sha...]
  transfers between devices with their start and end apart: 4 -> 4, of which waited for: 2 -> 1; matrix products, arithmetic and copies ran while one was open for 0% -> 0% of each run, Pallas kernels for 13% -> 13%
where the time goes in v4:
time: 21.7 us; the launch traced here: 21.4 us
  starting transfers between devices  9.29 us (43%)
  Pallas kernels  5.76 us (27%)
  waiting for transfers between devices  4.19 us (19%)
  between operations  1.44 us (7%)
  local copies, waits for them, and re-layouts  0.7 us (3%)
    all_to_all x1, starting transfers between devices, local(): arrived = lax.all_to_all(packet, ('region', 'pair'), 0, 0, tiled=True)  8.48 us
    all_to_all x1, waiting for transfers between devices, local(): arrived = lax.all_to_all(packet, ('region', 'pair'), 0, 0, tiled=True)  4.18 us
    pallas_call x1, Pallas kernels, local(): pl.pallas_call(functools.partial(pack_kernel, dims), out_shape=(jax.Shape...  1.84 us
    pallas_call x1, Pallas kernels, local(): pl.pallas_call(functools.partial(contact_kernel, dims), out_shape=jax.Sha...  1.22 us
    pallas_call x1, Pallas kernels, local(): pl.pallas_call(functools.partial(finish_kernel, dims), out_shape=(jax.Sha...  1.2 us
    pallas_call x1, Pallas kernels, local(): pl.pallas_call(functools.partial(inner_kernel, dims), out_shape=(jax.Shap...  1.09 us
    unnamed x12, local copies, waits for them, and re-layouts  0.67 us
    ppermute x1, starting transfers between devices, local(): face_b = lax.ppermute(face_b, ('pair', 'core'), links[1])  0.66 us
  transfers between devices with their start and end apart: 4, of which 1 were waited for; matrix products, arithmetic and copies ran while one was open for 0% of the time, Pallas kernels for 13%

profile of v4, /device:TPU:0, one launch (start us, length us, event | category | flops | bytes accessed | tf_op | source)
XLA Modules:
  0.0 21.4 jit_solution(13449828286215789214)
XLA Ops:
  0.6 1.8 %pack.1 = (f32[256,128]{1,0:T(8,128)}, f32[5,16,128]{2,1,0:T(8,128)}, f32[5,16,128]{2,1,0:T(8,128)}) custom-call(f32[192,128]{1,0:T(8,128)} %bitcast.14, f32[4,16,128]{2,1,0:T(8,128)} %growth.3, f32[4,16,128]{2,1,0:T(8,128)} %shear.3, s32[1,3,1,16]{3,2,1,0:T(1,128)} %bitcast.22), custom_call_target="tpu_custom_call" | custom-call | tf_op jit(solution)/shard_map/pack/pallas_call | solution.py:582
  2.5 0.0 copy-start
  2.5 0.0 copy-start.1
  2.5 0.0 copy-start.2
  2.5 0.0 copy-start.3
  2.5 8.5 %all-to-all-start = ((f32[16,16,128]{2,1,0:T(8,128)}), f32[16,16,128]{2,1,0:T(8,128)S(1)}, u32[]{:S(2)}, u32[]{:S(2)}) async-start(f32[16,16,128]{2,1,0:T(8,128)} %bitcast.27), calls=%async_computation | async-start | bytes 262144 | tf_op jit(solution)/shard_map/all_to_all | solution.py:609
  11.0 0.1 collective-permute-start
  11.1 0.7 %collective-permute-start.1 = (f32[5,16,128]{2,1,0:T(8,128)}, f32[5,16,128]{2,1,0:T(8,128)S(1)}, u32[]{:S(2)}, u32[]{:S(2)}) collective-permute-start(f32[5,16,128]{2,1,0:T(8,128)} %get-tuple-element.23), channel_id=1, source_target_pairs={{1,2},{2,1},{5,6},{6,5},{9,10},{10,9},{13,14},{14,13},{17,18},{18,... | collective-permute-start | bytes 122888 | tf_op jit(solution)/shard_map/ppermute | solution.py:606
  12.4 0.0 copy-start.4
  12.4 0.0 copy-start.5
  12.4 0.0 copy-done
  12.4 0.0 copy-done.1
  12.5 0.0 copy-done.2
  12.5 0.0 copy-done.3
  12.5 0.6 %copy-done.4 = s32[1,1,3,16]{3,1,2,0:T(1,128)S(1)} copy-done((s32[1,1,3,16]{3,1,2,0:T(1,128)S(1)}, s32[1,1,3,16]{3,1,2,0:T(1,128)}, u32[]{:S(2)}) %copy-start.4) | copy-done | bytes 216
  13.1 0.0 copy-done.5
  13.1 1.1 %inner.1 = (f32[4,3,16,128]{3,2,1,0:T(8,128)S(1)}, f32[3,16,128]{2,1,0:T(8,128)S(1)}, f32[64,16]{1,0:T(8,128)S(1)}) custom-call(f32[4,3,16,128]{3,2,1,0:T(8,128)S(1)} %bitcast.15, f32[4,16,128]{2,1,0:T(8,128)S(1)} %copy-done.1, f32[4,16,128]{2,1,0:T(8,128)S(1)} %copy-done.2, f32[4,3,16,128]{3,2,1,0:T(8,128)S(1)} %bitcast.21, s32[1,3,1,16]{3,2,1,0:T(1,128)S(1)} %bitcast.23, ...), custom_call_target="tpu_custom_call" | custom-call | flops 4096000 | bytes 1048576 | tf_op jit(solution)/shard_map/inner/pallas_call | solution.py:611
  14.2 0.0 collective-permute-done.face_a
  14.2 0.0 collective-permute-done.1.face_b
  14.2 0.4 %outer.1 = (f32[3,16,128]{2,1,0:T(8,128)S(1)}, f32[3,16,128]{2,1,0:T(8,128)S(1)}, f32[2,8,128]{2,1,0:T(8,128)S(1)}) custom-call(f32[4,3,16,128]{3,2,1,0:T(8,128)S(1)} %bitcast.16, f32[4,16,128]{2,1,0:T(8,128)S(1)} %copy-done.1, f32[4,16,128]{2,1,0:T(8,128)S(1)} %copy-done.2, f32[5,16,128]{2,1,0:T(8,128)S(1)} %collective-permute-done.face_a, ...), custom_call_target="tpu_custom_call" | custom-call | flops 2048000 | bytes 1048576 | tf_op jit(solution)/shard_map/outer/pallas_call | solution.py:625
  14.6 4.2 %all-to-all-done = f32[16,16,128]{2,1,0:T(8,128)S(1)} async-done(((f32[16,16,128]{2,1,0:T(8,128)}), f32[16,16,128]{2,1,0:T(8,128)S(1)}, u32[]{:S(2)}, u32[]{:S(2)}) %all-to-all-start) | async-done | bytes 131104 | tf_op jit(solution)/shard_map/all_to_all | solution.py:609
  18.9 0.1 collective-permute-start.2
  18.9 1.2 %contact.1.moved = f32[4,3,16,128]{3,2,1,0:T(8,128)S(1)} custom-call(f32[256,128]{1,0:T(8,128)S(1)} %bitcast.19, f32[3,16,128]{2,1,0:T(8,128)S(1)} %get-tuple-element.26.near, s32[1,3,1,16]{3,2,1,0:T(1,128)S(1)} %bitcast.25, f32[4,3,16,128]{3,2,1,0:T(8,128)S(1)} %get-tuple-element.27.before, f32[3,16,128]{2,1,0:T(8,128)S(1)} %get-tuple-element.28.lowest, ...), custom_call_target="tpu_custom_call" | custom-call | flops 6144000 | bytes 1048576 | tf_op jit(solution)/shard_map/contact/pallas_call | solution.py:643
  20.2 0.0 collective-permute-done.2.relayed
  20.2 1.2 %finish.1 = (f32[4,3,16,128]{3,2,1,0:T(8,128)}, f32[4,3,16,128]{3,2,1,0:T(8,128)}) custom-call(f32[256,128]{1,0:T(8,128)S(1)} %bitcast.20, f32[64,128]{1,0:T(8,128)S(1)} %collective-permute-done.2.relayed, f32[4,3,16,128]{3,2,1,0:T(8,128)S(1)} %contact.1.moved, f32[2,8,128]{2,1,0:T(8,128)S(1)} %get-tuple-element.31.own_columns, f32[4,3,16,128]{3,2,1,0:T(8,128)S(1)} %bitcast.17), custom_call_target="tpu_custom_call" | custom-call | tf_op jit(solution)/shard_map/finish/pallas_call | solution.py:658
  (1 shorter events, 0.0 us)
Async XLA Ops:
  2.5 10.0 %copy-start = (f32[4,16,3,128]{3,1,2,0:T(8,128)S(1)}, f32[4,16,3,128]{3,1,2,0:T(8,128)}, u32[]{:S(2)}) copy-start(f32[4,16,3,128]{3,1,2,0:T(8,128)} %param.7) | copy-start | bytes 294916
  2.5 10.0 %copy-start.1 = (f32[4,16,128]{2,1,0:T(8,128)S(1)}, f32[4,16,128]{2,1,0:T(8,128)}, u32[]{:S(2)}) copy-start(f32[4,16,128]{2,1,0:T(8,128)} %growth.3) | copy-start | bytes 98308
  2.5 10.0 %copy-start.2 = (f32[4,16,128]{2,1,0:T(8,128)S(1)}, f32[4,16,128]{2,1,0:T(8,128)}, u32[]{:S(2)}) copy-start(f32[4,16,128]{2,1,0:T(8,128)} %shear.3) | copy-start | bytes 98308
  2.5 10.0 %copy-start.3 = (f32[4,16,3,128]{3,1,2,0:T(8,128)S(1)}, f32[4,16,3,128]{3,1,2,0:T(8,128)}, u32[]{:S(2)}) copy-start(f32[4,16,3,128]{3,1,2,0:T(8,128)} %param.8) | copy-start | bytes 294916
  2.5 16.3 %all-to-all-start = ((f32[16,16,128]{2,1,0:T(8,128)}), f32[16,16,128]{2,1,0:T(8,128)S(1)}, u32[]{:S(2)}, u32[]{:S(2)}) async-start(f32[16,16,128]{2,1,0:T(8,128)} %bitcast.27), calls=%async_computation | async-start | bytes 262144 | tf_op jit(solution)/shard_map/all_to_all | solution.py:609
  11.0 3.2 %collective-permute-start = (f32[5,16,128]{2,1,0:T(8,128)}, f32[5,16,128]{2,1,0:T(8,128)S(1)}, u32[]{:S(2)}, u32[]{:S(2)}) collective-permute-start(f32[5,16,128]{2,1,0:T(8,128)} %get-tuple-element.22), channel_id=1, source_target_pairs={{0,1},{2,3},{1,0},{3,2},{4,5},{6,7},{5,4},{7,6},{8,9},{10,11},{9,8... | collective-permute-start | bytes 122888 | tf_op jit(solution)/shard_map/ppermute | solution.py:605
  11.1 3.1 %collective-permute-start.1 = (f32[5,16,128]{2,1,0:T(8,128)}, f32[5,16,128]{2,1,0:T(8,128)S(1)}, u32[]{:S(2)}, u32[]{:S(2)}) collective-permute-start(f32[5,16,128]{2,1,0:T(8,128)} %get-tuple-element.23), channel_id=1, source_target_pairs={{1,2},{2,1},{5,6},{6,5},{9,10},{10,9},{13,14},{14,13},{17,18},{18,... | collective-permute-start | bytes 122888 | tf_op jit(solution)/shard_map/ppermute | solution.py:606
  12.4 0.7 %copy-start.4 = (s32[1,1,3,16]{3,1,2,0:T(1,128)S(1)}, s32[1,1,3,16]{3,1,2,0:T(1,128)}, u32[]{:S(2)}) copy-start(s32[1,1,3,16]{3,1,2,0:T(1,128)} %param.11) | copy-start | bytes 580
  12.4 0.7 %copy-start.5 = (f32[1,1,3,16]{3,1,2,0:T(1,128)S(1)}, f32[1,1,3,16]{3,1,2,0:T(1,128)}, u32[]{:S(2)}) copy-start(f32[1,1,3,16]{3,1,2,0:T(1,128)} %param.13) | copy-start | bytes 580
  18.9 1.3 %collective-permute-start.2 = (f32[64,128]{1,0:T(8,128)S(1)}, f32[64,128]{1,0:T(8,128)S(1)}, u32[]{:S(2)}, u32[]{:S(2)}) collective-permute-start(f32[64,128]{1,0:T(8,128)S(1)} %bitcast.28), channel_id=1, source_target_pairs={{0,1},{2,3},{1,0},{3,2},{4,5},{6,7},{5,4},{7,6},{8,9},{10,11},{9,8... | collective-permute-start | bytes 98312 | tf_op jit(solution)/shard_map/ppermute | solution.py:641

commit v5 on v4

--- a/solution.py
+++ b/solution.py
@@ -14,6 +14,7 @@
 REST_VOLUME = 1.0 / 6.0
 PERMUTATIONS = ((0, 1, 2), (0, 2, 1), (1, 0, 2), (1, 2, 0), (2, 0, 1), (2, 1, 0))
 ROWS = 4
+TILES = CAP // 2
 
 VMEM = pl.BlockSpec(memory_space=pltpu.VMEM)
 SMEM = pl.BlockSpec(memory_space=pltpu.SMEM)
@@ -160,9 +161,10 @@
     slab_len, width_y, patch_len, regions, slabs, pairs = dims
     region = lax.axis_index("region")
     depth = slab_index()
-    pair = lax.axis_index("pair")
-    blocks = slabs // 2
+    core = lax.axis_index("core")
+    partner = depth + 1 - 2 * core
     stride = slab_len + 2
+    half = patch_len // 2
     moves = [
         pltpu.make_async_copy(source, target, sems.at[index])
         for index, (source, target) in enumerate(
@@ -176,15 +178,16 @@
     ]
     for move in moves:
         move.start()
-    tall = CAP * ROWS
+    tall = TILES * ROWS
     blank = jnp.zeros((tall, patch_len), jnp.float32)
 
-    def base_of(m, block):
-        return pl.multiple_of((m * blocks + block) * tall, tall)
+    def base_of(m, slab):
+        return pl.multiple_of((m * slabs + slab) * tall, tall)
 
     def clear(m):
         counted[m] = 0
-        packet[pl.ds(base_of(m, pair), tall), :] = blank
+        packet[pl.ds(base_of(m, depth), tall), :] = blank
+        packet[pl.ds(base_of(m, partner), tall), :] = blank
 
     disp[slab_len * 3 * width_y :, :] = jnp.zeros((ROWS * width_y, patch_len), jnp.float32)
     each(regions, clear, 16)
@@ -192,19 +195,29 @@
         move.wait()
 
     tile_row = lax.broadcasted_iota(jnp.int32, (ROWS, patch_len), 0)
+
+    lane = lane_of((ROWS, patch_len))
 
     def place(k):
         own, other = slots[0, 0, 0, k], slots[0, 1, 0, k]
         position = counted[other]
         counted[other] = position + 1
         fits = position < CAP
-        base = (jnp.where(fits, other, region) * blocks + pair) * tall
-        base = pl.multiple_of(base + jnp.where(fits, position, 0) * ROWS, ROWS)
+        place_in = jnp.where(fits, position, 0)
+        side, offset = split(place_in, TILES)
+        m = jnp.where(fits, other, region)
         z, y = split(own, width_y)
-        row = z * (3 * width_y) + y
-        tile = disp[pl.ds(row, ROWS, stride=width_y), :]
+        tile = disp[pl.ds(z * (3 * width_y) + y, ROWS, stride=width_y), :]
         label = jnp.full((ROWS, patch_len), own, jnp.int32).astype(jnp.float32)
-        packet[pl.ds(base, ROWS), :] = jnp.where(tile_row == 3, label, tile)
+        tile = jnp.where(tile_row == 3, label, tile)
+        turned = roll(tile, half, 1)
+        mask = (lane >= half) == (side > 0)
+        for slab, value in (
+            (depth, jnp.where(lane < half, tile, turned)),
+            (partner, jnp.where(lane < half, turned, tile)),
+        ):
+            base = pl.multiple_of((m * slabs + slab) * tall + offset * ROWS, ROWS)
+            pltpu.store(packet.at[pl.ds(base, ROWS), :], value, mask=mask)
 
     each(pairs, place, 16)
 
@@ -217,8 +230,10 @@
         out[3] = growth[last]
         out[4] = shear[last]
 
-    groups = width_y // CAP
+    half_rows = width_y // 2
+    groups = half_rows // TILES
     width = patch_len // groups
+
     def plane(z, c):
         start = (z * 3 + c) * width_y
         return disp[start : start + width_y, :]
@@ -226,19 +241,23 @@
     fields = [[plane(z, c) for z in range(slab_len)] for c in range(3)]
     fields = fields + [[growth[z] for z in range(slab_len)], [shear[z] for z in range(slab_len)]]
     sides = ((patch_len - 1, fields, 1), (0, fields[:3], regions - 1))
-    lane = lane_of((CAP, patch_len))
+    lane = lane_of((TILES, patch_len))
     for side, (lane_from, chosen, step) in enumerate(sides):
         ringed = [[layers[-1]] + layers + [layers[0]] for layers in chosen]
         face[side] = column_pack(ringed, lane_from, stride, 0)
-        folded = jnp.zeros((CAP, patch_len), jnp.float32)
-        for g in range(groups):
-            at = (g % 2) * (groups // 2) + g // 2
-            part = roll(face[side, at * CAP : (at + 1) * CAP, :], g * width, 1)
-            folded = jnp.where((lane >= g * width) & (lane < (g + 1) * width), part, folded)
+        folded = []
+        for part in range(2):
+            value = jnp.zeros((TILES, patch_len), jnp.float32)
+            for g in range(groups):
+                start = part * half_rows + g * TILES
+                rows = roll(face[side, start : start + TILES, :], g * width, 1)
+                value = jnp.where((lane >= g * width) & (lane < (g + 1) * width), rows, value)
+            folded.append(value)
         other = lax.rem(region + step, regions)
-        for block in range(blocks):
-            rows = pl.ds(base_of(other, block) + 3, CAP, stride=ROWS)
-            packet[rows, :] = jnp.where(lane < patch_len - 1, folded, packet[rows, :])
+        for slab in range(slabs):
+            value = jnp.where(core == slab % 2, folded[0], folded[1])
+            rows = pl.ds(base_of(other, slab) + 3, TILES, stride=ROWS)
+            packet[rows, :] = jnp.where(lax.rem(lane, half) == half - 1, packet[rows, :], value)
 
 
 def layer_edges(layer):
@@ -379,32 +398,36 @@
     slab_len, width_y, patch_len, regions, slabs, pairs = dims
     region = lax.axis_index("region")
     depth = slab_index()
-    pair = lax.axis_index("pair")
-    core = lax.axis_index("core")
-    blocks = slabs // 2
     stride = slab_len + 2
-    groups = width_y // CAP
+    half_rows = width_y // 2
+    groups = half_rows // TILES
     width = patch_len // groups
     half = patch_len // 2
-    fold_lane = lane_of((CAP, patch_len))
-    fold_z = lax.rem(lax.rem(fold_lane, width), stride)
+    fold_z = lax.rem(lax.rem(lane_of((TILES, patch_len)), width), stride)
+    row_group = lax.broadcasted_iota(jnp.int32, (half_rows, patch_len), 0) // TILES
+    lower_y = lane_of((half_rows, patch_len)) < half // 2
     gathered = []
     for step in (regions - 1, 1):
         other = lax.rem(region + step, regions)
 
-        def columns(block):
-            base = (other * blocks + lax.rem(block + blocks, blocks)) * CAP
-            return relayed[pl.ds(pl.multiple_of(base, CAP), CAP), :]
-
-        base = (other * blocks + pair) * (CAP * ROWS)
-        merged = arrived[pl.ds(base + 3, CAP, stride=ROWS), :]
-        merged = jnp.where(fold_z == 0, columns(pair - 1 + core), merged)
-        merged = jnp.where(fold_z == slab_len + 1, columns(pair + core), merged)
-        gathered.append(jnp.concatenate([merged] * (groups // 2), axis=0))
+        def columns(source, slab):
+            base = (other * slabs + lax.rem(slab + slabs, slabs)) * (TILES * ROWS)
+            return source[pl.ds(base + 3, TILES, stride=ROWS), :]
+
+        total = jnp.zeros((half_rows, patch_len), jnp.float32)
+        for part, (direct, across) in enumerate(((arrived, relayed), (relayed, arrived))):
+            merged = columns(direct, depth)
+            merged = jnp.where(fold_z == 0, columns(across, depth - 1), merged)
+            merged = jnp.where(fold_z == slab_len + 1, columns(across, depth + 1), merged)
+            merged = jnp.concatenate([merged] * groups, axis=0)
+            for g in range(groups):
+                here = (row_group == g) & (lower_y if part == 0 else ~lower_y)
+                shift = part * (half // 2) - g * width
+                total = jnp.where(here, roll(merged, shift, 1), total)
+        gathered.append(total)
     from_left, from_right = gathered
     own_last = own_columns[0]
     own_first = own_columns[1]
-    half_rows = width_y // 2
     shape = (half_rows, patch_len)
     lane = lane_of(shape)
     row = lax.broadcasted_iota(jnp.int32, shape, 0)
@@ -421,23 +444,15 @@
     valid = (z_cell <= slab_len) & (z_global >= 0) & (z_global <= slab_len * slabs - 2)
     valid = valid & (row_y < width_y - 1)
 
-    part = row // CAP
-
-    def unfolded(source, shift):
-        value = roll(source, shift, 1)
-        for p in range(1, groups // 2):
-            value = jnp.where(part == p, roll(source, shift - p * 2 * width, 1), value)
-        return value
-
     low_x = [
         jnp.where(
-            first_side, unfolded(from_left, -c * stride), roll(own_last, half - c * stride, 1)
+            first_side, roll(from_left, -c * stride, 1), roll(own_last, half - c * stride, 1)
         )
         for c in range(5)
     ]
     high_x = [
         jnp.where(
-            first_side, roll(own_first, -c * stride, 1), unfolded(from_right, half - c * stride)
+            first_side, roll(own_first, -c * stride, 1), roll(from_right, half - c * stride, 1)
         )
         for c in range(3)
     ]
@@ -476,48 +491,70 @@
     return forces
 
 
-def contact_kernel(
-    dims, arrived, near, slots, before, lowest, highest, selector, moved, far, tiles, pushes
-):
+def far_points(dims, source, chosen, tiles):
     slab_len, width_y, patch_len, regions, slabs, pairs = dims
+    depth = slab_index()
+    half = patch_len // 2
+    tall = TILES * ROWS
+
+    def take(m):
+        rows = pl.ds(pl.multiple_of((m * slabs + depth) * tall, tall), tall)
+        tiles[pl.ds(pl.multiple_of(m * tall, tall), tall), :] = source[rows, :]
+
+    each(regions, take, 16)
+    if chosen is None:
+        chosen = yield
+    lane = lane_of((pairs, patch_len))
+    for c in range(3):
+        value = picked(chosen, tiles[pl.ds(c, regions * TILES, stride=ROWS), :], 0)
+        value = jnp.where(lane < half, value[:pairs], value[pairs:])
+        yield value + roll(value, half, 1)
+
+
+def tile_choice(dims, slots, tiles):
+    slab_len, width_y, patch_len, regions, slabs, pairs = dims
+    half = patch_len // 2
+    rows = regions * TILES
+    found = tiles[pl.ds(3, rows, stride=ROWS), :]
+    wide = max(pairs, patch_len)
+    labels = [
+        jnp.broadcast_to(found[:, side * half + half - 1 : side * half + half], (rows, wide))
+        for side in range(2)
+    ]
+    row = lax.broadcasted_iota(jnp.int32, (rows, wide), 0)
+    upper = lax.rem(row, TILES) > 0
+    others = [jnp.where(upper, roll(label, 1, 0), roll(label, -1, 0)) for label in labels]
+    again = [
+        upper & (others[0] == labels[0]),
+        (labels[1] == labels[0])
+        | (labels[1] == others[0])
+        | (upper & (others[1] == labels[1])),
+    ]
+    region_row = lax.broadcasted_iota(jnp.int32, (rows, pairs), 0) // TILES
+    named = slots[0, 2].astype(jnp.float32)
+    chosen = []
+    for label, repeated in zip(labels, again):
+        label = jnp.where(repeated, -1.0, label)[:, 0:pairs]
+        chosen.append(jnp.where((region_row == slots[0, 1]) & (label == named), 1.0, 0.0))
+    return jnp.concatenate(chosen, axis=1)
+
+
+def contact_half(dims, near, far, part, write):
+    slab_len, width_y, patch_len, regions, slabs, pairs = dims
+    half = patch_len // 2
     block = 8
-    pair = lax.axis_index("pair")
-    blocks = slabs // 2
-    tall = CAP * ROWS
-
-    def take(m):
-        rows = pl.ds(pl.multiple_of((m * blocks + pair) * tall, tall), tall)
-        tiles[pl.ds(pl.multiple_of(m * tall, tall), tall), :] = arrived[rows, :]
-
-    each(regions, take, 16)
-
-    total_tiles = regions * CAP
-    wide = (total_tiles, pairs)
-    label = tiles[pl.ds(3, total_tiles, stride=ROWS), :][:, patch_len - 1 :]
-    label = jnp.broadcast_to(label, (total_tiles, max(pairs, patch_len)))
-    tile_row = lax.broadcasted_iota(jnp.int32, label.shape, 0)
-    again = tile_row < 0
-    for back in range(1, CAP):
-        same = (roll(label, back, 0) == label) & (lax.rem(tile_row, CAP) >= back)
-        again = again | same
-    label = jnp.where(again, -1.0, label)[:, 0:pairs]
-    tile_row = lax.broadcasted_iota(jnp.int32, wide, 0) // CAP
-    wanted = (tile_row == slots[0, 1]) & (label == slots[0, 2].astype(jnp.float32))
-    chosen = jnp.where(wanted, 1.0, 0.0)
-    for c in range(3):
-        far[c] = picked(chosen, tiles[pl.ds(c, total_tiles, stride=ROWS), :], 0)
-    along = lane_of((block, patch_len)).astype(jnp.float32)
-
-    def contact(start):
+    along = lax.rem(lane_of((block, patch_len)), half) + part * half
+    along = along.astype(jnp.float32)
+
+    def some(start):
         rows = pl.ds(start, block)
         mine = [near[c, rows, :] for c in range(3)]
         theirs = [far[c, rows, :] for c in range(3)]
         theirs = [(theirs[0] + along) * ROOT, theirs[1] * ROOT, theirs[2] * ROOT]
-
-        starts = range(0, patch_len, patch_len // NEAR_TURNS)
+        starts = range(0, half, half // NEAR_TURNS)
         turned = [[roll(value, -a, 1) for value in mine] for a in starts]
         sums = [[None] * 3 for _ in starts]
-        for b in range(patch_len // NEAR_TURNS):
+        for b in range(half // NEAR_TURNS):
             other = [roll(value, b, 1) for value in theirs]
             for total, here in zip(sums, turned):
                 delta = [here[c] - other[c] for c in range(3)]
@@ -525,42 +562,77 @@
                 weight = jnp.exp2(-square)
                 for c in range(3):
                     total[c] = add(total[c], delta[c] * weight)
-        total = [None] * 3
-        for a, part in zip(starts, sums):
-            for c in range(3):
-                total[c] = add(total[c], roll(part[c], a, 1))
         for c in range(3):
-            pushes[c, rows, :] = total[c]
-
-    each(pairs // block, lambda step: contact(step * block), 2)
-
-    for c in range(3):
-        push = picked(selector[...], pushes[c], 1) * (1.0 / ROOT)
-        for z in range(slab_len):
-            force = push[z * width_y : (z + 1) * width_y, :]
-            if z == 0:
-                force = force + lowest[c]
-            if z == slab_len - 1:
-                force = force + highest[c]
-            moved[z, c] = before[z, c] + STEP_TIME * force
-
-
-def finish_kernel(dims, arrived, relayed, moved, own_columns, disp, new_velocity, new_disp):
+            total = None
+            for a, sum_a in zip(starts, sums):
+                total = add(total, roll(sum_a[c], a, 1))
+            write(c, rows, total)
+
+    each(pairs // block, lambda step: some(step * block), 2)
+
+
+def contact_kernel(dims, arrived, near, slots, chosen, pushes, far, tiles):
+    points = far_points(dims, arrived, None, tiles)
+    next(points)
+    chosen[...] = tile_choice(dims, slots, tiles)
+    far[0] = points.send(chosen[...])
+    far[1] = next(points)
+    far[2] = next(points)
+
+    def write(c, rows, total):
+        pushes[c, rows, :] = total
+
+    contact_half(dims, near, far, 0, write)
+
+
+def finish_kernel(
+    dims,
+    arrived,
+    relayed,
+    before,
+    lowest,
+    highest,
+    near,
+    chosen,
+    pushes,
+    own_columns,
+    disp,
+    selector,
+    new_velocity,
+    new_disp,
+    far,
+    tiles,
+    total_push,
+):
     slab_len, width_y, patch_len, regions, slabs, pairs = dims
     half = patch_len // 2
+    for c, value in enumerate(far_points(dims, relayed, chosen[...], tiles)):
+        far[c] = value
+
+    def write(c, rows, total):
+        total_push[c, rows, :] = pushes[c, rows, :] + total
+
+    contact_half(dims, near, far, 1, write)
     borders = border_forces(dims, arrived, relayed, own_columns)
     half_rows = width_y // 2
     lane = lane_of((half_rows, patch_len))
     last = patch_len - 1
     for c in range(3):
-        edge = borders[c] * STEP_TIME
+        push = picked(selector[...], total_push[c], 1) * (1.0 / ROOT)
+        edge = borders[c]
         for z in range(slab_len):
             for part in range(2):
                 at = part * (half // 2) + z + 1
                 rows = slice(part * half_rows, (part + 1) * half_rows)
-                speed = moved[z, c, rows, :]
-                speed = speed + jnp.where(lane == 0, roll(edge, -at, 1), 0.0)
-                speed = speed + jnp.where(lane == last, roll(edge, last - half - at, 1), 0.0)
+                start = z * width_y + part * half_rows
+                force = push[start : start + half_rows, :]
+                if z == 0:
+                    force = force + lowest[c, rows, :]
+                if z == slab_len - 1:
+                    force = force + highest[c, rows, :]
+                force = force + jnp.where(lane == 0, roll(edge, -at, 1), 0.0)
+                force = force + jnp.where(lane == last, roll(edge, last - half - at, 1), 0.0)
+                speed = before[z, c, rows, :] + STEP_TIME * force
                 new_velocity[z, c, rows, :] = speed
                 new_disp[z, c, rows, :] = disp[z, c, rows, :] + STEP_TIME * speed
 
@@ -582,7 +654,7 @@
     packet, face_a, face_b = pl.pallas_call(
         functools.partial(pack_kernel, dims),
         out_shape=(
-            jax.ShapeDtypeStruct((regions * (slabs // 2) * CAP * ROWS, patch_len), f32),
+            jax.ShapeDtypeStruct((regions * slabs * TILES * ROWS, patch_len), f32),
             jax.ShapeDtypeStruct((5, *plane), f32),
             jax.ShapeDtypeStruct((5, *plane), f32),
         ),
@@ -606,7 +678,7 @@
     face_b = lax.ppermute(face_b, ("pair", "core"), links[1])
 
     packet, pair_count = lax.optimization_barrier((packet, pair_count))
-    arrived = lax.all_to_all(packet, ("region", "pair"), 0, 0, tiled=True)
+    arrived = lax.all_to_all(packet, ("region", "pair", "core"), 0, 0, tiled=True)
 
     before, near, selector = pl.pallas_call(
         functools.partial(inner_kernel, dims),
@@ -637,23 +709,25 @@
     )(disp, growth, shear_modulus, face_a, face_b)
 
     arrived, before, lowest = lax.optimization_barrier((arrived, before, lowest))
-    columns = arrived.reshape(-1, ROWS, patch_len)[:, ROWS - 1, :]
-    relayed = lax.ppermute(columns, ("pair", "core"), links[0])
-
-    moved = pl.pallas_call(
+    relayed = lax.ppermute(arrived, ("pair", "core"), links[0])
+
+    tile_rows = regions * TILES
+    chosen, pushes = pl.pallas_call(
         functools.partial(contact_kernel, dims),
-        out_shape=jax.ShapeDtypeStruct((slab_len, 3, *plane), f32),
-        in_specs=[VMEM] * 7,
-        out_specs=VMEM,
+        out_shape=(
+            jax.ShapeDtypeStruct((tile_rows, 2 * pairs), f32),
+            jax.ShapeDtypeStruct((3, pairs, patch_len), f32),
+        ),
+        in_specs=[VMEM] * 3,
+        out_specs=(VMEM,) * 2,
         scratch_shapes=[
             pltpu.VMEM((3, pairs, patch_len), f32),
-            pltpu.VMEM((regions * CAP * ROWS, patch_len), f32),
-            pltpu.VMEM((3, pairs, patch_len), f32),
+            pltpu.VMEM((tile_rows * ROWS, patch_len), f32),
         ],
         compiler_params=PARAMS,
         name="contact",
         cost_estimate=pl.CostEstimate(flops=6000 * 1024, bytes_accessed=1 << 20, transcendentals=0),
-    )(arrived, near, slots, before, lowest, highest, selector)
+    )(arrived, near, slots)
 
     new_velocity, new_disp = pl.pallas_call(
         functools.partial(finish_kernel, dims),
@@ -661,11 +735,28 @@
             jax.ShapeDtypeStruct((slab_len, 3, *plane), f32),
             jax.ShapeDtypeStruct((slab_len, 3, *plane), f32),
         ),
-        in_specs=[VMEM] * 5,
+        in_specs=[VMEM] * 11,
         out_specs=(VMEM, VMEM),
+        scratch_shapes=[
+            pltpu.VMEM((3, pairs, patch_len), f32),
+            pltpu.VMEM((tile_rows * ROWS, patch_len), f32),
+            pltpu.VMEM((3, pairs, patch_len), f32),
+        ],
         compiler_params=PARAMS,
         name="finish",
-    )(arrived, relayed, moved, own_columns, disp)
+    )(
+        arrived,
+        relayed,
+        before,
+        lowest,
+        highest,
+        near,
+        chosen,
+        pushes,
+        own_columns,
+        disp,
+        selector,
+    )
     order = (0, 2, 1, 3)
     return jnp.transpose(new_velocity, order), jnp.transpose(new_disp, order)
 

time: 21.7 us -> 21.4 us (0.986)
  starting transfers between devices: 9.29 us -> 8.51 us
  waiting for transfers between devices: 4.19 us -> 4.66 us
    all_to_all x1, starting transfers between devices: 8.48 us -> 7.33 us  [local(): lax.all_to_all(packet, ('region', 'pair', 'core'), 0, 0, tiled=True)]
    pallas_call x1, Pallas kernels: 1.2 us -> 1.7 us  [local(): pl.pallas_call(functools.partial(finish_kernel, dims), out_shape=(jax.Sha...]
    pallas_call x1, Pallas kernels: 1.22 us -> 0.84 us  [local(): pl.pallas_call(functools.partial(contact_kernel, dims), out_shape=(jax.Sh...]
    ppermute x1, waiting for transfers between devices: 0.01 us -> 0.3 us  [local(): relayed = lax.ppermute(arrived, ('pair', 'core'), links[0])]
    ppermute x1, starting transfers between devices: 0.07 us -> 0.32 us  [local(): face_a = lax.ppermute(face_a, ('pair', 'core'), links[0])]
  transfers between devices with their start and end apart: 4 -> 4, of which waited for: 1 -> 2; matrix products, arithmetic and copies ran while one was open for 0% -> 0% of each run, Pallas kernels for 13% -> 11%
where the time goes in v5:
time: 21.4 us; the launch traced here: 21.2 us
  starting transfers between devices  8.51 us (40%)
  Pallas kernels  5.92 us (28%)
  waiting for transfers between devices  4.66 us (22%)
  between operations  1.4 us (7%)
  local copies, waits for them, and re-layouts  0.67 us (3%)
    all_to_all x1, starting transfers between devices, local(): lax.all_to_all(packet, ('region', 'pair', 'core'), 0, 0, tiled=True)  7.33 us
    all_to_all x1, waiting for transfers between devices, local(): lax.all_to_all(packet, ('region', 'pair', 'core'), 0, 0, tiled=True)  4.36 us
    pallas_call x1, Pallas kernels, local(): pl.pallas_call(functools.partial(pack_kernel, dims), out_shape=(jax.Shape...  1.89 us
    pallas_call x1, Pallas kernels, local(): pl.pallas_call(functools.partial(finish_kernel, dims), out_shape=(jax.Sha...  1.7 us
    pallas_call x1, Pallas kernels, local(): pl.pallas_call(functools.partial(inner_kernel, dims), out_shape=(jax.Shap...  1.09 us
    pallas_call x1, Pallas kernels, local(): pl.pallas_call(functools.partial(contact_kernel, dims), out_shape=(jax.Sh...  0.84 us
    unnamed x12, local copies, waits for them, and re-layouts  0.67 us
    ppermute x1, starting transfers between devices, local(): face_b = lax.ppermute(face_b, ('pair', 'core'), links[1])  0.65 us
  transfers between devices with their start and end apart: 4, of which 2 were waited for; matrix products, arithmetic and copies ran while one was open for 0% of the time, Pallas kernels for 11%

profile of v5, /device:TPU:0, one launch (start us, length us, event | category | flops | bytes accessed | tf_op | source)
XLA Modules:
  0.0 21.2 jit_solution(510461916324826360)
XLA Ops:
  0.6 1.9 %pack.1 = (f32[256,128]{1,0:T(8,128)}, f32[5,16,128]{2,1,0:T(8,128)}, f32[5,16,128]{2,1,0:T(8,128)}) custom-call(f32[192,128]{1,0:T(8,128)} %bitcast.10, f32[4,16,128]{2,1,0:T(8,128)} %growth.3, f32[4,16,128]{2,1,0:T(8,128)} %shear.3, s32[1,3,1,16]{3,2,1,0:T(1,128)} %bitcast.18), custom_call_target="tpu_custom_call" | custom-call | tf_op jit(solution)/shard_map/pack/pallas_call | solution.py:654
  2.5 0.0 copy-start
  2.5 0.0 copy-start.1
  2.5 0.0 copy-start.2
  2.6 0.0 copy-start.3
  2.6 7.3 %all-to-all-start = ((f32[32,8,128]{2,1,0:T(8,128)}), f32[32,8,128]{2,1,0:T(8,128)S(1)}, u32[]{:S(2)}, u32[]{:S(2)}) async-start(f32[32,8,128]{2,1,0:T(8,128)} %bitcast.23), calls=%async_computation | async-start | bytes 262144 | tf_op jit(solution)/shard_map/all_to_all | solution.py:681
  9.9 0.3 %collective-permute-start = (f32[5,16,128]{2,1,0:T(8,128)}, f32[5,16,128]{2,1,0:T(8,128)S(1)}, u32[]{:S(2)}, u32[]{:S(2)}) collective-permute-start(f32[5,16,128]{2,1,0:T(8,128)} %get-tuple-element.24), channel_id=1, source_target_pairs={{0,1},{2,3},{1,0},{3,2},{4,5},{6,7},{5,4},{7,6},{8,9},{10,11},{9,8... | collective-permute-start | bytes 122888 | tf_op jit(solution)/shard_map/ppermute | solution.py:677
  10.2 0.7 %collective-permute-start.1 = (f32[5,16,128]{2,1,0:T(8,128)}, f32[5,16,128]{2,1,0:T(8,128)S(1)}, u32[]{:S(2)}, u32[]{:S(2)}) collective-permute-start(f32[5,16,128]{2,1,0:T(8,128)} %get-tuple-element.25), channel_id=1, source_target_pairs={{1,2},{2,1},{5,6},{6,5},{9,10},{10,9},{13,14},{14,13},{17,18},{18,... | collective-permute-start | bytes 122888 | tf_op jit(solution)/shard_map/ppermute | solution.py:678
  11.5 0.0 copy-start.4
  11.5 0.0 copy-start.5
  11.6 0.0 copy-done
  11.6 0.0 copy-done.1
  11.6 0.0 copy-done.2
  11.6 0.0 copy-done.3
  11.6 0.6 %copy-done.4 = s32[1,1,3,16]{3,1,2,0:T(1,128)S(1)} copy-done((s32[1,1,3,16]{3,1,2,0:T(1,128)S(1)}, s32[1,1,3,16]{3,1,2,0:T(1,128)}, u32[]{:S(2)}) %copy-start.4) | copy-done | bytes 216
  12.2 0.0 copy-done.5
  12.2 1.1 %inner.1 = (f32[4,3,16,128]{3,2,1,0:T(8,128)S(1)}, f32[3,16,128]{2,1,0:T(8,128)S(1)}, f32[64,16]{1,0:T(8,128)S(1)}) custom-call(f32[4,3,16,128]{3,2,1,0:T(8,128)S(1)} %bitcast.11, f32[4,16,128]{2,1,0:T(8,128)S(1)} %copy-done.1, f32[4,16,128]{2,1,0:T(8,128)S(1)} %copy-done.2, f32[4,3,16,128]{3,2,1,0:T(8,128)S(1)} %bitcast.17, s32[1,3,1,16]{3,2,1,0:T(1,128)S(1)} %bitcast.19, ...), custom_call_target="tpu_custom_call" | custom-call | flops 4096000 | bytes 1048576 | tf_op jit(solution)/shard_map/inner/pallas_call | solution.py:683
  13.3 0.0 collective-permute-done.face_a
  13.3 0.0 collective-permute-done.1.face_b
  13.4 0.4 %outer.1 = (f32[3,16,128]{2,1,0:T(8,128)S(1)}, f32[3,16,128]{2,1,0:T(8,128)S(1)}, f32[2,8,128]{2,1,0:T(8,128)S(1)}) custom-call(f32[4,3,16,128]{3,2,1,0:T(8,128)S(1)} %bitcast.12, f32[4,16,128]{2,1,0:T(8,128)S(1)} %copy-done.1, f32[4,16,128]{2,1,0:T(8,128)S(1)} %copy-done.2, f32[5,16,128]{2,1,0:T(8,128)S(1)} %collective-permute-done.face_a, ...), custom_call_target="tpu_custom_call" | custom-call | flops 2048000 | bytes 1048576 | tf_op jit(solution)/shard_map/outer/pallas_call | solution.py:697
  13.8 4.4 %all-to-all-done = f32[32,8,128]{2,1,0:T(8,128)S(1)} async-done(((f32[32,8,128]{2,1,0:T(8,128)}), f32[32,8,128]{2,1,0:T(8,128)S(1)}, u32[]{:S(2)}, u32[]{:S(2)}) %all-to-all-start) | async-done | bytes 131104 | tf_op jit(solution)/shard_map/all_to_all | solution.py:681
  18.1 0.2 %collective-permute-start.2 = (f32[256,128]{1,0:T(8,128)S(1)}, f32[256,128]{1,0:T(8,128)S(1)}, u32[]{:S(2)}, u32[]{:S(2)}) collective-permute-start(f32[256,128]{1,0:T(8,128)S(1)} %bitcast.14), channel_id=1, source_target_pairs={{0,1},{2,3},{1,0},{3,2},{4,5},{6,7},{5,4},{7,6},{8,9},{10,11},{9,8... | collective-permute-start | bytes 393224 | tf_op jit(solution)/shard_map/ppermute | solution.py:712
  18.3 0.8 %contact.1 = (f32[16,32]{1,0:T(8,128)S(1)}, f32[3,16,128]{2,1,0:T(8,128)S(1)}) custom-call(f32[256,128]{1,0:T(8,128)S(1)} %bitcast.15, f32[3,16,128]{2,1,0:T(8,128)S(1)} %get-tuple-element.31.near, s32[1,3,1,16]{3,2,1,0:T(1,128)S(1)} %bitcast.21), custom_call_target="tpu_custom_call" | custom-call | flops 6144000 | bytes 1048576 | tf_op jit(solution)/shard_map/contact/pallas_call | solution.py:715
  19.2 0.3 %collective-permute-done.2.relayed = f32[256,128]{1,0:T(8,128)S(1)} collective-permute-done((f32[256,128]{1,0:T(8,128)S(1)}, f32[256,128]{1,0:T(8,128)S(1)}, u32[]{:S(2)}, u32[]{:S(2)}) %collective-permute-start.2) | collective-permute-done | bytes 131104 | tf_op jit(solution)/shard_map/ppermute | solution.py:712
  19.5 1.7 %finish.1 = (f32[4,3,16,128]{3,2,1,0:T(8,128)}, f32[4,3,16,128]{3,2,1,0:T(8,128)}) custom-call(f32[256,128]{1,0:T(8,128)S(1)} %bitcast.16, f32[256,128]{1,0:T(8,128)S(1)} %collective-permute-done.2.relayed, f32[4,3,16,128]{3,2,1,0:T(8,128)S(1)} %get-tuple-element.28.before, f32[3,16,128]{2,1,0:T(8,128)S(1)} %get-tuple-element.29.lowest, ...), custom_call_target="tpu_custom_call" | custom-call | tf_op jit(solution)/shard_map/finish/pallas_call | solution.py:732
Async XLA Ops:
  2.5 9.0 %copy-start = (f32[4,16,3,128]{3,1,2,0:T(8,128)S(1)}, f32[4,16,3,128]{3,1,2,0:T(8,128)}, u32[]{:S(2)}) copy-start(f32[4,16,3,128]{3,1,2,0:T(8,128)} %param.7) | copy-start | bytes 294916
  2.5 9.0 %copy-start.1 = (f32[4,16,128]{2,1,0:T(8,128)S(1)}, f32[4,16,128]{2,1,0:T(8,128)}, u32[]{:S(2)}) copy-start(f32[4,16,128]{2,1,0:T(8,128)} %growth.3) | copy-start | bytes 98308
  2.5 9.0 %copy-start.2 = (f32[4,16,128]{2,1,0:T(8,128)S(1)}, f32[4,16,128]{2,1,0:T(8,128)}, u32[]{:S(2)}) copy-start(f32[4,16,128]{2,1,0:T(8,128)} %shear.3) | copy-start | bytes 98308
  2.6 9.0 %copy-start.3 = (f32[4,16,3,128]{3,1,2,0:T(8,128)S(1)}, f32[4,16,3,128]{3,1,2,0:T(8,128)}, u32[]{:S(2)}) copy-start(f32[4,16,3,128]{3,1,2,0:T(8,128)} %param.8) | copy-start | bytes 294916
  2.6 15.5 %all-to-all-start = ((f32[32,8,128]{2,1,0:T(8,128)}), f32[32,8,128]{2,1,0:T(8,128)S(1)}, u32[]{:S(2)}, u32[]{:S(2)}) async-start(f32[32,8,128]{2,1,0:T(8,128)} %bitcast.23), calls=%async_computation | async-start | bytes 262144 | tf_op jit(solution)/shard_map/all_to_all | solution.py:681
  9.9 3.4 %collective-permute-start = (f32[5,16,128]{2,1,0:T(8,128)}, f32[5,16,128]{2,1,0:T(8,128)S(1)}, u32[]{:S(2)}, u32[]{:S(2)}) collective-permute-start(f32[5,16,128]{2,1,0:T(8,128)} %get-tuple-element.24), channel_id=1, source_target_pairs={{0,1},{2,3},{1,0},{3,2},{4,5},{6,7},{5,4},{7,6},{8,9},{10,11},{9,8... | collective-permute-start | bytes 122888 | tf_op jit(solution)/shard_map/ppermute | solution.py:677
  10.2 3.1 %collective-permute-start.1 = (f32[5,16,128]{2,1,0:T(8,128)}, f32[5,16,128]{2,1,0:T(8,128)S(1)}, u32[]{:S(2)}, u32[]{:S(2)}) collective-permute-start(f32[5,16,128]{2,1,0:T(8,128)} %get-tuple-element.25), channel_id=1, source_target_pairs={{1,2},{2,1},{5,6},{6,5},{9,10},{10,9},{13,14},{14,13},{17,18},{18,... | collective-permute-start | bytes 122888 | tf_op jit(solution)/shard_map/ppermute | solution.py:678
  11.5 0.7 %copy-start.4 = (s32[1,1,3,16]{3,1,2,0:T(1,128)S(1)}, s32[1,1,3,16]{3,1,2,0:T(1,128)}, u32[]{:S(2)}) copy-start(s32[1,1,3,16]{3,1,2,0:T(1,128)} %param.11) | copy-start | bytes 580
  11.5 0.7 %copy-start.5 = (f32[1,1,3,16]{3,1,2,0:T(1,128)S(1)}, f32[1,1,3,16]{3,1,2,0:T(1,128)}, u32[]{:S(2)}) copy-start(f32[1,1,3,16]{3,1,2,0:T(1,128)} %param.13) | copy-start | bytes 580
  18.1 1.3 %collective-permute-start.2 = (f32[256,128]{1,0:T(8,128)S(1)}, f32[256,128]{1,0:T(8,128)S(1)}, u32[]{:S(2)}, u32[]{:S(2)}) collective-permute-start(f32[256,128]{1,0:T(8,128)S(1)} %bitcast.14), channel_id=1, source_target_pairs={{0,1},{2,3},{1,0},{3,2},{4,5},{6,7},{5,4},{7,6},{8,9},{10,11},{9,8... | collective-permute-start | bytes 393224 | tf_op jit(solution)/shard_map/ppermute | solution.py:712

commit v6 on v5

--- a/solution.py
+++ b/solution.py
@@ -20,7 +20,7 @@
 SMEM = pl.BlockSpec(memory_space=pltpu.SMEM)
 HBM = pl.BlockSpec(memory_space=pltpu.HBM)
 PARAMS = pltpu.CompilerParams(vmem_limit_bytes=16 << 20)
-NEAR_TURNS = 4
+NEAR_TURNS = 8
 ROOT = math.sqrt(math.log2(math.e))
 
 
@@ -179,17 +179,19 @@
     for move in moves:
         move.start()
     tall = TILES * ROWS
+    span = 1 << pairs.bit_length()
     blank = jnp.zeros((tall, patch_len), jnp.float32)
 
     def base_of(m, slab):
         return pl.multiple_of((m * slabs + slab) * tall, tall)
 
     def clear(m):
-        counted[m] = 0
+        counted[m] = m * (slabs * tall * span)
         packet[pl.ds(base_of(m, depth), tall), :] = blank
         packet[pl.ds(base_of(m, partner), tall), :] = blank
 
     disp[slab_len * 3 * width_y :, :] = jnp.zeros((ROWS * width_y, patch_len), jnp.float32)
+    spare = region * (slabs * tall)
     each(regions, clear, 16)
     for move in moves:
         move.wait()
@@ -200,12 +202,13 @@
 
     def place(k):
         own, other = slots[0, 0, 0, k], slots[0, 1, 0, k]
-        position = counted[other]
-        counted[other] = position + 1
+        state = counted[other]
+        counted[other] = state + 1
+        first, position = split(state, span)
         fits = position < CAP
-        place_in = jnp.where(fits, position, 0)
-        side, offset = split(place_in, TILES)
-        m = jnp.where(fits, other, region)
+        first = jnp.where(fits, first, spare)
+        side, offset = split(jnp.where(fits, position, 0), TILES)
+        first = first + offset * ROWS
         z, y = split(own, width_y)
         tile = disp[pl.ds(z * (3 * width_y) + y, ROWS, stride=width_y), :]
         label = jnp.full((ROWS, patch_len), own, jnp.int32).astype(jnp.float32)
@@ -216,7 +219,7 @@
             (depth, jnp.where(lane < half, tile, turned)),
             (partner, jnp.where(lane < half, turned, tile)),
         ):
-            base = pl.multiple_of((m * slabs + slab) * tall + offset * ROWS, ROWS)
+            base = pl.multiple_of(first + slab * tall, ROWS)
             pltpu.store(packet.at[pl.ds(base, ROWS), :], value, mask=mask)
 
     each(pairs, place, 16)
@@ -506,7 +509,7 @@
         chosen = yield
     lane = lane_of((pairs, patch_len))
     for c in range(3):
-        value = picked(chosen, tiles[pl.ds(c, regions * TILES, stride=ROWS), :], 0)
+        value = picked(chosen, tiles[pl.ds(c, regions * TILES, stride=ROWS), :], 1)
         value = jnp.where(lane < half, value[:pairs], value[pairs:])
         yield value + roll(value, half, 1)
 
@@ -536,7 +539,7 @@
     for label, repeated in zip(labels, again):
         label = jnp.where(repeated, -1.0, label)[:, 0:pairs]
         chosen.append(jnp.where((region_row == slots[0, 1]) & (label == named), 1.0, 0.0))
-    return jnp.concatenate(chosen, axis=1)
+    return jnp.concatenate([jnp.transpose(value) for value in chosen], axis=0)
 
 
 def contact_half(dims, near, far, part, write):
@@ -571,7 +574,9 @@
     each(pairs // block, lambda step: some(step * block), 2)
 
 
-def contact_kernel(dims, arrived, near, slots, chosen, pushes, far, tiles):
+def contact_kernel(
+    dims, arrived, near, slots, before, lowest, highest, selector, chosen, moved, far, tiles, pushes
+):
     points = far_points(dims, arrived, None, tiles)
     next(points)
     chosen[...] = tile_choice(dims, slots, tiles)
@@ -583,18 +588,25 @@
         pushes[c, rows, :] = total
 
     contact_half(dims, near, far, 0, write)
+    slab_len, width_y, patch_len, regions, slabs, pairs = dims
+    for c in range(3):
+        push = picked(selector[...], pushes[c], 1) * (1.0 / ROOT)
+        for z in range(slab_len):
+            force = push[z * width_y : (z + 1) * width_y, :]
+            if z == 0:
+                force = force + lowest[c]
+            if z == slab_len - 1:
+                force = force + highest[c]
+            moved[z, c] = before[z, c] + STEP_TIME * force
 
 
 def finish_kernel(
     dims,
     arrived,
     relayed,
-    before,
-    lowest,
-    highest,
+    moved,
     near,
     chosen,
-    pushes,
     own_columns,
     disp,
     selector,
@@ -606,14 +618,14 @@
 ):
     slab_len, width_y, patch_len, regions, slabs, pairs = dims
     half = patch_len // 2
+    borders = border_forces(dims, arrived, relayed, own_columns)
     for c, value in enumerate(far_points(dims, relayed, chosen[...], tiles)):
         far[c] = value
 
     def write(c, rows, total):
-        total_push[c, rows, :] = pushes[c, rows, :] + total
+        total_push[c, rows, :] = total
 
     contact_half(dims, near, far, 1, write)
-    borders = border_forces(dims, arrived, relayed, own_columns)
     half_rows = width_y // 2
     lane = lane_of((half_rows, patch_len))
     last = patch_len - 1
@@ -626,13 +638,9 @@
                 rows = slice(part * half_rows, (part + 1) * half_rows)
                 start = z * width_y + part * half_rows
                 force = push[start : start + half_rows, :]
-                if z == 0:
-                    force = force + lowest[c, rows, :]
-                if z == slab_len - 1:
-                    force = force + highest[c, rows, :]
                 force = force + jnp.where(lane == 0, roll(edge, -at, 1), 0.0)
                 force = force + jnp.where(lane == last, roll(edge, last - half - at, 1), 0.0)
-                speed = before[z, c, rows, :] + STEP_TIME * force
+                speed = moved[z, c, rows, :] + STEP_TIME * force
                 new_velocity[z, c, rows, :] = speed
                 new_disp[z, c, rows, :] = disp[z, c, rows, :] + STEP_TIME * speed
 
@@ -712,22 +720,23 @@
     relayed = lax.ppermute(arrived, ("pair", "core"), links[0])
 
     tile_rows = regions * TILES
-    chosen, pushes = pl.pallas_call(
+    chosen, moved = pl.pallas_call(
         functools.partial(contact_kernel, dims),
         out_shape=(
-            jax.ShapeDtypeStruct((tile_rows, 2 * pairs), f32),
-            jax.ShapeDtypeStruct((3, pairs, patch_len), f32),
+            jax.ShapeDtypeStruct((2 * pairs, tile_rows), f32),
+            jax.ShapeDtypeStruct((slab_len, 3, *plane), f32),
         ),
-        in_specs=[VMEM] * 3,
+        in_specs=[VMEM] * 7,
         out_specs=(VMEM,) * 2,
         scratch_shapes=[
             pltpu.VMEM((3, pairs, patch_len), f32),
             pltpu.VMEM((tile_rows * ROWS, patch_len), f32),
+            pltpu.VMEM((3, pairs, patch_len), f32),
         ],
         compiler_params=PARAMS,
         name="contact",
         cost_estimate=pl.CostEstimate(flops=6000 * 1024, bytes_accessed=1 << 20, transcendentals=0),
-    )(arrived, near, slots)
+    )(arrived, near, slots, before, lowest, highest, selector)
 
     new_velocity, new_disp = pl.pallas_call(
         functools.partial(finish_kernel, dims),
@@ -735,7 +744,7 @@
             jax.ShapeDtypeStruct((slab_len, 3, *plane), f32),
             jax.ShapeDtypeStruct((slab_len, 3, *plane), f32),
         ),
-        in_specs=[VMEM] * 11,
+        in_specs=[VMEM] * 8,
         out_specs=(VMEM, VMEM),
         scratch_shapes=[
             pltpu.VMEM((3, pairs, patch_len), f32),
@@ -747,12 +756,9 @@
     )(
         arrived,
         relayed,
-        before,
-        lowest,
-        highest,
+        moved,
         near,
         chosen,
-        pushes,
         own_columns,
         disp,
         selector,

time: 21.4 us -> 21.3 us (level)
  no operation moved by 1% of the time
where the time goes in v6:
time: 21.3 us; the launch traced here: 21.1 us
  starting transfers between devices  8.51 us (40%)
  Pallas kernels  5.93 us (28%)
  waiting for transfers between devices  4.56 us (21%)
  between operations  1.41 us (7%)
  local copies, waits for them, and re-layouts  0.67 us (3%)
    all_to_all x1, starting transfers between devices, local(): lax.all_to_all(packet, ('region', 'pair', 'core'), 0, 0, tiled=True)  7.33 us
    all_to_all x1, waiting for transfers between devices, local(): lax.all_to_all(packet, ('region', 'pair', 'core'), 0, 0, tiled=True)  4.36 us
    pallas_call x1, Pallas kernels, local(): pl.pallas_call(functools.partial(pack_kernel, dims), out_shape=(jax.Shape...  1.89 us
    pallas_call x1, Pallas kernels, local(): pl.pallas_call(functools.partial(finish_kernel, dims), out_shape=(jax.Sha...  1.61 us
    pallas_call x1, Pallas kernels, local(): pl.pallas_call(functools.partial(inner_kernel, dims), out_shape=(jax.Shap...  1.09 us
    pallas_call x1, Pallas kernels, local(): pl.pallas_call(functools.partial(contact_kernel, dims), out_shape=(jax.Sh...  0.93 us
    unnamed x12, local copies, waits for them, and re-layouts  0.67 us
    ppermute x1, starting transfers between devices, local(): face_b = lax.ppermute(face_b, ('pair', 'core'), links[1])  0.65 us
  transfers between devices with their start and end apart: 4, of which 2 were waited for; matrix products, arithmetic and copies ran while one was open for 0% of the time, Pallas kernels for 11%

profile of v6, /device:TPU:0, one launch (start us, length us, event | category | flops | bytes accessed | tf_op | source)
XLA Modules:
  0.0 21.1 jit_solution(9014923853052445714)
XLA Ops:
  0.6 1.9 %pack.1 = (f32[256,128]{1,0:T(8,128)}, f32[5,16,128]{2,1,0:T(8,128)}, f32[5,16,128]{2,1,0:T(8,128)}) custom-call(f32[192,128]{1,0:T(8,128)} %bitcast.10, f32[4,16,128]{2,1,0:T(8,128)} %growth.3, f32[4,16,128]{2,1,0:T(8,128)} %shear.3, s32[1,3,1,16]{3,2,1,0:T(1,128)} %bitcast.18), custom_call_target="tpu_custom_call" | custom-call | tf_op jit(solution)/shard_map/pack/pallas_call | solution.py:662
  2.5 0.0 copy-start
  2.5 0.0 copy-start.1
  2.6 0.0 copy-start.2
  2.6 0.0 copy-start.3
  2.6 7.3 %all-to-all-start = ((f32[32,8,128]{2,1,0:T(8,128)}), f32[32,8,128]{2,1,0:T(8,128)S(1)}, u32[]{:S(2)}, u32[]{:S(2)}) async-start(f32[32,8,128]{2,1,0:T(8,128)} %bitcast.23), calls=%async_computation | async-start | bytes 262144 | tf_op jit(solution)/shard_map/all_to_all | solution.py:689
  9.9 0.3 %collective-permute-start = (f32[5,16,128]{2,1,0:T(8,128)}, f32[5,16,128]{2,1,0:T(8,128)S(1)}, u32[]{:S(2)}, u32[]{:S(2)}) collective-permute-start(f32[5,16,128]{2,1,0:T(8,128)} %get-tuple-element.24), channel_id=1, source_target_pairs={{0,1},{2,3},{1,0},{3,2},{4,5},{6,7},{5,4},{7,6},{8,9},{10,11},{9,8... | collective-permute-start | bytes 122888 | tf_op jit(solution)/shard_map/ppermute | solution.py:685
  10.2 0.7 %collective-permute-start.1 = (f32[5,16,128]{2,1,0:T(8,128)}, f32[5,16,128]{2,1,0:T(8,128)S(1)}, u32[]{:S(2)}, u32[]{:S(2)}) collective-permute-start(f32[5,16,128]{2,1,0:T(8,128)} %get-tuple-element.25), channel_id=1, source_target_pairs={{1,2},{2,1},{5,6},{6,5},{9,10},{10,9},{13,14},{14,13},{17,18},{18,... | collective-permute-start | bytes 122888 | tf_op jit(solution)/shard_map/ppermute | solution.py:686
  11.5 0.0 copy-start.4
  11.6 0.0 copy-start.5
  11.6 0.0 copy-done
  11.6 0.0 copy-done.1
  11.6 0.0 copy-done.2
  11.6 0.0 copy-done.3
  11.6 0.6 %copy-done.4 = s32[1,1,3,16]{3,1,2,0:T(1,128)S(1)} copy-done((s32[1,1,3,16]{3,1,2,0:T(1,128)S(1)}, s32[1,1,3,16]{3,1,2,0:T(1,128)}, u32[]{:S(2)}) %copy-start.4) | copy-done | bytes 216
  12.2 0.0 copy-done.5
  12.2 1.1 %inner.1 = (f32[4,3,16,128]{3,2,1,0:T(8,128)S(1)}, f32[3,16,128]{2,1,0:T(8,128)S(1)}, f32[64,16]{1,0:T(8,128)S(1)}) custom-call(f32[4,3,16,128]{3,2,1,0:T(8,128)S(1)} %bitcast.11, f32[4,16,128]{2,1,0:T(8,128)S(1)} %copy-done.1, f32[4,16,128]{2,1,0:T(8,128)S(1)} %copy-done.2, f32[4,3,16,128]{3,2,1,0:T(8,128)S(1)} %bitcast.17, s32[1,3,1,16]{3,2,1,0:T(1,128)S(1)} %bitcast.19, ...), custom_call_target="tpu_custom_call" | custom-call | flops 4096000 | bytes 1048576 | tf_op jit(solution)/shard_map/inner/pallas_call | solution.py:691
  13.3 0.0 collective-permute-done.face_a
  13.3 0.0 collective-permute-done.1.face_b
  13.4 0.4 %outer.1 = (f32[3,16,128]{2,1,0:T(8,128)S(1)}, f32[3,16,128]{2,1,0:T(8,128)S(1)}, f32[2,8,128]{2,1,0:T(8,128)S(1)}) custom-call(f32[4,3,16,128]{3,2,1,0:T(8,128)S(1)} %bitcast.12, f32[4,16,128]{2,1,0:T(8,128)S(1)} %copy-done.1, f32[4,16,128]{2,1,0:T(8,128)S(1)} %copy-done.2, f32[5,16,128]{2,1,0:T(8,128)S(1)} %collective-permute-done.face_a, ...), custom_call_target="tpu_custom_call" | custom-call | flops 2048000 | bytes 1048576 | tf_op jit(solution)/shard_map/outer/pallas_call | solution.py:705
  13.8 4.4 %all-to-all-done = f32[32,8,128]{2,1,0:T(8,128)S(1)} async-done(((f32[32,8,128]{2,1,0:T(8,128)}), f32[32,8,128]{2,1,0:T(8,128)S(1)}, u32[]{:S(2)}, u32[]{:S(2)}) %all-to-all-start) | async-done | bytes 131104 | tf_op jit(solution)/shard_map/all_to_all | solution.py:689
  18.1 0.2 %collective-permute-start.2 = (f32[256,128]{1,0:T(8,128)S(1)}, f32[256,128]{1,0:T(8,128)S(1)}, u32[]{:S(2)}, u32[]{:S(2)}) collective-permute-start(f32[256,128]{1,0:T(8,128)S(1)} %bitcast.14), channel_id=1, source_target_pairs={{0,1},{2,3},{1,0},{3,2},{4,5},{6,7},{5,4},{7,6},{8,9},{10,11},{9,8... | collective-permute-start | bytes 393224 | tf_op jit(solution)/shard_map/ppermute | solution.py:720
  18.3 0.9 %contact.1 = (f32[32,16]{1,0:T(8,128)S(1)}, f32[4,3,16,128]{3,2,1,0:T(8,128)S(1)}) custom-call(f32[256,128]{1,0:T(8,128)S(1)} %bitcast.15, f32[3,16,128]{2,1,0:T(8,128)S(1)} %get-tuple-element.28.near, s32[1,3,1,16]{3,2,1,0:T(1,128)S(1)} %bitcast.21, f32[4,3,16,128]{3,2,1,0:T(8,128)S(1)} %get-tuple-element.29.before, ...), custom_call_target="tpu_custom_call" | custom-call | flops 6144000 | bytes 1048576 | tf_op jit(solution)/shard_map/contact/pallas_call | solution.py:723
  19.3 0.2 collective-permute-done.2.relayed
  19.5 1.6 %finish.1 = (f32[4,3,16,128]{3,2,1,0:T(8,128)}, f32[4,3,16,128]{3,2,1,0:T(8,128)}) custom-call(f32[256,128]{1,0:T(8,128)S(1)} %bitcast.16, f32[256,128]{1,0:T(8,128)S(1)} %collective-permute-done.2.relayed, f32[4,3,16,128]{3,2,1,0:T(8,128)S(1)} %get-tuple-element.33.moved, f32[3,16,128]{2,1,0:T(8,128)S(1)} %get-tuple-element.28.near, ...), custom_call_target="tpu_custom_call" | custom-call | tf_op jit(solution)/shard_map/finish/pallas_call | solution.py:741
Async XLA Ops:
  2.5 9.0 %copy-start = (f32[4,16,3,128]{3,1,2,0:T(8,128)S(1)}, f32[4,16,3,128]{3,1,2,0:T(8,128)}, u32[]{:S(2)}) copy-start(f32[4,16,3,128]{3,1,2,0:T(8,128)} %param.7) | copy-start | bytes 294916
  2.5 9.0 %copy-start.1 = (f32[4,16,128]{2,1,0:T(8,128)S(1)}, f32[4,16,128]{2,1,0:T(8,128)}, u32[]{:S(2)}) copy-start(f32[4,16,128]{2,1,0:T(8,128)} %growth.3) | copy-start | bytes 98308
  2.6 9.0 %copy-start.2 = (f32[4,16,128]{2,1,0:T(8,128)S(1)}, f32[4,16,128]{2,1,0:T(8,128)}, u32[]{:S(2)}) copy-start(f32[4,16,128]{2,1,0:T(8,128)} %shear.3) | copy-start | bytes 98308
  2.6 9.0 %copy-start.3 = (f32[4,16,3,128]{3,1,2,0:T(8,128)S(1)}, f32[4,16,3,128]{3,1,2,0:T(8,128)}, u32[]{:S(2)}) copy-start(f32[4,16,3,128]{3,1,2,0:T(8,128)} %param.8) | copy-start | bytes 294916
  2.6 15.5 %all-to-all-start = ((f32[32,8,128]{2,1,0:T(8,128)}), f32[32,8,128]{2,1,0:T(8,128)S(1)}, u32[]{:S(2)}, u32[]{:S(2)}) async-start(f32[32,8,128]{2,1,0:T(8,128)} %bitcast.23), calls=%async_computation | async-start | bytes 262144 | tf_op jit(solution)/shard_map/all_to_all | solution.py:689
  9.9 3.4 %collective-permute-start = (f32[5,16,128]{2,1,0:T(8,128)}, f32[5,16,128]{2,1,0:T(8,128)S(1)}, u32[]{:S(2)}, u32[]{:S(2)}) collective-permute-start(f32[5,16,128]{2,1,0:T(8,128)} %get-tuple-element.24), channel_id=1, source_target_pairs={{0,1},{2,3},{1,0},{3,2},{4,5},{6,7},{5,4},{7,6},{8,9},{10,11},{9,8... | collective-permute-start | bytes 122888 | tf_op jit(solution)/shard_map/ppermute | solution.py:685
  10.2 3.1 %collective-permute-start.1 = (f32[5,16,128]{2,1,0:T(8,128)}, f32[5,16,128]{2,1,0:T(8,128)S(1)}, u32[]{:S(2)}, u32[]{:S(2)}) collective-permute-start(f32[5,16,128]{2,1,0:T(8,128)} %get-tuple-element.25), channel_id=1, source_target_pairs={{1,2},{2,1},{5,6},{6,5},{9,10},{10,9},{13,14},{14,13},{17,18},{18,... | collective-permute-start | bytes 122888 | tf_op jit(solution)/shard_map/ppermute | solution.py:686
  11.5 0.7 %copy-start.4 = (s32[1,1,3,16]{3,1,2,0:T(1,128)S(1)}, s32[1,1,3,16]{3,1,2,0:T(1,128)}, u32[]{:S(2)}) copy-start(s32[1,1,3,16]{3,1,2,0:T(1,128)} %param.11) | copy-start | bytes 580
  11.6 0.7 %copy-start.5 = (f32[1,1,3,16]{3,1,2,0:T(1,128)S(1)}, f32[1,1,3,16]{3,1,2,0:T(1,128)}, u32[]{:S(2)}) copy-start(f32[1,1,3,16]{3,1,2,0:T(1,128)} %param.13) | copy-start | bytes 580
  18.1 1.3 %collective-permute-start.2 = (f32[256,128]{1,0:T(8,128)S(1)}, f32[256,128]{1,0:T(8,128)S(1)}, u32[]{:S(2)}, u32[]{:S(2)}) collective-permute-start(f32[256,128]{1,0:T(8,128)S(1)} %bitcast.14), channel_id=1, source_target_pairs={{0,1},{2,3},{1,0},{3,2},{4,5},{6,7},{5,4},{7,6},{8,9},{10,11},{9,8... | collective-permute-start | bytes 393224 | tf_op jit(solution)/shard_map/ppermute | solution.py:720

commit v7 on v6

--- a/solution.py
+++ b/solution.py
@@ -20,7 +20,7 @@
 SMEM = pl.BlockSpec(memory_space=pltpu.SMEM)
 HBM = pl.BlockSpec(memory_space=pltpu.HBM)
 PARAMS = pltpu.CompilerParams(vmem_limit_bytes=16 << 20)
-NEAR_TURNS = 8
+NEAR_TURNS = 32
 ROOT = math.sqrt(math.log2(math.e))
 
 
@@ -350,9 +350,13 @@
             point = disp[z, c, pl.ds(y, 1), :]
             if c == 0:
                 point = point + along
-            near[c, pl.ds(k, 1), :] = (point - separation[0, c, 0, k]) * ROOT
+            near[0, c, pl.ds(k, 1), :] = (point - separation[0, c, 0, k]) * ROOT
 
     each(pairs, fetch, 16)
+    for c in range(3):
+        value = near[0, c]
+        for turn in range(1, NEAR_TURNS):
+            near[turn, c] = roll(value, -turn * (patch_len // 2 // NEAR_TURNS), 1)
     patch_row = lax.broadcasted_iota(jnp.int32, selector.shape, 0)
     live = lax.broadcasted_iota(jnp.int32, selector.shape, 1) < count[0, 0]
     selector[...] = jnp.where((patch_row == slot_row[0, 0]) & live, 1.0, 0.0)
@@ -551,11 +555,10 @@
 
     def some(start):
         rows = pl.ds(start, block)
-        mine = [near[c, rows, :] for c in range(3)]
         theirs = [far[c, rows, :] for c in range(3)]
         theirs = [(theirs[0] + along) * ROOT, theirs[1] * ROOT, theirs[2] * ROOT]
         starts = range(0, half, half // NEAR_TURNS)
-        turned = [[roll(value, -a, 1) for value in mine] for a in starts]
+        turned = [[near[turn, c, rows, :] for c in range(3)] for turn in range(NEAR_TURNS)]
         sums = [[None] * 3 for _ in starts]
         for b in range(half // NEAR_TURNS):
             other = [roll(value, b, 1) for value in theirs]
@@ -692,7 +695,7 @@
         functools.partial(inner_kernel, dims),
         out_shape=(
             jax.ShapeDtypeStruct((slab_len, 3, *plane), f32),
-            jax.ShapeDtypeStruct((3, pairs, patch_len), f32),
+            jax.ShapeDtypeStruct((NEAR_TURNS, 3, pairs, patch_len), f32),
             jax.ShapeDtypeStruct((slab_len * width_y, pairs), f32),
         ),
         in_specs=[VMEM] * 4 + [SMEM, VMEM, SMEM, SMEM],

time: 21.3 us -> 21.3 us (level)
    pallas_call x1, Pallas kernels: 1.09 us -> 1.31 us  [local(): pl.pallas_call(functools.partial(inner_kernel, dims), out_shape=(jax.Shap...]
    all_to_all x1, waiting for transfers between devices: 4.36 us -> 4.14 us  [local(): lax.all_to_all(packet, ('region', 'pair', 'core'), 0, 0, tiled=True)]
  transfers between devices with their start and end apart: 4 -> 4, of which waited for: 2 -> 2; matrix products, arithmetic and copies ran while one was open for 0% -> 0% of each run, Pallas kernels for 11% -> 12%
where the time goes in v7:
time: 21.3 us; the launch traced here: 21 us
  starting transfers between devices  8.52 us (40%)
  Pallas kernels  6.04 us (28%)
  waiting for transfers between devices  4.36 us (20%)
  between operations  1.41 us (7%)
  local copies, waits for them, and re-layouts  0.67 us (3%)
    all_to_all x1, starting transfers between devices, local(): lax.all_to_all(packet, ('region', 'pair', 'core'), 0, 0, tiled=True)  7.33 us
    all_to_all x1, waiting for transfers between devices, local(): lax.all_to_all(packet, ('region', 'pair', 'core'), 0, 0, tiled=True)  4.14 us
    pallas_call x1, Pallas kernels, local(): pl.pallas_call(functools.partial(pack_kernel, dims), out_shape=(jax.Shape...  1.89 us
    pallas_call x1, Pallas kernels, local(): pl.pallas_call(functools.partial(finish_kernel, dims), out_shape=(jax.Sha...  1.53 us
    pallas_call x1, Pallas kernels, local(): pl.pallas_call(functools.partial(inner_kernel, dims), out_shape=(jax.Shap...  1.31 us
    pallas_call x1, Pallas kernels, local(): pl.pallas_call(functools.partial(contact_kernel, dims), out_shape=(jax.Sh...  0.91 us
    unnamed x12, local copies, waits for them, and re-layouts  0.67 us
    ppermute x1, starting transfers between devices, local(): face_b = lax.ppermute(face_b, ('pair', 'core'), links[1])  0.65 us
  transfers between devices with their start and end apart: 4, of which 2 were waited for; matrix products, arithmetic and copies ran while one was open for 0% of the time, Pallas kernels for 12%

profile of v7, /device:TPU:0, one launch (start us, length us, event | category | flops | bytes accessed | tf_op | source)
XLA Modules:
  0.0 21.0 jit_solution(16746481879737335220)
XLA Ops:
  0.6 1.9 %pack.1 = (f32[256,128]{1,0:T(8,128)}, f32[5,16,128]{2,1,0:T(8,128)}, f32[5,16,128]{2,1,0:T(8,128)}) custom-call(f32[192,128]{1,0:T(8,128)} %bitcast.10, f32[4,16,128]{2,1,0:T(8,128)} %growth.3, f32[4,16,128]{2,1,0:T(8,128)} %shear.3, s32[1,3,1,16]{3,2,1,0:T(1,128)} %bitcast.18), custom_call_target="tpu_custom_call" | custom-call | tf_op jit(solution)/shard_map/pack/pallas_call | solution.py:665
  2.5 0.0 copy-start
  2.5 0.0 copy-start.1
  2.6 0.0 copy-start.2
  2.6 0.0 copy-start.3
  2.6 7.3 %all-to-all-start = ((f32[32,8,128]{2,1,0:T(8,128)}), f32[32,8,128]{2,1,0:T(8,128)S(1)}, u32[]{:S(2)}, u32[]{:S(2)}) async-start(f32[32,8,128]{2,1,0:T(8,128)} %bitcast.23), calls=%async_computation | async-start | bytes 262144 | tf_op jit(solution)/shard_map/all_to_all | solution.py:692
  9.9 0.3 %collective-permute-start = (f32[5,16,128]{2,1,0:T(8,128)}, f32[5,16,128]{2,1,0:T(8,128)S(1)}, u32[]{:S(2)}, u32[]{:S(2)}) collective-permute-start(f32[5,16,128]{2,1,0:T(8,128)} %get-tuple-element.24), channel_id=1, source_target_pairs={{0,1},{2,3},{1,0},{3,2},{4,5},{6,7},{5,4},{7,6},{8,9},{10,11},{9,8... | collective-permute-start | bytes 122888 | tf_op jit(solution)/shard_map/ppermute | solution.py:688
  10.2 0.7 %collective-permute-start.1 = (f32[5,16,128]{2,1,0:T(8,128)}, f32[5,16,128]{2,1,0:T(8,128)S(1)}, u32[]{:S(2)}, u32[]{:S(2)}) collective-permute-start(f32[5,16,128]{2,1,0:T(8,128)} %get-tuple-element.25), channel_id=1, source_target_pairs={{1,2},{2,1},{5,6},{6,5},{9,10},{10,9},{13,14},{14,13},{17,18},{18,... | collective-permute-start | bytes 122888 | tf_op jit(solution)/shard_map/ppermute | solution.py:689
  11.5 0.0 copy-start.4
  11.6 0.0 copy-start.5
  11.6 0.0 copy-done
  11.6 0.0 copy-done.1
  11.6 0.0 copy-done.2
  11.6 0.0 copy-done.3
  11.6 0.6 %copy-done.4 = s32[1,1,3,16]{3,1,2,0:T(1,128)S(1)} copy-done((s32[1,1,3,16]{3,1,2,0:T(1,128)S(1)}, s32[1,1,3,16]{3,1,2,0:T(1,128)}, u32[]{:S(2)}) %copy-start.4) | copy-done | bytes 216
  12.2 0.0 copy-done.5
  12.2 1.3 %inner.1 = (f32[4,3,16,128]{3,2,1,0:T(8,128)S(1)}, f32[32,3,16,128]{3,2,1,0:T(8,128)S(1)}, f32[64,16]{1,0:T(8,128)S(1)}) custom-call(f32[4,3,16,128]{3,2,1,0:T(8,128)S(1)} %bitcast.11, f32[4,16,128]{2,1,0:T(8,128)S(1)} %copy-done.1, f32[4,16,128]{2,1,0:T(8,128)S(1)} %copy-done.2, f32[4,3,16,128]{3,2,1,0:T(8,128)S(1)} %bitcast.17, ...), custom_call_target="tpu_custom_call" | custom-call | flops 4096000 | bytes 1048576 | tf_op jit(solution)/shard_map/inner/pallas_call | solution.py:694
  13.6 0.0 collective-permute-done.face_a
  13.6 0.0 collective-permute-done.1.face_b
  13.6 0.4 %outer.1 = (f32[3,16,128]{2,1,0:T(8,128)S(1)}, f32[3,16,128]{2,1,0:T(8,128)S(1)}, f32[2,8,128]{2,1,0:T(8,128)S(1)}) custom-call(f32[4,3,16,128]{3,2,1,0:T(8,128)S(1)} %bitcast.12, f32[4,16,128]{2,1,0:T(8,128)S(1)} %copy-done.1, f32[4,16,128]{2,1,0:T(8,128)S(1)} %copy-done.2, f32[5,16,128]{2,1,0:T(8,128)S(1)} %collective-permute-done.face_a, ...), custom_call_target="tpu_custom_call" | custom-call | flops 2048000 | bytes 1048576 | tf_op jit(solution)/shard_map/outer/pallas_call | solution.py:708
  14.0 4.1 %all-to-all-done = f32[32,8,128]{2,1,0:T(8,128)S(1)} async-done(((f32[32,8,128]{2,1,0:T(8,128)}), f32[32,8,128]{2,1,0:T(8,128)S(1)}, u32[]{:S(2)}, u32[]{:S(2)}) %all-to-all-start) | async-done | bytes 131104 | tf_op jit(solution)/shard_map/all_to_all | solution.py:692
  18.1 0.2 %collective-permute-start.2 = (f32[256,128]{1,0:T(8,128)S(1)}, f32[256,128]{1,0:T(8,128)S(1)}, u32[]{:S(2)}, u32[]{:S(2)}) collective-permute-start(f32[256,128]{1,0:T(8,128)S(1)} %bitcast.14), channel_id=1, source_target_pairs={{0,1},{2,3},{1,0},{3,2},{4,5},{6,7},{5,4},{7,6},{8,9},{10,11},{9,8... | collective-permute-start | bytes 393224 | tf_op jit(solution)/shard_map/ppermute | solution.py:723
  18.3 0.9 %contact.1 = (f32[32,16]{1,0:T(8,128)S(1)}, f32[4,3,16,128]{3,2,1,0:T(8,128)S(1)}) custom-call(f32[256,128]{1,0:T(8,128)S(1)} %bitcast.15, f32[32,3,16,128]{3,2,1,0:T(8,128)S(1)} %get-tuple-element.28.near, s32[1,3,1,16]{3,2,1,0:T(1,128)S(1)} %bitcast.21, f32[4,3,16,128]{3,2,1,0:T(8,128)S(1)} %get-tuple-element.29.before, ...), custom_call_target="tpu_custom_call" | custom-call | flops 6144000 | bytes 1048576 | tf_op jit(solution)/shard_map/contact/pallas_call | solution.py:726
  19.3 0.2 %collective-permute-done.2.relayed = f32[256,128]{1,0:T(8,128)S(1)} collective-permute-done((f32[256,128]{1,0:T(8,128)S(1)}, f32[256,128]{1,0:T(8,128)S(1)}, u32[]{:S(2)}, u32[]{:S(2)}) %collective-permute-start.2) | collective-permute-done | bytes 131104 | tf_op jit(solution)/shard_map/ppermute | solution.py:723
  19.5 1.5 %finish.1 = (f32[4,3,16,128]{3,2,1,0:T(8,128)}, f32[4,3,16,128]{3,2,1,0:T(8,128)}) custom-call(f32[256,128]{1,0:T(8,128)S(1)} %bitcast.16, f32[256,128]{1,0:T(8,128)S(1)} %collective-permute-done.2.relayed, f32[4,3,16,128]{3,2,1,0:T(8,128)S(1)} %get-tuple-element.33.moved, f32[32,3,16,128]{3,2,1,0:T(8,128)S(1)} %get-tuple-element.28.near, ...), custom_call_target="tpu_custom_call" | custom-call | tf_op jit(solution)/shard_map/finish/pallas_call | solution.py:744
Async XLA Ops:
  2.5 9.0 %copy-start = (f32[4,16,3,128]{3,1,2,0:T(8,128)S(1)}, f32[4,16,3,128]{3,1,2,0:T(8,128)}, u32[]{:S(2)}) copy-start(f32[4,16,3,128]{3,1,2,0:T(8,128)} %param.7) | copy-start | bytes 294916
  2.5 9.0 %copy-start.1 = (f32[4,16,128]{2,1,0:T(8,128)S(1)}, f32[4,16,128]{2,1,0:T(8,128)}, u32[]{:S(2)}) copy-start(f32[4,16,128]{2,1,0:T(8,128)} %growth.3) | copy-start | bytes 98308
  2.6 9.0 %copy-start.2 = (f32[4,16,128]{2,1,0:T(8,128)S(1)}, f32[4,16,128]{2,1,0:T(8,128)}, u32[]{:S(2)}) copy-start(f32[4,16,128]{2,1,0:T(8,128)} %shear.3) | copy-start | bytes 98308
  2.6 9.0 %copy-start.3 = (f32[4,16,3,128]{3,1,2,0:T(8,128)S(1)}, f32[4,16,3,128]{3,1,2,0:T(8,128)}, u32[]{:S(2)}) copy-start(f32[4,16,3,128]{3,1,2,0:T(8,128)} %param.8) | copy-start | bytes 294916
  2.6 15.5 %all-to-all-start = ((f32[32,8,128]{2,1,0:T(8,128)}), f32[32,8,128]{2,1,0:T(8,128)S(1)}, u32[]{:S(2)}, u32[]{:S(2)}) async-start(f32[32,8,128]{2,1,0:T(8,128)} %bitcast.23), calls=%async_computation | async-start | bytes 262144 | tf_op jit(solution)/shard_map/all_to_all | solution.py:692
  9.9 3.6 %collective-permute-start = (f32[5,16,128]{2,1,0:T(8,128)}, f32[5,16,128]{2,1,0:T(8,128)S(1)}, u32[]{:S(2)}, u32[]{:S(2)}) collective-permute-start(f32[5,16,128]{2,1,0:T(8,128)} %get-tuple-element.24), channel_id=1, source_target_pairs={{0,1},{2,3},{1,0},{3,2},{4,5},{6,7},{5,4},{7,6},{8,9},{10,11},{9,8... | collective-permute-start | bytes 122888 | tf_op jit(solution)/shard_map/ppermute | solution.py:688
  10.2 3.3 %collective-permute-start.1 = (f32[5,16,128]{2,1,0:T(8,128)}, f32[5,16,128]{2,1,0:T(8,128)S(1)}, u32[]{:S(2)}, u32[]{:S(2)}) collective-permute-start(f32[5,16,128]{2,1,0:T(8,128)} %get-tuple-element.25), channel_id=1, source_target_pairs={{1,2},{2,1},{5,6},{6,5},{9,10},{10,9},{13,14},{14,13},{17,18},{18,... | collective-permute-start | bytes 122888 | tf_op jit(solution)/shard_map/ppermute | solution.py:689
  11.5 0.7 %copy-start.4 = (s32[1,1,3,16]{3,1,2,0:T(1,128)S(1)}, s32[1,1,3,16]{3,1,2,0:T(1,128)}, u32[]{:S(2)}) copy-start(s32[1,1,3,16]{3,1,2,0:T(1,128)} %param.11) | copy-start | bytes 580
  11.6 0.7 %copy-start.5 = (f32[1,1,3,16]{3,1,2,0:T(1,128)S(1)}, f32[1,1,3,16]{3,1,2,0:T(1,128)}, u32[]{:S(2)}) copy-start(f32[1,1,3,16]{3,1,2,0:T(1,128)} %param.13) | copy-start | bytes 580
  18.1 1.3 %collective-permute-start.2 = (f32[256,128]{1,0:T(8,128)S(1)}, f32[256,128]{1,0:T(8,128)S(1)}, u32[]{:S(2)}, u32[]{:S(2)}) collective-permute-start(f32[256,128]{1,0:T(8,128)S(1)} %bitcast.14), channel_id=1, source_target_pairs={{0,1},{2,3},{1,0},{3,2},{4,5},{6,7},{5,4},{7,6},{8,9},{10,11},{9,8... | collective-permute-start | bytes 393224 | tf_op jit(solution)/shard_map/ppermute | solution.py:723

commit v8 on v7

--- a/solution.py
+++ b/solution.py
@@ -621,7 +621,6 @@
 ):
     slab_len, width_y, patch_len, regions, slabs, pairs = dims
     half = patch_len // 2
-    borders = border_forces(dims, arrived, relayed, own_columns)
     for c, value in enumerate(far_points(dims, relayed, chosen[...], tiles)):
         far[c] = value
 
@@ -629,6 +628,7 @@
         total_push[c, rows, :] = total
 
     contact_half(dims, near, far, 1, write)
+    borders = border_forces(dims, arrived, relayed, own_columns)
     half_rows = width_y // 2
     lane = lane_of((half_rows, patch_len))
     last = patch_len - 1

time: 21.3 us -> 21.4 us (level)
  no operation moved by 1% of the time
where the time goes in v8:
time: 21.4 us; the launch traced here: 21.1 us
  starting transfers between devices  8.51 us (40%)
  Pallas kernels  6.14 us (29%)
  waiting for transfers between devices  4.37 us (20%)
  between operations  1.41 us (7%)
  local copies, waits for them, and re-layouts  0.67 us (3%)
    all_to_all x1, starting transfers between devices, local(): lax.all_to_all(packet, ('region', 'pair', 'core'), 0, 0, tiled=True)  7.33 us
    all_to_all x1, waiting for transfers between devices, local(): lax.all_to_all(packet, ('region', 'pair', 'core'), 0, 0, tiled=True)  4.15 us
    pallas_call x1, Pallas kernels, local(): pl.pallas_call(functools.partial(pack_kernel, dims), out_shape=(jax.Shape...  1.89 us
    pallas_call x1, Pallas kernels, local(): pl.pallas_call(functools.partial(finish_kernel, dims), out_shape=(jax.Sha...  1.63 us
    pallas_call x1, Pallas kernels, local(): pl.pallas_call(functools.partial(inner_kernel, dims), out_shape=(jax.Shap...  1.31 us
    pallas_call x1, Pallas kernels, local(): pl.pallas_call(functools.partial(contact_kernel, dims), out_shape=(jax.Sh...  0.91 us
    unnamed x12, local copies, waits for them, and re-layouts  0.67 us
    ppermute x1, starting transfers between devices, local(): face_b = lax.ppermute(face_b, ('pair', 'core'), links[1])  0.65 us
  transfers between devices with their start and end apart: 4, of which 2 were waited for; matrix products, arithmetic and copies ran while one was open for 0% of the time, Pallas kernels for 12%

profile of v8, /device:TPU:0, one launch (start us, length us, event | category | flops | bytes accessed | tf_op | source)
XLA Modules:
  0.0 21.1 jit_solution(7252329957794478876)
XLA Ops:
  0.6 1.9 %pack.1 = (f32[256,128]{1,0:T(8,128)}, f32[5,16,128]{2,1,0:T(8,128)}, f32[5,16,128]{2,1,0:T(8,128)}) custom-call(f32[192,128]{1,0:T(8,128)} %bitcast.10, f32[4,16,128]{2,1,0:T(8,128)} %growth.3, f32[4,16,128]{2,1,0:T(8,128)} %shear.3, s32[1,3,1,16]{3,2,1,0:T(1,128)} %bitcast.18), custom_call_target="tpu_custom_call" | custom-call | tf_op jit(solution)/shard_map/pack/pallas_call | solution.py:665
  2.5 0.0 copy-start
  2.5 0.0 copy-start.1
  2.6 0.0 copy-start.2
  2.6 0.0 copy-start.3
  2.6 7.3 %all-to-all-start = ((f32[32,8,128]{2,1,0:T(8,128)}), f32[32,8,128]{2,1,0:T(8,128)S(1)}, u32[]{:S(2)}, u32[]{:S(2)}) async-start(f32[32,8,128]{2,1,0:T(8,128)} %bitcast.23), calls=%async_computation | async-start | bytes 262144 | tf_op jit(solution)/shard_map/all_to_all | solution.py:692
  9.9 0.3 %collective-permute-start = (f32[5,16,128]{2,1,0:T(8,128)}, f32[5,16,128]{2,1,0:T(8,128)S(1)}, u32[]{:S(2)}, u32[]{:S(2)}) collective-permute-start(f32[5,16,128]{2,1,0:T(8,128)} %get-tuple-element.24), channel_id=1, source_target_pairs={{0,1},{2,3},{1,0},{3,2},{4,5},{6,7},{5,4},{7,6},{8,9},{10,11},{9,8... | collective-permute-start | bytes 122888 | tf_op jit(solution)/shard_map/ppermute | solution.py:688
  10.2 0.7 %collective-permute-start.1 = (f32[5,16,128]{2,1,0:T(8,128)}, f32[5,16,128]{2,1,0:T(8,128)S(1)}, u32[]{:S(2)}, u32[]{:S(2)}) collective-permute-start(f32[5,16,128]{2,1,0:T(8,128)} %get-tuple-element.25), channel_id=1, source_target_pairs={{1,2},{2,1},{5,6},{6,5},{9,10},{10,9},{13,14},{14,13},{17,18},{18,... | collective-permute-start | bytes 122888 | tf_op jit(solution)/shard_map/ppermute | solution.py:689
  11.5 0.0 copy-start.4
  11.6 0.0 copy-start.5
  11.6 0.0 copy-done
  11.6 0.0 copy-done.1
  11.6 0.0 copy-done.2
  11.6 0.0 copy-done.3
  11.6 0.6 %copy-done.4 = s32[1,1,3,16]{3,1,2,0:T(1,128)S(1)} copy-done((s32[1,1,3,16]{3,1,2,0:T(1,128)S(1)}, s32[1,1,3,16]{3,1,2,0:T(1,128)}, u32[]{:S(2)}) %copy-start.4) | copy-done | bytes 216
  12.2 0.0 copy-done.5
  12.2 1.3 %inner.1 = (f32[4,3,16,128]{3,2,1,0:T(8,128)S(1)}, f32[32,3,16,128]{3,2,1,0:T(8,128)S(1)}, f32[64,16]{1,0:T(8,128)S(1)}) custom-call(f32[4,3,16,128]{3,2,1,0:T(8,128)S(1)} %bitcast.11, f32[4,16,128]{2,1,0:T(8,128)S(1)} %copy-done.1, f32[4,16,128]{2,1,0:T(8,128)S(1)} %copy-done.2, f32[4,3,16,128]{3,2,1,0:T(8,128)S(1)} %bitcast.17, ...), custom_call_target="tpu_custom_call" | custom-call | flops 4096000 | bytes 1048576 | tf_op jit(solution)/shard_map/inner/pallas_call | solution.py:694
  13.6 0.0 collective-permute-done.face_a
  13.6 0.0 collective-permute-done.1.face_b
  13.6 0.4 %outer.1 = (f32[3,16,128]{2,1,0:T(8,128)S(1)}, f32[3,16,128]{2,1,0:T(8,128)S(1)}, f32[2,8,128]{2,1,0:T(8,128)S(1)}) custom-call(f32[4,3,16,128]{3,2,1,0:T(8,128)S(1)} %bitcast.12, f32[4,16,128]{2,1,0:T(8,128)S(1)} %copy-done.1, f32[4,16,128]{2,1,0:T(8,128)S(1)} %copy-done.2, f32[5,16,128]{2,1,0:T(8,128)S(1)} %collective-permute-done.face_a, ...), custom_call_target="tpu_custom_call" | custom-call | flops 2048000 | bytes 1048576 | tf_op jit(solution)/shard_map/outer/pallas_call | solution.py:708
  14.0 4.1 %all-to-all-done = f32[32,8,128]{2,1,0:T(8,128)S(1)} async-done(((f32[32,8,128]{2,1,0:T(8,128)}), f32[32,8,128]{2,1,0:T(8,128)S(1)}, u32[]{:S(2)}, u32[]{:S(2)}) %all-to-all-start) | async-done | bytes 131104 | tf_op jit(solution)/shard_map/all_to_all | solution.py:692
  18.1 0.2 %collective-permute-start.2 = (f32[256,128]{1,0:T(8,128)S(1)}, f32[256,128]{1,0:T(8,128)S(1)}, u32[]{:S(2)}, u32[]{:S(2)}) collective-permute-start(f32[256,128]{1,0:T(8,128)S(1)} %bitcast.14), channel_id=1, source_target_pairs={{0,1},{2,3},{1,0},{3,2},{4,5},{6,7},{5,4},{7,6},{8,9},{10,11},{9,8... | collective-permute-start | bytes 393224 | tf_op jit(solution)/shard_map/ppermute | solution.py:723
  18.3 0.9 %contact.1 = (f32[32,16]{1,0:T(8,128)S(1)}, f32[4,3,16,128]{3,2,1,0:T(8,128)S(1)}) custom-call(f32[256,128]{1,0:T(8,128)S(1)} %bitcast.15, f32[32,3,16,128]{3,2,1,0:T(8,128)S(1)} %get-tuple-element.28.near, s32[1,3,1,16]{3,2,1,0:T(1,128)S(1)} %bitcast.21, f32[4,3,16,128]{3,2,1,0:T(8,128)S(1)} %get-tuple-element.29.before, ...), custom_call_target="tpu_custom_call" | custom-call | flops 6144000 | bytes 1048576 | tf_op jit(solution)/shard_map/contact/pallas_call | solution.py:726
  19.3 0.2 %collective-permute-done.2.relayed = f32[256,128]{1,0:T(8,128)S(1)} collective-permute-done((f32[256,128]{1,0:T(8,128)S(1)}, f32[256,128]{1,0:T(8,128)S(1)}, u32[]{:S(2)}, u32[]{:S(2)}) %collective-permute-start.2) | collective-permute-done | bytes 131104 | tf_op jit(solution)/shard_map/ppermute | solution.py:723
  19.5 1.6 %finish.1 = (f32[4,3,16,128]{3,2,1,0:T(8,128)}, f32[4,3,16,128]{3,2,1,0:T(8,128)}) custom-call(f32[256,128]{1,0:T(8,128)S(1)} %bitcast.16, f32[256,128]{1,0:T(8,128)S(1)} %collective-permute-done.2.relayed, f32[4,3,16,128]{3,2,1,0:T(8,128)S(1)} %get-tuple-element.33.moved, f32[32,3,16,128]{3,2,1,0:T(8,128)S(1)} %get-tuple-element.28.near, ...), custom_call_target="tpu_custom_call" | custom-call | tf_op jit(solution)/shard_map/finish/pallas_call | solution.py:744
Async XLA Ops:
  2.5 9.0 %copy-start = (f32[4,16,3,128]{3,1,2,0:T(8,128)S(1)}, f32[4,16,3,128]{3,1,2,0:T(8,128)}, u32[]{:S(2)}) copy-start(f32[4,16,3,128]{3,1,2,0:T(8,128)} %param.7) | copy-start | bytes 294916
  2.5 9.0 %copy-start.1 = (f32[4,16,128]{2,1,0:T(8,128)S(1)}, f32[4,16,128]{2,1,0:T(8,128)}, u32[]{:S(2)}) copy-start(f32[4,16,128]{2,1,0:T(8,128)} %growth.3) | copy-start | bytes 98308
  2.6 9.0 %copy-start.2 = (f32[4,16,128]{2,1,0:T(8,128)S(1)}, f32[4,16,128]{2,1,0:T(8,128)}, u32[]{:S(2)}) copy-start(f32[4,16,128]{2,1,0:T(8,128)} %shear.3) | copy-start | bytes 98308
  2.6 9.0 %copy-start.3 = (f32[4,16,3,128]{3,1,2,0:T(8,128)S(1)}, f32[4,16,3,128]{3,1,2,0:T(8,128)}, u32[]{:S(2)}) copy-start(f32[4,16,3,128]{3,1,2,0:T(8,128)} %param.8) | copy-start | bytes 294916
  2.6 15.5 %all-to-all-start = ((f32[32,8,128]{2,1,0:T(8,128)}), f32[32,8,128]{2,1,0:T(8,128)S(1)}, u32[]{:S(2)}, u32[]{:S(2)}) async-start(f32[32,8,128]{2,1,0:T(8,128)} %bitcast.23), calls=%async_computation | async-start | bytes 262144 | tf_op jit(solution)/shard_map/all_to_all | solution.py:692
  9.9 3.6 %collective-permute-start = (f32[5,16,128]{2,1,0:T(8,128)}, f32[5,16,128]{2,1,0:T(8,128)S(1)}, u32[]{:S(2)}, u32[]{:S(2)}) collective-permute-start(f32[5,16,128]{2,1,0:T(8,128)} %get-tuple-element.24), channel_id=1, source_target_pairs={{0,1},{2,3},{1,0},{3,2},{4,5},{6,7},{5,4},{7,6},{8,9},{10,11},{9,8... | collective-permute-start | bytes 122888 | tf_op jit(solution)/shard_map/ppermute | solution.py:688
  10.2 3.3 %collective-permute-start.1 = (f32[5,16,128]{2,1,0:T(8,128)}, f32[5,16,128]{2,1,0:T(8,128)S(1)}, u32[]{:S(2)}, u32[]{:S(2)}) collective-permute-start(f32[5,16,128]{2,1,0:T(8,128)} %get-tuple-element.25), channel_id=1, source_target_pairs={{1,2},{2,1},{5,6},{6,5},{9,10},{10,9},{13,14},{14,13},{17,18},{18,... | collective-permute-start | bytes 122888 | tf_op jit(solution)/shard_map/ppermute | solution.py:689
  11.5 0.7 %copy-start.4 = (s32[1,1,3,16]{3,1,2,0:T(1,128)S(1)}, s32[1,1,3,16]{3,1,2,0:T(1,128)}, u32[]{:S(2)}) copy-start(s32[1,1,3,16]{3,1,2,0:T(1,128)} %param.11) | copy-start | bytes 580
  11.6 0.7 %copy-start.5 = (f32[1,1,3,16]{3,1,2,0:T(1,128)S(1)}, f32[1,1,3,16]{3,1,2,0:T(1,128)}, u32[]{:S(2)}) copy-start(f32[1,1,3,16]{3,1,2,0:T(1,128)} %param.13) | copy-start | bytes 580
  18.1 1.3 %collective-permute-start.2 = (f32[256,128]{1,0:T(8,128)S(1)}, f32[256,128]{1,0:T(8,128)S(1)}, u32[]{:S(2)}, u32[]{:S(2)}) collective-permute-start(f32[256,128]{1,0:T(8,128)S(1)} %bitcast.14), channel_id=1, source_target_pairs={{0,1},{2,3},{1,0},{3,2},{4,5},{6,7},{5,4},{7,6},{8,9},{10,11},{9,8... | collective-permute-start | bytes 393224 | tf_op jit(solution)/shard_map/ppermute | solution.py:723

commit v9 on v8

--- a/solution.py
+++ b/solution.py
@@ -557,22 +557,22 @@
         rows = pl.ds(start, block)
         theirs = [far[c, rows, :] for c in range(3)]
         theirs = [(theirs[0] + along) * ROOT, theirs[1] * ROOT, theirs[2] * ROOT]
-        starts = range(0, half, half // NEAR_TURNS)
-        turned = [[near[turn, c, rows, :] for c in range(3)] for turn in range(NEAR_TURNS)]
-        sums = [[None] * 3 for _ in starts]
-        for b in range(half // NEAR_TURNS):
-            other = [roll(value, b, 1) for value in theirs]
-            for total, here in zip(sums, turned):
+        count = half // NEAR_TURNS
+        others = [[roll(value, b, 1) for value in theirs] for b in range(count)]
+        total = [None] * 3
+        for turn in range(NEAR_TURNS):
+            here = [near[turn, c, rows, :] for c in range(3)]
+            sums = [None] * 3
+            for other in others:
                 delta = [here[c] - other[c] for c in range(3)]
                 square = delta[0] * delta[0] + delta[1] * delta[1] + delta[2] * delta[2]
                 weight = jnp.exp2(-square)
                 for c in range(3):
-                    total[c] = add(total[c], delta[c] * weight)
+                    sums[c] = add(sums[c], delta[c] * weight)
+            for c in range(3):
+                total[c] = add(total[c], roll(sums[c], turn * count, 1))
         for c in range(3):
-            total = None
-            for a, sum_a in zip(starts, sums):
-                total = add(total, roll(sum_a[c], a, 1))
-            write(c, rows, total)
+            write(c, rows, total[c])
 
     each(pairs // block, lambda step: some(step * block), 2)
 

time: 21.4 us -> 21.3 us (level)
  no operation moved by 1% of the time
where the time goes in v9:
time: 21.3 us; the launch traced here: 21.1 us
  starting transfers between devices  8.51 us (40%)
  Pallas kernels  6.13 us (29%)
  waiting for transfers between devices  4.37 us (21%)
  between operations  1.41 us (7%)
  local copies, waits for them, and re-layouts  0.67 us (3%)
    all_to_all x1, starting transfers between devices, local(): lax.all_to_all(packet, ('region', 'pair', 'core'), 0, 0, tiled=True)  7.33 us
    all_to_all x1, waiting for transfers between devices, local(): lax.all_to_all(packet, ('region', 'pair', 'core'), 0, 0, tiled=True)  4.15 us
    pallas_call x1, Pallas kernels, local(): pl.pallas_call(functools.partial(pack_kernel, dims), out_shape=(jax.Shape...  1.89 us
    pallas_call x1, Pallas kernels, local(): pl.pallas_call(functools.partial(finish_kernel, dims), out_shape=(jax.Sha...  1.62 us
    pallas_call x1, Pallas kernels, local(): pl.pallas_call(functools.partial(inner_kernel, dims), out_shape=(jax.Shap...  1.31 us
    pallas_call x1, Pallas kernels, local(): pl.pallas_call(functools.partial(contact_kernel, dims), out_shape=(jax.Sh...  0.91 us
    unnamed x12, local copies, waits for them, and re-layouts  0.67 us
    ppermute x1, starting transfers between devices, local(): face_b = lax.ppermute(face_b, ('pair', 'core'), links[1])  0.65 us
  transfers between devices with their start and end apart: 4, of which 2 were waited for; matrix products, arithmetic and copies ran while one was open for 0% of the time, Pallas kernels for 12%

profile of v9, /device:TPU:0, one launch (start us, length us, event | category | flops | bytes accessed | tf_op | source)
XLA Modules:
  0.0 21.1 jit_solution(7155707998593655974)
XLA Ops:
  0.6 1.9 %pack.1 = (f32[256,128]{1,0:T(8,128)}, f32[5,16,128]{2,1,0:T(8,128)}, f32[5,16,128]{2,1,0:T(8,128)}) custom-call(f32[192,128]{1,0:T(8,128)} %bitcast.10, f32[4,16,128]{2,1,0:T(8,128)} %growth.3, f32[4,16,128]{2,1,0:T(8,128)} %shear.3, s32[1,3,1,16]{3,2,1,0:T(1,128)} %bitcast.18), custom_call_target="tpu_custom_call" | custom-call | tf_op jit(solution)/shard_map/pack/pallas_call | solution.py:665
  2.5 0.0 copy-start
  2.5 0.0 copy-start.1
  2.6 0.0 copy-start.2
  2.6 0.0 copy-start.3
  2.6 7.3 %all-to-all-start = ((f32[32,8,128]{2,1,0:T(8,128)}), f32[32,8,128]{2,1,0:T(8,128)S(1)}, u32[]{:S(2)}, u32[]{:S(2)}) async-start(f32[32,8,128]{2,1,0:T(8,128)} %bitcast.23), calls=%async_computation | async-start | bytes 262144 | tf_op jit(solution)/shard_map/all_to_all | solution.py:692
  9.9 0.3 %collective-permute-start = (f32[5,16,128]{2,1,0:T(8,128)}, f32[5,16,128]{2,1,0:T(8,128)S(1)}, u32[]{:S(2)}, u32[]{:S(2)}) collective-permute-start(f32[5,16,128]{2,1,0:T(8,128)} %get-tuple-element.24), channel_id=1, source_target_pairs={{0,1},{2,3},{1,0},{3,2},{4,5},{6,7},{5,4},{7,6},{8,9},{10,11},{9,8... | collective-permute-start | bytes 122888 | tf_op jit(solution)/shard_map/ppermute | solution.py:688
  10.2 0.7 %collective-permute-start.1 = (f32[5,16,128]{2,1,0:T(8,128)}, f32[5,16,128]{2,1,0:T(8,128)S(1)}, u32[]{:S(2)}, u32[]{:S(2)}) collective-permute-start(f32[5,16,128]{2,1,0:T(8,128)} %get-tuple-element.25), channel_id=1, source_target_pairs={{1,2},{2,1},{5,6},{6,5},{9,10},{10,9},{13,14},{14,13},{17,18},{18,... | collective-permute-start | bytes 122888 | tf_op jit(solution)/shard_map/ppermute | solution.py:689
  11.5 0.0 copy-start.4
  11.6 0.0 copy-start.5
  11.6 0.0 copy-done
  11.6 0.0 copy-done.1
  11.6 0.0 copy-done.2
  11.6 0.0 copy-done.3
  11.6 0.6 %copy-done.4 = s32[1,1,3,16]{3,1,2,0:T(1,128)S(1)} copy-done((s32[1,1,3,16]{3,1,2,0:T(1,128)S(1)}, s32[1,1,3,16]{3,1,2,0:T(1,128)}, u32[]{:S(2)}) %copy-start.4) | copy-done | bytes 216
  12.2 0.0 copy-done.5
  12.2 1.3 %inner.1 = (f32[4,3,16,128]{3,2,1,0:T(8,128)S(1)}, f32[32,3,16,128]{3,2,1,0:T(8,128)S(1)}, f32[64,16]{1,0:T(8,128)S(1)}) custom-call(f32[4,3,16,128]{3,2,1,0:T(8,128)S(1)} %bitcast.11, f32[4,16,128]{2,1,0:T(8,128)S(1)} %copy-done.1, f32[4,16,128]{2,1,0:T(8,128)S(1)} %copy-done.2, f32[4,3,16,128]{3,2,1,0:T(8,128)S(1)} %bitcast.17, ...), custom_call_target="tpu_custom_call" | custom-call | flops 4096000 | bytes 1048576 | tf_op jit(solution)/shard_map/inner/pallas_call | solution.py:694
  13.6 0.0 collective-permute-done.face_a
  13.6 0.0 collective-permute-done.1.face_b
  13.6 0.4 %outer.1 = (f32[3,16,128]{2,1,0:T(8,128)S(1)}, f32[3,16,128]{2,1,0:T(8,128)S(1)}, f32[2,8,128]{2,1,0:T(8,128)S(1)}) custom-call(f32[4,3,16,128]{3,2,1,0:T(8,128)S(1)} %bitcast.12, f32[4,16,128]{2,1,0:T(8,128)S(1)} %copy-done.1, f32[4,16,128]{2,1,0:T(8,128)S(1)} %copy-done.2, f32[5,16,128]{2,1,0:T(8,128)S(1)} %collective-permute-done.face_a, ...), custom_call_target="tpu_custom_call" | custom-call | flops 2048000 | bytes 1048576 | tf_op jit(solution)/shard_map/outer/pallas_call | solution.py:708
  14.0 4.1 %all-to-all-done = f32[32,8,128]{2,1,0:T(8,128)S(1)} async-done(((f32[32,8,128]{2,1,0:T(8,128)}), f32[32,8,128]{2,1,0:T(8,128)S(1)}, u32[]{:S(2)}, u32[]{:S(2)}) %all-to-all-start) | async-done | bytes 131104 | tf_op jit(solution)/shard_map/all_to_all | solution.py:692
  18.1 0.2 %collective-permute-start.2 = (f32[256,128]{1,0:T(8,128)S(1)}, f32[256,128]{1,0:T(8,128)S(1)}, u32[]{:S(2)}, u32[]{:S(2)}) collective-permute-start(f32[256,128]{1,0:T(8,128)S(1)} %bitcast.14), channel_id=1, source_target_pairs={{0,1},{2,3},{1,0},{3,2},{4,5},{6,7},{5,4},{7,6},{8,9},{10,11},{9,8... | collective-permute-start | bytes 393224 | tf_op jit(solution)/shard_map/ppermute | solution.py:723
  18.3 0.9 %contact.1 = (f32[32,16]{1,0:T(8,128)S(1)}, f32[4,3,16,128]{3,2,1,0:T(8,128)S(1)}) custom-call(f32[256,128]{1,0:T(8,128)S(1)} %bitcast.15, f32[32,3,16,128]{3,2,1,0:T(8,128)S(1)} %get-tuple-element.28.near, s32[1,3,1,16]{3,2,1,0:T(1,128)S(1)} %bitcast.21, f32[4,3,16,128]{3,2,1,0:T(8,128)S(1)} %get-tuple-element.29.before, ...), custom_call_target="tpu_custom_call" | custom-call | flops 6144000 | bytes 1048576 | tf_op jit(solution)/shard_map/contact/pallas_call | solution.py:726
  19.3 0.2 %collective-permute-done.2.relayed = f32[256,128]{1,0:T(8,128)S(1)} collective-permute-done((f32[256,128]{1,0:T(8,128)S(1)}, f32[256,128]{1,0:T(8,128)S(1)}, u32[]{:S(2)}, u32[]{:S(2)}) %collective-permute-start.2) | collective-permute-done | bytes 131104 | tf_op jit(solution)/shard_map/ppermute | solution.py:723
  19.5 1.6 %finish.1 = (f32[4,3,16,128]{3,2,1,0:T(8,128)}, f32[4,3,16,128]{3,2,1,0:T(8,128)}) custom-call(f32[256,128]{1,0:T(8,128)S(1)} %bitcast.16, f32[256,128]{1,0:T(8,128)S(1)} %collective-permute-done.2.relayed, f32[4,3,16,128]{3,2,1,0:T(8,128)S(1)} %get-tuple-element.33.moved, f32[32,3,16,128]{3,2,1,0:T(8,128)S(1)} %get-tuple-element.28.near, ...), custom_call_target="tpu_custom_call" | custom-call | tf_op jit(solution)/shard_map/finish/pallas_call | solution.py:744
Async XLA Ops:
  2.5 9.0 %copy-start = (f32[4,16,3,128]{3,1,2,0:T(8,128)S(1)}, f32[4,16,3,128]{3,1,2,0:T(8,128)}, u32[]{:S(2)}) copy-start(f32[4,16,3,128]{3,1,2,0:T(8,128)} %param.7) | copy-start | bytes 294916
  2.5 9.0 %copy-start.1 = (f32[4,16,128]{2,1,0:T(8,128)S(1)}, f32[4,16,128]{2,1,0:T(8,128)}, u32[]{:S(2)}) copy-start(f32[4,16,128]{2,1,0:T(8,128)} %growth.3) | copy-start | bytes 98308
  2.6 9.0 %copy-start.2 = (f32[4,16,128]{2,1,0:T(8,128)S(1)}, f32[4,16,128]{2,1,0:T(8,128)}, u32[]{:S(2)}) copy-start(f32[4,16,128]{2,1,0:T(8,128)} %shear.3) | copy-start | bytes 98308
  2.6 9.0 %copy-start.3 = (f32[4,16,3,128]{3,1,2,0:T(8,128)S(1)}, f32[4,16,3,128]{3,1,2,0:T(8,128)}, u32[]{:S(2)}) copy-start(f32[4,16,3,128]{3,1,2,0:T(8,128)} %param.8) | copy-start | bytes 294916
  2.6 15.5 %all-to-all-start = ((f32[32,8,128]{2,1,0:T(8,128)}), f32[32,8,128]{2,1,0:T(8,128)S(1)}, u32[]{:S(2)}, u32[]{:S(2)}) async-start(f32[32,8,128]{2,1,0:T(8,128)} %bitcast.23), calls=%async_computation | async-start | bytes 262144 | tf_op jit(solution)/shard_map/all_to_all | solution.py:692
  9.9 3.6 %collective-permute-start = (f32[5,16,128]{2,1,0:T(8,128)}, f32[5,16,128]{2,1,0:T(8,128)S(1)}, u32[]{:S(2)}, u32[]{:S(2)}) collective-permute-start(f32[5,16,128]{2,1,0:T(8,128)} %get-tuple-element.24), channel_id=1, source_target_pairs={{0,1},{2,3},{1,0},{3,2},{4,5},{6,7},{5,4},{7,6},{8,9},{10,11},{9,8... | collective-permute-start | bytes 122888 | tf_op jit(solution)/shard_map/ppermute | solution.py:688
  10.2 3.3 %collective-permute-start.1 = (f32[5,16,128]{2,1,0:T(8,128)}, f32[5,16,128]{2,1,0:T(8,128)S(1)}, u32[]{:S(2)}, u32[]{:S(2)}) collective-permute-start(f32[5,16,128]{2,1,0:T(8,128)} %get-tuple-element.25), channel_id=1, source_target_pairs={{1,2},{2,1},{5,6},{6,5},{9,10},{10,9},{13,14},{14,13},{17,18},{18,... | collective-permute-start | bytes 122888 | tf_op jit(solution)/shard_map/ppermute | solution.py:689
  11.5 0.7 %copy-start.4 = (s32[1,1,3,16]{3,1,2,0:T(1,128)S(1)}, s32[1,1,3,16]{3,1,2,0:T(1,128)}, u32[]{:S(2)}) copy-start(s32[1,1,3,16]{3,1,2,0:T(1,128)} %param.11) | copy-start | bytes 580
  11.6 0.7 %copy-start.5 = (f32[1,1,3,16]{3,1,2,0:T(1,128)S(1)}, f32[1,1,3,16]{3,1,2,0:T(1,128)}, u32[]{:S(2)}) copy-start(f32[1,1,3,16]{3,1,2,0:T(1,128)} %param.13) | copy-start | bytes 580
  18.1 1.3 %collective-permute-start.2 = (f32[256,128]{1,0:T(8,128)S(1)}, f32[256,128]{1,0:T(8,128)S(1)}, u32[]{:S(2)}, u32[]{:S(2)}) collective-permute-start(f32[256,128]{1,0:T(8,128)S(1)} %bitcast.14), channel_id=1, source_target_pairs={{0,1},{2,3},{1,0},{3,2},{4,5},{6,7},{5,4},{7,6},{8,9},{10,11},{9,8... | collective-permute-start | bytes 393224 | tf_op jit(solution)/shard_map/ppermute | solution.py:723
